TPU v7x, 256 devices: a whole 4x4x8 slice. The times are simulated.
256 devices in a mesh: leaf: 16 (over x, y), blk: 16 (over z, core).
Axes of the slice: x: 4, y: 4, z: 8, core: 2. Of those that a mesh axis runs over, the one named last changes fastest.
Arguments:
- near_tiles: bfloat16 [128, 16, 512, 512], P('leaf', 'blk'), may hold values from -0.25 to 0.25
- near_cols: int32 [128, 16], P('leaf', 'blk'), may hold values from 0 to 127, as said below
- near_count: int32 [128], P('leaf'), may hold values from 1 to 16, as said below
- probes: bfloat16 [128, 512, 512], P('leaf'), may hold values from -6 to 6
- mixing: float32 [512, 64], replicated, may hold values from -0.25 to 0.25
- far_tiles: bfloat16 [128, 16, 512, 512], P('leaf', 'blk'), may hold values from -6 to 6
- far_cols: int32 [128, 16], P('leaf', 'blk'), may hold values from 0 to 127, as said below
Outputs:
- coupling: float32 [128, 16, 64, 64], P('leaf', 'blk')
- root_part: float32 [128, 64, 64], P('leaf')
Inputs may be any that keep to these rules, and one draw needn't show every extreme that they name: near_cols[r, k] lies within 8 of r; the slots below near_count[r] name distinct clusters. Slots at or past near_count[r] hold arbitrary tiles that must be ignored. far_cols[r, j] differs from r by more than 8.
All inputs are finite; a program needn't handle non-finite values.
Results may differ from a plain program's by a relative error of at most 0.0041.
Values may be sent and summed in bfloat16 or wider, within the bound.
No kernel may reach another device: no remote copies, remote signals or barrier semaphores. Data moves between devices by JAX's collectives and lax.ppermute only.
A program may use at most 128 MiB of HBM per device.

v0:
```python
import math

import jax
import jax.numpy as jnp
from jax import lax
from jax.sharding import PartitionSpec as P

RANK = 64
REACH = 8


highest = lax.Precision.HIGHEST


def padded(value, sides, width):
    for axis, dim in sides:
        peers, length = (lax.axis_size(axis), value.shape[dim])
        up = [(i, (i + 1) % peers) for i in range(peers - 1)]
        down = [(j, i) for i, j in up]
        last = lax.slice_in_dim(value, length - width, length, axis=dim)
        leading = lax.slice_in_dim(value, 0, width, axis=dim)
        before = lax.ppermute(last, axis, up)
        after = lax.ppermute(leading, axis, down)
        value = jnp.concatenate([before, value, after], axis=dim)
    return value


def partner_2(block, axis, apart):
    count = lax.axis_size(axis)
    route = []
    for low in range(count):
        high = low | 1 << apart
        if high != low and high < count:
            route += [(low, high), (high, low)]
    return lax.ppermute(block, axis, route)


def basis_from(gram_matrix, mixed_rows):
    lower_factor = jnp.linalg.cholesky(gram_matrix)
    solved = jax.scipy.linalg.solve_triangular(
        lower_factor, jnp.swapaxes(mixed_rows, -1, -2), lower=True
    )
    return jnp.swapaxes(solved, -1, -2)


def merge(stacked, mixing):
    mixed_rows = jnp.einsum("...mp,pk->...mk", stacked, mixing, precision=highest)
    gram_matrix = jnp.einsum("...mk,...ml->...kl", mixed_rows, mixed_rows, precision=highest)
    transfer = basis_from(gram_matrix, mixed_rows)
    merged = jnp.einsum("...mk,...mp->...kp", transfer, stacked, precision=highest)
    return (transfer, merged)


def shards(near_tiles, near_cols, near_count, probes, mixing, far_tiles, far_cols):
    local_rows = probes.shape[0]
    near_dev = near_tiles.shape[1]
    leaf_pos = lax.axis_index("leaf")
    blk_pos = lax.axis_index("blk")
    subtrees = lax.axis_size("leaf")
    clusters = local_rows * subtrees
    first_cluster = leaf_pos * local_rows - REACH
    window = padded(probes, (("leaf", 0),), REACH)

    def leaf_sketch(row_index):
        running = jnp.zeros((probes.shape[1], probes.shape[2]), jnp.float32)
        column = near_cols[row_index, 0] - first_cluster
        probe_block = lax.dynamic_index_in_dim(window, column, 0, keepdims=False)
        near_tile = near_tiles[row_index, 0]
        is_live = blk_pos * near_dev + 0 < near_count[row_index]
        running = lax.cond(
            is_live,
            lambda current: jnp.dot(near_tile, probe_block, preferred_element_type=jnp.float32),
            lambda current: current,
            running,
        )
        return running

    partial_sketch = lax.map(leaf_sketch, jnp.arange(local_rows))
    sketch_rows = lax.psum_scatter(partial_sketch, "blk", scatter_dimension=1, tiled=True)
    mixed_rows = jnp.einsum("rbp,pk->rbk", sketch_rows, mixing, precision=highest)
    gram_part = jnp.einsum("rbk,rbl->rkl", mixed_rows, mixed_rows, precision=highest)
    gram_matrix = lax.psum(gram_part, "blk")
    basis_part = basis_from(gram_matrix, mixed_rows)
    proj_part = jnp.einsum("rbk,rbp->rkp", basis_part, sketch_rows, precision=highest)
    leaf_proj = lax.psum(proj_part, "blk")
    basis_low = lax.all_gather(basis_part.astype(jnp.bfloat16), "blk", axis=1, tiled=True)
    all_bases = lax.all_gather(basis_low, "leaf", axis=0, tiled=True)
    far_basis = all_bases[far_cols]
    far_image = jnp.einsum(
        "rjab,rjbk->rjak", far_tiles, far_basis, preferred_element_type=jnp.float32
    )
    coupling = jnp.einsum(
        "rak,rjal->rjkl", basis_low.astype(jnp.float32), far_image, precision=highest
    )
    sub_stack = leaf_proj.reshape(local_rows * RANK, leaf_proj.shape[2])
    sub_transfer, node_sketch = merge(sub_stack, mixing)
    levels = subtrees.bit_length() - 1
    path_factor = jnp.eye(RANK, dtype=jnp.float32)
    for depth_index in range(levels):
        partner = partner_2(node_sketch.astype(jnp.bfloat16), "leaf", depth_index).astype(
            node_sketch.dtype
        )
        is_upper = leaf_pos >> depth_index & 1
        lower_half = jnp.where(is_upper == 1, partner, node_sketch)
        upper_half = jnp.where(is_upper == 1, node_sketch, partner)
        transfer, node_sketch = merge(jnp.concatenate([lower_half, upper_half], 0), mixing)
        picked = lax.dynamic_slice_in_dim(transfer, is_upper * RANK, RANK, 0)
        path_factor = jnp.dot(path_factor, picked, precision=highest)
    sub_blocks = sub_transfer.reshape(local_rows, RANK, RANK)
    root_part = jnp.einsum("cab,bd->cad", sub_blocks, path_factor, precision=highest)
    root_part = root_part * math.sqrt(clusters * RANK)
    return (coupling, root_part)


def solution(mesh):
    in_specs = (
        P("leaf", "blk", None, None),
        P("leaf", "blk"),
        P("leaf"),
        P("leaf", None, None),
        P(),
        P("leaf", "blk", None, None),
        P("leaf", "blk"),
    )
    out_specs = (P("leaf", "blk", None, None), P("leaf", None, None))
    return jax.shard_map(shards, mesh=mesh, in_specs=in_specs, out_specs=out_specs, check_vma=False)
```

profile of v0, /device:TPU:1, one launch (start us, length us, event | category | flops | bytes accessed | tf_op | source)
XLA Modules:
  0.0 676.1 jit_solution(7134080984132930772)
XLA Ops:
  7.2 6.0 collective-permute-start
  13.2 1.3 collective-permute-start.1
  14.6 86.2 %collective-permute-done = bf16[8,512,512]{2,1,0:T(8,128)(2,1)} collective-permute-done((bf16[8,512,512]{2,1,0:T(8,128)(2,1)}, bf16[8,512,512]{2,1,0:T(8,128)(2,1)}, u32[]{:S(2)}, u32[]{:S(2)}) %collective-permute-start) | collective-permute-done | bytes 4194336 | tf_op jit(solution)/shard_map/ppermute | solution.py:22
  100.8 5.8 collective-permute-done.1
  106.6 10.8 %pad_maximum_fusion = bf16[24,512,512]{2,1,0:T(8,128)(2,1)} fusion(bf16[8,512,512]{2,1,0:T(8,128)(2,1)} %collective-permute-done.1, bf16[8,512,512]{2,1,0:T(8,128)(2,1)} %param.17, bf16[8,512,512]{2,1,0:T(8,128)(2,1)} %collective-permute-done), kind=kLoop, calls=%fused_computation.9 | loop fusion | flops 12582912 | bytes 25165824 | tf_op jit(solution)/shard_map/concatenate | solution.py:24
  117.4 60.4 %while.10 = (s32[]{:T(128)}, f32[8,512,512]{2,1,0:T(8,128)}, s32[8]{0:T(128)S(1)}, s32[8]{0:T(128)S(1)}, s32[]{:T(128)}, /*index=5*/bf16[8,1,512,512]{3,2,1,0:T(...) while((s32[]{:T(128)}, f32[8,512,512]{2,1,0:T(8,128)}, ...), condition=%wide.region_3.4_spmd, body=%wide.region_0.3_spmd.sunk | while | flops 268435456 | bytes 4195627 | solution.py:78
  121.0 2.8 conditional.2
  122.2 1.6 convolution_bitcast_fusion
  123.9 1.1 constant_dynamic-update-slice_fusion.2
  128.6 2.8 conditional.2
  129.8 1.6 convolution_bitcast_fusion
  131.4 1.0 constant_dynamic-update-slice_fusion.2
  136.1 2.8 conditional.2
  137.3 1.6 convolution_bitcast_fusion
  139.0 1.1 constant_dynamic-update-slice_fusion.2
  143.7 2.8 conditional.2
  144.8 1.6 convolution_bitcast_fusion
  146.5 1.1 constant_dynamic-update-slice_fusion.2
  151.2 2.8 conditional.2
  152.4 1.6 convolution_bitcast_fusion
  154.0 1.1 constant_dynamic-update-slice_fusion.2
  158.7 2.8 conditional.2
  159.9 1.6 convolution_bitcast_fusion
  161.6 1.1 constant_dynamic-update-slice_fusion.2
  166.3 2.8 conditional.2
  167.5 1.6 convolution_bitcast_fusion
  169.1 1.1 constant_dynamic-update-slice_fusion.2
  173.9 2.8 conditional.2
  175.0 1.6 convolution_bitcast_fusion
  176.7 1.1 constant_dynamic-update-slice_fusion.2
  177.8 69.7 %reduce-scatter.2.cloned.1.call-done = f32[8,32,512]{2,1,0:T(8,128)} async-done(((f32[8,512,512]{2,1,0:T(8,128)}), f32[8,32,512]{2,1,0:T(8,128)}) %reduce-scatter.2.cloned.1.call-update) | async-done | bytes 524304 | tf_op jit(solution)/shard_map/reduce_scatter | solution.py:79
  247.5 1.6 fusion.20
  249.2 1.3 fusion.69
  250.6 111.7 %all-reduce.3.cloned.1.call-done = f32[8,64,64]{1,2,0:T(8,128)} async-done(((f32[8,64,64]{1,2,0:T(8,128)}), f32[8,64,64]{1,2,0:T(8,128)}) %all-reduce.3.cloned.1.call-update) | async-done | bytes 131088 | tf_op jit(solution)/shard_map/psum | solution.py:82
  362.3 1.1 copy.31
  364.4 46.9 %custom-call.17 = f32[8,64,64]{2,1,0:T(8,128)S(1)} custom-call(f32[8,64,64]{2,1,0:T(8,128)S(1)} %fusion.13), custom_call_target="Cholesky" | custom-call | tf_op jit(solution)/shard_map/jit(cholesky)/cholesky | solution.py:39
  411.6 39.3 %custom-call.18 = f32[8,1,64,64]{2,3,1,0:T(8,128)S(1)} custom-call(f32[8,1,64,64]{3,2,1,0:T(8,128)S(1)} %select_bitcast_fusion), custom_call_target="InvertDiagBlocksLowerTriangular" | custom-call | tf_op jit(solution)/shard_map/jit(_solve_triangular)/vmap()/triangular_solve | solution.py:40
  451.3 3.1 fusion.70
  454.5 19.0 %all_gather.6 = bf16[8,512,64]{2,1,0:T(8,128)(2,1)S(1)} all-gather(bf16[8,32,64]{2,1,0:T(8,128)(2,1)S(1)} %convert_bitcast_fusion), channel_id=1, replica_groups=mesh['leaf'=16,'blk'=16] {'blk'}, dimensions={1}, use_global_device_ids=true | all-gather | bytes 557056 | tf_op jit(solution)/shard_map/all_gather | solution.py:86
  473.5 1.2 copy.33
  474.7 92.5 %all-reduce.5.cloned.1.call-done = f32[512,512]{1,0:T(8,128)} async-done(((f32[512,512]{1,0:T(8,128)}), f32[512,512]{1,0:T(8,128)}) %all-reduce.5.cloned.1.call-update) | async-done | bytes 1048592 | tf_op jit(solution)/shard_map/psum | solution.py:85
  567.2 2.4 fusion.71
  569.9 5.8 cholesky.127
  577.1 4.9 custom-call.19
  582.4 2.1 fusion.65
  584.4 1.5 collective-permute-start.2
  586.0 3.8 collective-permute-done.2
  590.5 5.8 cholesky.138
  597.7 4.9 custom-call.23
  603.2 2.6 collective-permute-start.3
  606.0 1.9 collective-permute-done.3
  608.6 5.8 cholesky.149
  615.8 4.9 custom-call.24
  621.2 1.3 collective-permute-start.4
  622.8 3.5 collective-permute-done.4
  627.0 5.8 cholesky.160
  634.2 4.9 custom-call.25
  639.7 3.1 collective-permute-start.5
  643.0 3.2 collective-permute-done.5
  646.9 5.8 cholesky.171
  654.1 4.9 custom-call.26
  659.5 1.1 convolution_multiply_fusion
  660.6 4.0 gather_fusion
  664.5 3.6 fusion.5
  (106 shorter events, 30.5 us)
Async XLA Ops:
  7.2 240.4 %copy-start = (f32[512,64]{0,1:T(8,128)S(1)}, f32[512,64]{0,1:T(8,128)}, u32[]{:S(2)}) copy-start(f32[512,64]{0,1:T(8,128)} %param.18) | copy-start | bytes 393220
  7.2 240.4 %reduce-scatter.2.cloned.1.call-start = ((), (), s32[]{:S(2)}) async-start(), calls=%async_computation.1 | async-start | bytes 8912896 | tf_op jit(solution)/shard_map/reduce_scatter | solution.py:79
  7.2 93.6 %collective-permute-start = (bf16[8,512,512]{2,1,0:T(8,128)(2,1)}, bf16[8,512,512]{2,1,0:T(8,128)(2,1)}, u32[]{:S(2)}, u32[]{:S(2)}) collective-permute-start(bf16[8,512,512]{2,1,0:T(8,128)(2,1)} %param.17), channel_id=1, source_target_pairs={{0,16},{16,32},{32,48},{48,64},{64,80},{80,96},{96,112},{112,128},... | collective-permute-start | bytes 12582920 | tf_op jit(solution)/shard_map/ppermute | solution.py:22
  13.2 93.4 %collective-permute-start.1 = (bf16[8,512,512]{2,1,0:T(8,128)(2,1)}, bf16[8,512,512]{2,1,0:T(8,128)(2,1)}, u32[]{:S(2)}, u32[]{:S(2)}) collective-permute-start(bf16[8,512,512]{2,1,0:T(8,128)(2,1)} %param.17), channel_id=1, source_target_pairs={{16,0},{32,16},{48,32},{64,48},{80,64},{96,80},{112,96},{128,112},... | collective-permute-start | bytes 12582920 | tf_op jit(solution)/shard_map/ppermute | solution.py:23
  14.5 102.8 %copy-start.1 = (s32[8]{0:T(128)S(1)}, s32[8]{0:T(128)}, u32[]{:S(2)}) copy-start(s32[8]{0:T(128)} %param.16) | copy-start | bytes 100
  14.5 102.8 %copy-start.2 = (s32[8,1]{0,1:T(1,128)S(1)}, s32[8,1]{0,1:T(1,128)}, u32[]{:S(2)}) copy-start(s32[8,1]{0,1:T(1,128)} %param.15) | copy-start | bytes 100
  177.7 297.0 %copy-start.3 = (s32[8,1]{0,1:T(1,128)S(1)}, s32[8,1]{0,1:T(1,128)}, u32[]{:S(2)}) copy-start(s32[8,1]{0,1:T(1,128)} %param.20) | copy-start | bytes 100
  177.7 184.6 %all-reduce.3.cloned.1.call-start = ((), (), s32[]{:S(2)}) async-start(), calls=%async_computation.2 | async-start | bytes 524288 | tf_op jit(solution)/shard_map/psum | solution.py:82
  250.5 316.7 %all-reduce.5.cloned.1.call-start = ((), (), s32[]{:S(2)}) async-start(), calls=%async_computation.4 | async-start | bytes 2097152 | tf_op jit(solution)/shard_map/psum | solution.py:85
  454.4 206.2 %all-gather.2.cloned.1.call-start = ((), (), s32[]{:S(2)}) async-start(), calls=%async_computation.3 | async-start | bytes 8912896 | tf_op jit(solution)/shard_map/all_gather | solution.py:87
  584.4 5.4 collective-permute-start.2
  603.2 4.7 collective-permute-start.3
  621.2 5.1 collective-permute-start.4
  639.7 6.5 collective-permute-start.5
Sparse Core Ops, SparseCore 0:
  177.9 69.6 reduce-scatter.1
  250.6 111.6 all-reduce.2
  454.5 112.6 all-reduce.4
  569.5 76.9 all-gather.1
where the time goes:
time: 679 us; the launch traced here: 676 us
  waiting for transfers between devices  378 us (56%)
  other arithmetic  159 us (23%)
  matrix products  35 us (5%)
  local copies, waits for them, and re-layouts  30.2 us (4%)
  loops' own time  24.6 us (4%)
  blocking collectives  19 us (3%)
  starting transfers between devices  15.9 us (2%)
  between operations  14.2 us (2%)
    psum x1, waiting for transfers between devices, shards(): gram_matrix = lax.psum(gram_part, 'blk')  112 us
    psum x1, waiting for transfers between devices, shards(): leaf_proj = lax.psum(proj_part, 'blk')  92.5 us
    ppermute x1, waiting for transfers between devices, padded(): before = lax.ppermute(last, axis, up)  86.2 us
    another operation x19, other arithmetic, basis_from(): lower_factor = jnp.linalg.cholesky(gram_matrix)  79.7 us
    reduce_scatter x1, waiting for transfers between devices, shards(): lax.psum_scatter(partial_sketch, 'blk', scatter_dimension=1, tiled=True)  69.7 us
    another operation x13, other arithmetic, basis_from(): jax.scipy.linalg.solve_triangular(lower_factor, jnp.swapaxes(mixed_rows,...  67.2 us
    another operation x1, loops' own time, shards(): partial_sketch = lax.map(leaf_sketch, jnp.arange(local_rows))  19.8 us
    all_gather x1, blocking collectives, shards(): lax.all_gather(basis_part.astype(jnp.bfloat16), 'blk', axis=1, tiled=True)  19 us
  transfers between devices with their start and end apart: 10, of which 9 were waited for; matrix products, arithmetic and copies ran while one was open for 11% of the time, Pallas kernels for 0%

commit v1 on v0

v1 whole, which is shorter than its diff:
```python
import functools
import math

import jax
import jax.numpy as jnp
from jax import lax
from jax.experimental import pallas as pl
from jax.experimental.pallas import tpu as pltpu
from jax.sharding import PartitionSpec as P

RANK = 64
REACH = 8
LANES = 128

f32 = jnp.float32
bf16 = jnp.bfloat16
highest = lax.Precision.HIGHEST

NN = (((1,), (0,)), ((), ()))
NT = (((1,), (1,)), ((), ()))
TN = (((0,), (0,)), ((), ()))


def dot(a, b, dims, precision=None):
    return lax.dot_general(a, b, dims, precision=precision, preferred_element_type=f32)


def pieces(x):
    high = x.astype(bf16)
    rest = x - high.astype(f32)
    middle = rest.astype(bf16)
    low = (rest - middle.astype(f32)).astype(bf16)
    return high, middle, low


def stacked_dot(stack, other, dims):
    full = dot(stack, other, dims)
    rows = full.shape[0] // 3
    return full[:rows] + full[rows : 2 * rows] + full[2 * rows :]


def factor(gram):
    n = gram.shape[0]
    row = lax.broadcasted_iota(jnp.int32, (n, n), 0)
    col = lax.broadcasted_iota(jnp.int32, (n, n), 1)
    tall = lax.broadcasted_iota(jnp.int32, (n, 1), 0)
    work = jnp.concatenate([gram, (row == col).astype(f32)], axis=1)
    scales = jnp.zeros((n, 1), f32)
    for j in range(n):
        pivot = work[j : j + 1, j : j + 1]
        scales = jnp.where(tall == j, pivot, scales)
        if j < n - 1:
            multiplier = jnp.where(tall > j, work[:, j : j + 1] / pivot, 0.0)
            work = work - multiplier * work[j : j + 1, :]
    work = work * (1.0 / jnp.sqrt(scales))
    upper = jnp.where(col >= row, work[:, :n], 0.0)
    return upper, work[:, n:]


def mixed_probes_kernel(half_ref, mixing_ref, probes_ref, out_ref, stack_ref):
    del half_ref

    @pl.when(pl.program_id(0) == 0)
    def _():
        stack_ref[...] = jnp.concatenate(pieces(mixing_ref[...].T), axis=0)

    out_ref[0] = stacked_dot(stack_ref[...], probes_ref[0], NT)


def mixed_probes(half, mixing, probes):
    count, rows, width = probes.shape
    part = count // 2
    return pl.pallas_call(
        mixed_probes_kernel,
        out_shape=jax.ShapeDtypeStruct((part, RANK, rows), f32),
        grid_spec=pltpu.PrefetchScalarGridSpec(
            num_scalar_prefetch=1,
            grid=(part,),
            in_specs=[
                pl.BlockSpec((width, RANK), lambda i, half: (0, 0)),
                pl.BlockSpec((1, rows, width), lambda i, half: (half[0] * part + i, 0, 0)),
            ],
            out_specs=pl.BlockSpec((1, RANK, rows), lambda i, half: (i, 0, 0)),
            scratch_shapes=[pltpu.VMEM((3 * RANK, width), bf16)],
        ),
        cost_estimate=pl.CostEstimate(
            flops=2 * part * rows * width * 3 * RANK,
            bytes_accessed=part * rows * (2 * width + 4 * RANK),
            transcendentals=0,
        ),
        name="mixed_probes",
    )(half, mixing, probes)


def sketch_kernel(
    meta_ref, own_a, own_b, before_a, before_b, after_a, after_b, tile_ref, keep_ref, send_ref, pick_ref
):
    i = pl.program_id(0)
    count = pl.num_programs(0)
    part = own_a.shape[0]
    core = meta_ref[2 * count]
    column = jnp.clip(meta_ref[i], 0, 6 * part - 1)
    segment = column // (2 * part)
    inner = column % (2 * part)
    mine = inner // part == core
    place = inner % part
    sources = ((before_a, before_b), (own_a, own_b), (after_a, after_b))
    for s, (first, second) in enumerate(sources):

        @pl.when((segment == s) & mine)
        def _():
            pick_ref[...] = first[place]

        @pl.when((segment == s) & jnp.logical_not(mine))
        def _():
            pick_ref[...] = second[place]

    stack = jnp.concatenate(pieces(pick_ref[...]), axis=0)
    mixed = stacked_dot(stack, tile_ref[0, 0], NT)
    mixed = jnp.where(meta_ref[count + i] > 0, mixed, 0.0)
    width = mixed.shape[1] // 2

    @pl.when(core == 0)
    def _():
        keep_ref[0] = mixed[:, :width]
        send_ref[0] = mixed[:, width:]

    @pl.when(core != 0)
    def _():
        keep_ref[0] = mixed[:, width:]
        send_ref[0] = mixed[:, :width]


def compress(meta, parts, near_tiles):
    count, _, rows, width = near_tiles.shape
    whole = pl.BlockSpec((count // 2, RANK, width), lambda i, meta: (0, 0, 0), pipeline_mode=pl.Buffered(1))
    half = pl.BlockSpec((1, RANK, rows // 2), lambda i, meta: (i, 0, 0))
    shape = jax.ShapeDtypeStruct((count, RANK, rows // 2), f32)
    return pl.pallas_call(
        sketch_kernel,
        out_shape=(shape, shape),
        grid_spec=pltpu.PrefetchScalarGridSpec(
            num_scalar_prefetch=1,
            grid=(count,),
            in_specs=[whole] * 6 + [pl.BlockSpec((1, 1, rows, width), lambda i, meta: (i, 0, 0, 0))],
            out_specs=(half, half),
            scratch_shapes=[pltpu.VMEM((RANK, width), f32)],
        ),
        cost_estimate=pl.CostEstimate(
            flops=2 * count * rows * width * 3 * RANK,
            bytes_accessed=count * rows * (2 * width + 16 * RANK),
            transcendentals=0,
        ),
        name="compress",
    )(meta, *parts, near_tiles)


def gram_kernel(terms_ref, mixed_ref, gram_ref):
    total = terms_ref[0]
    for k in range(1, terms_ref.shape[0]):
        total = total + terms_ref[k]
    mixed_ref[...] = total
    gram_ref[...] = dot(total, total, NT, highest)


def gram_of(terms):
    return pl.pallas_call(
        gram_kernel,
        out_shape=(
            jax.ShapeDtypeStruct(terms.shape[1:], f32),
            jax.ShapeDtypeStruct((RANK, RANK), f32),
        ),
        name="gram",
    )(terms)


def basis_kernel(core_ref, mixed_ref, gram_ref, other_ref, out_ref):
    upper, inverse = factor(gram_ref[...] + other_ref[...])
    basis = dot(inverse, mixed_ref[...], NN, highest)
    half = RANK // 2
    rows = jnp.where(core_ref[0] == 0, upper[:half], upper[half:])
    high = rows.astype(bf16).astype(f32)
    middle = (rows - high).astype(bf16).astype(f32)
    low = rows - high - middle
    left = jnp.concatenate([high, middle], axis=0)
    right = jnp.concatenate([low, jnp.zeros_like(low)], axis=0)
    block = jnp.concatenate([basis, left, right], axis=1).astype(bf16)
    for k in range(out_ref.shape[0]):
        out_ref[k] = block


def basis_of(core, mixed, gram, other, copies):
    vmem = pl.BlockSpec(memory_space=pltpu.VMEM)
    return pl.pallas_call(
        basis_kernel,
        out_shape=jax.ShapeDtypeStruct((copies, RANK, mixed.shape[1] + LANES), bf16),
        in_specs=[pl.BlockSpec(memory_space=pltpu.SMEM), vmem, vmem, vmem],
        out_specs=vmem,
        name="basis",
    )(core, mixed, gram, other)


def spread_kernel(meta_ref, own_ref, other_ref, out_ref, basis_ref, upper_ref, work_ref):
    count = own_ref.shape[0]
    groups = out_ref.shape[0] // count
    blocks = RANK // groups
    width = own_ref.shape[2] - LANES
    half = RANK // 2
    tiles = work_ref.shape[0]
    first = meta_ref[count] == 0
    total = jnp.zeros((RANK, RANK), f32)
    for r in range(count):
        mine, others = own_ref[r].astype(f32), other_ref[r].astype(f32)
        sides = (jnp.where(first, mine, others), jnp.where(first, others, mine))
        uppers = []
        for h, side in enumerate(sides):
            basis_ref[r, :, h * width : (h + 1) * width] = side[:, :width].astype(bf16)
            for q in range(blocks):
                for t in range(width // LANES):
                    work_ref[(q * 2 + h) * width // LANES + t, pl.ds(r, groups, stride=count), :] = side[
                        q * groups : (q + 1) * groups, t * LANES : (t + 1) * LANES
                    ]
            uppers.append(
                side[:half, width : width + RANK]
                + side[half:, width : width + RANK]
                + side[:half, width + RANK :]
            )
        upper = jnp.concatenate(uppers, axis=0)
        upper_ref[r] = upper
        total = total + dot(upper, upper, TN, highest)
        work_ref[tiles - 2, pl.ds(r, groups, stride=count), :] = jnp.full(
            (groups, LANES), meta_ref[r].astype(f32), f32
        )
    work_ref[tiles - 1] = jnp.zeros((groups * count, LANES), f32)
    for p in range(2):
        low_row = 2 * p * groups
        packed = jnp.concatenate(
            [total[low_row : low_row + groups], total[low_row + groups : low_row + 2 * groups]], axis=1
        )
        for k, piece in enumerate(pieces(packed)):
            work_ref[tiles - 1, pl.ds(2 * k + p, groups, stride=count), :] = piece.astype(f32)
    for t in range(tiles):
        out_ref[:, t * LANES : (t + 1) * LANES] = work_ref[t].astype(bf16)


def spread(meta, own, other, groups):
    count, _, width = own.shape
    rows = 2 * (width - LANES)
    total = RANK // groups * rows + 2 * LANES
    vmem = pl.BlockSpec(memory_space=pltpu.VMEM)
    return pl.pallas_call(
        spread_kernel,
        out_shape=(
            jax.ShapeDtypeStruct((groups * count, total), bf16),
            jax.ShapeDtypeStruct((count, RANK, rows), bf16),
            jax.ShapeDtypeStruct((count, RANK, RANK), f32),
        ),
        in_specs=[pl.BlockSpec(memory_space=pltpu.SMEM), vmem, vmem],
        out_specs=(vmem, vmem, vmem),
        scratch_shapes=[pltpu.VMEM((total // LANES, groups * count, LANES), f32)],
        name="spread",
    )(meta, own, other)


def choose_kernel(count, in_ref, out_ref):
    clusters, total = in_ref.shape
    body = total - 2 * LANES
    wanted = in_ref[:, body : body + LANES].astype(f32)
    column = lax.broadcasted_iota(jnp.int32, (clusters, clusters), 1).astype(f32)
    select = (wanted == column).astype(bf16)
    out_ref[:, :body] = dot(select, in_ref[:, :body], NN).astype(bf16)
    row = lax.broadcasted_iota(jnp.int32, (count, clusters), 0)
    column = lax.broadcasted_iota(jnp.int32, (count, clusters), 1) % count
    gather = (((column == row) | (column == row + 2) | (column == row + 4)) & (row < 2)).astype(bf16)
    sums = dot(gather, in_ref[:, body + LANES :], NN)[:2]
    block = jnp.concatenate([piece.astype(f32) for piece in pieces(sums)] + [jnp.zeros((count - 6, LANES), f32)], axis=0)
    out_ref[:, body:] = jnp.concatenate([block] * (clusters // count), axis=0).astype(bf16)


def choose(received, count):
    rows, total = received.shape
    return pl.pallas_call(
        functools.partial(choose_kernel, count),
        out_shape=jax.ShapeDtypeStruct((rows, total - LANES), bf16),
        name="choose",
    )(received)


def couple_kernel(scale, basis_ref, upper_ref, received_ref, tile_ref, coupling_ref, root_ref, work_ref):
    i = pl.program_id(0)
    count = upper_ref.shape[0]
    rows, total = received_ref.shape
    body = total - LANES
    groups = rows // count
    blocks = RANK // groups
    width = body // blocks
    tiles = work_ref.shape[0]

    @pl.when(i == 0)
    def _():
        for t in range(tiles):
            work_ref[t] = received_ref[:, t * LANES : (t + 1) * LANES].astype(f32)
        parts = []
        for p in range(2):
            packed = sum(work_ref[tiles - 1, pl.ds(2 * k + p, groups, stride=count), :] for k in range(3))
            parts += [packed[:, :RANK], packed[:, RANK:]]
        _, inverse = factor(jnp.concatenate(parts, axis=0))
        for r in range(count):
            root_ref[r] = dot(upper_ref[r], inverse, NT, highest) * scale

    image = dot(basis_ref[0], tile_ref[0, 0], NN)
    wide = width // LANES
    far = jnp.concatenate(
        [
            jnp.concatenate(
                [work_ref[q * wide + t, pl.ds(i, groups, stride=count), :] for t in range(wide)], axis=1
            ).astype(bf16)
            for q in range(blocks)
        ],
        axis=0,
    )
    coupling_ref[0, 0] = stacked_dot(jnp.concatenate(pieces(image), axis=0), far, NT)


def couple(basis, upper, received, far_tiles, scale):
    count, _, rows, width = far_tiles.shape
    return pl.pallas_call(
        functools.partial(couple_kernel, scale),
        out_shape=(
            jax.ShapeDtypeStruct((count, 1, RANK, RANK), f32),
            jax.ShapeDtypeStruct((count, RANK, RANK), f32),
        ),
        grid=(count,),
        in_specs=[
            pl.BlockSpec((1, RANK, rows), lambda i: (i, 0, 0)),
            pl.BlockSpec((count, RANK, RANK), lambda i: (0, 0, 0)),
            pl.BlockSpec(received.shape, lambda i: (0, 0)),
            pl.BlockSpec((1, 1, rows, width), lambda i: (i, 0, 0, 0)),
        ],
        out_specs=(
            pl.BlockSpec((1, 1, RANK, RANK), lambda i: (i, 0, 0, 0)),
            pl.BlockSpec((count, RANK, RANK), lambda i: (0, 0, 0)),
        ),
        scratch_shapes=[pltpu.VMEM((received.shape[1] // LANES, received.shape[0], LANES), f32)],
        name="couple",
    )(basis, upper, received, far_tiles)


def shards(near_tiles, near_cols, near_count, probes, mixing, far_tiles, far_cols):
    count = probes.shape[0]
    subtrees = lax.axis_size("leaf")
    members = lax.axis_size("blk")
    leaf_pos = lax.axis_index("leaf")
    blk_pos = lax.axis_index("blk")
    core = blk_pos % 2
    up = [(i, i + 1) for i in range(subtrees - 1)]
    down = [(j, i) for i, j in up]
    pair = [(i, i ^ 1) for i in range(members)]
    lanes = [list(range(c, members, 2)) for c in range(2)]

    core_vec = core.reshape(1).astype(jnp.int32)
    live = (blk_pos < near_count).astype(jnp.int32)
    near_meta = jnp.concatenate([near_cols[:, 0] - (leaf_pos * count - REACH), live, core_vec])
    far_meta = jnp.concatenate([far_cols[:, 0], core_vec])

    own_a = mixed_probes(core_vec, mixing, probes)
    before_a = lax.ppermute(own_a, "leaf", up)
    after_a = lax.ppermute(own_a, "leaf", down)
    own_b = mixed_probes(1 - core_vec, mixing, probes)
    before_b = lax.ppermute(before_a, "blk", pair)
    after_b = lax.ppermute(after_a, "blk", pair)
    keep, send = compress(near_meta, (own_a, own_b, before_a, before_b, after_a, after_b), near_tiles)
    halves = keep + lax.ppermute(send, "blk", pair)
    terms = lax.all_to_all(halves, "blk", 0, 0, tiled=True, axis_index_groups=lanes)
    mixed, gram = gram_of(terms)
    own = basis_of(core_vec, mixed, gram, lax.ppermute(gram, "blk", pair), count)
    own = lax.all_to_all(own, "blk", 0, 0, tiled=True, axis_index_groups=lanes)
    other = lax.ppermute(own, "blk", pair)
    payload, basis, upper = spread(far_meta, own, other, subtrees)
    slices = lax.all_to_all(payload.reshape(subtrees, count, -1), "leaf", 0, 0, tiled=True)
    chosen = choose(slices.reshape(payload.shape), count)
    received = lax.all_to_all(chosen.reshape(subtrees, count, -1), "leaf", 0, 0, tiled=True)
    scale = math.sqrt(subtrees * count * RANK)
    return couple(basis, upper, received.reshape(chosen.shape), far_tiles, scale)


def solution(mesh):
    in_specs = (
        P("leaf", "blk", None, None),
        P("leaf", "blk"),
        P("leaf"),
        P("leaf", None, None),
        P(),
        P("leaf", "blk", None, None),
        P("leaf", "blk"),
    )
    out_specs = (P("leaf", "blk", None, None), P("leaf", None, None))
    return jax.shard_map(shards, mesh=mesh, in_specs=in_specs, out_specs=out_specs, check_vma=False)
```

time: 679 us -> 155 us (0.23)
  waiting for transfers between devices: 378 us -> 12 us
  other arithmetic: 159 us -> 2.29 us
  blocking collectives: 19 us -> 77.6 us
  Pallas kernels: 0 us -> 46.2 us
  matrix products: 35 us -> 0 us
  local copies, waits for them, and re-layouts: 30.2 us -> 3.91 us
  loops' own time: 24.6 us -> 0 us
  between operations: 14.2 us -> 0.7 us
    psum x2 -> x0, waiting for transfers between devices: 204 us -> none  [the longest x1 112 us: shards(): gram_matrix = lax.psum(gram_part, 'blk')]
    another operation x32 -> x0, other arithmetic: 147 us -> none  [the longest x19 79.7 us: basis_from(): lower_factor = jnp.linalg.cholesky(gram_matrix)]
    ppermute x6 -> x7, waiting for transfers between devices: 104 us -> 12 us  [the longest x1 5.29 us: shards(): before_a = lax.ppermute(own_a, 'leaf', up)]
    all_to_all x0 -> x4, blocking collectives: none -> 77.6 us  [the longest x1 25 us: shards(): lax.all_to_all(halves, 'blk', 0, 0, tiled=True, axis_index_groups=lanes)]
    reduce_scatter x1 -> x0, waiting for transfers between devices: 69.7 us -> none  [shards(): lax.psum_scatter(partial_sketch, 'blk', scatter_dimension=1, tiled=True)]
    pallas_call x0 -> x8, Pallas kernels: none -> 46.2 us  [the longest x1 14 us: couple(): pl.pallas_call(functools.partial(couple_kernel, scale), out_shape=(jax.Sh...]
    dot_general x32 -> x0, matrix products: 33.3 us -> none  [the longest x8 13.1 us: leaf_sketch(): jnp.dot(near_tile, probe_block, preferred_element_type=jnp.float32)]
    another operation x9 -> x0, loops' own time: 24.6 us -> none  [the longest x1 19.8 us: shards(): partial_sketch = lax.map(leaf_sketch, jnp.arange(local_rows))]
  transfers between devices with their start and end apart: 10 -> 7, of which waited for: 9 -> 6; matrix products, arithmetic and copies ran while one was open for 11% -> 1% of each run, Pallas kernels for 0% -> 3%
where the time goes in v1:
time: 155 us; the launch traced here: 154 us
  blocking collectives  77.6 us (50%)
  Pallas kernels  46.2 us (30%)
  waiting for transfers between devices  12 us (8%)
  starting transfers between devices  11.1 us (7%)
  local copies, waits for them, and re-layouts  3.91 us (3%)
  other arithmetic  2.29 us (1%)
    all_to_all x1, blocking collectives, shards(): lax.all_to_all(halves, 'blk', 0, 0, tiled=True, axis_index_groups=lanes)  25 us
    all_to_all x1, blocking collectives, shards(): lax.all_to_all(payload.reshape(subtrees, count, -1), 'leaf', 0, 0, tiled=...  19.5 us
    all_to_all x1, blocking collectives, shards(): own = lax.all_to_all(own, 'blk', 0, 0, tiled=True, axis_index_groups=lanes)  18.5 us
    all_to_all x1, blocking collectives, shards(): lax.all_to_all(chosen.reshape(subtrees, count, -1), 'leaf', 0, 0, tiled=T...  14.5 us
    pallas_call x1, Pallas kernels, couple(): pl.pallas_call(functools.partial(couple_kernel, scale), out_shape=(jax.Sh...  14 us
    pallas_call x1, Pallas kernels, compress(): pl.pallas_call(sketch_kernel, out_shape=(shape, shape), grid_spec=pltpu.P...  8.76 us
    pallas_call x2, Pallas kernels, mixed_probes(): pl.pallas_call(mixed_probes_kernel, out_shape=jax.ShapeDtypeStruct((part,...  8.55 us
    pallas_call x1, Pallas kernels, basis_of(): pl.pallas_call(basis_kernel, out_shape=jax.ShapeDtypeStruct((copies, RANK...  7.61 us
  transfers between devices with their start and end apart: 7, of which 6 were waited for; matrix products, arithmetic and copies ran while one was open for 1% of the time, Pallas kernels for 3%

profile of v1, /device:TPU:1, one launch (start us, length us, event | category | flops | bytes accessed | tf_op | source)
XLA Modules:
  0.0 153.7 jit_solution(1335614563994931206)
XLA Ops:
  0.6 1.7 %copy.9.mixing_ref = f32[512,64]{1,0:T(8,128)} copy(f32[512,64]{0,1:T(8,128)} %param.11) | data formatting | bytes 262144 | tf_op args[4]
  2.4 0.0 copy-start.7
  2.4 0.0 copy-start.8
  2.4 4.3 %mixed_probes.2.own_a = f32[4,64,512]{2,1,0:T(8,128)} custom-call(s32[1]{0:T(128)} %bitcast.1.half_ref.core_ref, f32[512,64]{1,0:T(8,128)} %copy.9.mixing_ref, bf16[8,512,512]{2,1,0:T(8,128)(2,1)} %probes_ref.3), custom_call_target="tpu_custom_call" | custom-call | flops 402653184 | bytes 2621440 | tf_op jit(solution)/shard_map/mixed_probes/pallas_call | solution.py:73
  6.7 4.0 %collective-permute-start = (f32[4,64,512]{2,1,0:T(8,128)}, f32[4,64,512]{2,1,0:T(8,128)S(1)}, u32[]{:S(2)}, u32[]{:S(2)}) collective-permute-start(f32[4,64,512]{2,1,0:T(8,128)} %mixed_probes.2.own_a), channel_id=1, source_target_pairs={{0,16},{16,32},{32,48},{48,64},{64,80},{80,96},{96,112},{112,128},... | collective-permute-start | bytes 1572872 | tf_op jit(solution)/shard_map/ppermute | solution.py:367
  10.7 1.3 collective-permute-start.2
  12.0 4.3 %mixed_probes.3.own_b = f32[4,64,512]{2,1,0:T(8,128)} custom-call(s32[1]{0:T(128)S(6)} %sub.19.half_ref, f32[512,64]{1,0:T(8,128)} %copy.9.mixing_ref, bf16[8,512,512]{2,1,0:T(8,128)(2,1)} %probes_ref.3), custom_call_target="tpu_custom_call" | custom-call | flops 402653184 | bytes 2621440 | tf_op jit(solution)/shard_map/mixed_probes/pallas_call | solution.py:73
  16.3 5.3 %collective-permute-done.before_a = f32[4,64,512]{2,1,0:T(8,128)S(1)} collective-permute-done((f32[4,64,512]{2,1,0:T(8,128)}, f32[4,64,512]{2,1,0:T(8,128)S(1)}, u32[]{:S(2)}, u32[]{:S(2)}) %collective-permute-start) | collective-permute-done | bytes 524320 | tf_op jit(solution)/shard_map/ppermute | solution.py:367
  21.6 0.0 copy-start.1
  21.6 1.5 collective-permute-start.1
  23.1 2.2 %collective-permute-done.2.after_a = f32[4,64,512]{2,1,0:T(8,128)S(1)} collective-permute-done((f32[4,64,512]{2,1,0:T(8,128)}, f32[4,64,512]{2,1,0:T(8,128)S(1)}, u32[]{:S(2)}, u32[]{:S(2)}) %collective-permute-start.2) | collective-permute-done | bytes 524320 | tf_op jit(solution)/shard_map/ppermute | solution.py:368
  25.3 0.0 copy-start.2
  25.3 1.8 %collective-permute-start.3 = (f32[4,64,512]{2,1,0:T(8,128)S(1)}, f32[4,64,512]{2,1,0:T(8,128)S(1)}, u32[]{:S(2)}, u32[]{:S(2)}) collective-permute-start(f32[4,64,512]{2,1,0:T(8,128)S(1)} %collective-permute-done.2.after_a), channel_id=1, source_target_pairs={{0,1},{1,0},{2,3},{3,2},{4,5},{5,4},{6,7},{7,6},{8,9},{9,8},{10,11... | collective-permute-start | bytes 1572872 | tf_op jit(solution)/shard_map/ppermute | solution.py:371
  27.2 0.0 copy-done.7
  27.2 0.0 copy-done.8
  27.2 0.6 pad_add_fusion.1.meta_ref
  27.8 0.0 copy-start.9
  27.8 0.0 collective-permute-done.1.before_b
  27.8 0.0 copy-start.3
  27.8 0.9 collective-permute-done.3.after_b
  28.7 0.0 copy-done.1
  28.7 0.0 copy-done.2
  28.7 0.0 copy-done.3
  28.7 0.0 copy-start.4
  28.7 0.8 copy-done.4
  29.5 8.8 %compress.1 = (f32[8,64,256]{2,1,0:T(8,128)}, f32[8,64,256]{2,1,0:T(8,128)}) custom-call(s32[17]{0:T(128)} %pad_add_fusion.1.meta_ref, f32[4,64,512]{2,1,0:T(8,128)} %mixed_probes.2.own_a, f32[4,64,512]{2,1,0:T(8,128)} %mixed_probes.3.own_b, f32[4,64,512]{2,1,0:T(8,128)} %copy-done.1, f32[4,64,512]{2,1,0:T(8,128)} %copy-done.3, f32[4,64,512]{2,1,0:T(8,128)} %copy-done.2, ...), custom_call_target="tpu_custom_call" | custom-call | flops 805306368 | bytes 8388608 | tf_op jit(solution)/shard_map/compress/pallas_call | solution.py:139
  38.3 0.3 collective-permute-start.4
  38.6 1.8 %collective-permute-done.4 = f32[8,64,256]{2,1,0:T(8,128)S(1)} collective-permute-done((f32[8,64,256]{2,1,0:T(8,128)}, f32[8,64,256]{2,1,0:T(8,128)S(1)}, u32[]{:S(2)}, u32[]{:S(2)}) %collective-permute-start.4) | collective-permute-done | bytes 524320 | tf_op jit(solution)/shard_map/ppermute | solution.py:373
  40.4 1.1 add.9
  41.5 25.0 %all_to_all.20.terms_ref = f32[8,64,256]{2,1,0:T(8,128)} all-to-all(f32[8,64,256]{2,1,0:T(8,128)S(1)} %add.9), channel_id=1, replica_groups={{0,2,4,6,8,10,12,14},{1,3,5,7,9,11,13,15},{16,18,20,22,24,26,28,30},{17..., dimensions={0} | all-to-all | bytes 1048576 | tf_op jit(solution)/shard_map/all_to_all | solution.py:374
  66.5 1.9 %gram.1 = (f32[64,256]{1,0:T(8,128)}, f32[64,64]{1,0:T(8,128)}) custom-call(f32[8,64,256]{2,1,0:T(8,128)} %all_to_all.20.terms_ref), custom_call_target="tpu_custom_call" | custom-call | tf_op jit(solution)/shard_map/gram/pallas_call | solution.py:167
  68.4 1.6 %collective-permute-start.5 = (f32[64,64]{1,0:T(8,128)}, f32[64,64]{1,0:T(8,128)S(1)}, u32[]{:S(2)}, u32[]{:S(2)}) collective-permute-start(f32[64,64]{1,0:T(8,128)} %get-tuple-element.12.gram_ref), channel_id=1, source_target_pairs={{0,1},{1,0},{2,3},{3,2},{4,5},{5,4},{6,7},{7,6},{8,9},{9,8},{10,11... | collective-permute-start | bytes 49160 | tf_op jit(solution)/shard_map/ppermute | solution.py:376
  69.9 1.1 collective-permute-done.5.other_ref
  71.0 0.0 copy-start.6
  71.0 0.6 copy-done.6
  71.6 7.6 %basis.1 = bf16[8,64,384]{2,1,0:T(8,128)(2,1)} custom-call(s32[1]{0:T(128)} %bitcast.1.half_ref.core_ref, f32[64,256]{1,0:T(8,128)} %get-tuple-element.11.mixed_ref, f32[64,64]{1,0:T(8,128)} %get-tuple-element.12.gram_ref, f32[64,64]{1,0:T(8,128)} %copy-done.6), custom_call_target="tpu_custom_call" | custom-call | tf_op jit(solution)/shard_map/basis/pallas_call | solution.py:194
  79.2 18.5 %all_to_all.21.own_ref = bf16[8,64,384]{2,1,0:T(8,128)(2,1)S(1)} all-to-all(bf16[8,64,384]{2,1,0:T(8,128)(2,1)} %basis.1), channel_id=1, replica_groups={{0,2,4,6,8,10,12,14},{1,3,5,7,9,11,13,15},{16,18,20,22,24,26,28,30},{17..., dimensions={0} | all-to-all | bytes 786432 | tf_op jit(solution)/shard_map/all_to_all | solution.py:377
  97.7 0.0 copy-start
  97.7 0.5 collective-permute-start.6
  98.2 0.0 copy-done.9
  98.2 0.6 pad_add_fusion.meta_ref
  98.8 0.8 collective-permute-done.6.other_ref
  99.5 0.0 copy-done
  99.5 0.0 copy-start.5
  99.5 0.8 copy-done.5
  100.3 3.2 %spread.1 = (bf16[128,2304]{1,0:T(8,128)(2,1)}, bf16[8,64,512]{2,1,0:T(8,128)(2,1)}, f32[8,64,64]{2,1,0:T(8,128)}) custom-call(s32[9]{0:T(128)} %pad_add_fusion.meta_ref, bf16[8,64,384]{2,1,0:T(8,128)(2,1)} %copy-done, bf16[8,64,384]{2,1,0:T(8,128)(2,1)} %copy-done.5), custom_call_target="tpu_custom_call" | custom-call | tf_op jit(solution)/shard_map/spread/pallas_call | solution.py:251
  103.5 19.5 %all_to_all.22 = bf16[16,8,2304]{2,1,0:T(8,128)(2,1)} all-to-all(bf16[16,8,2304]{2,1,0:T(8,128)(2,1)} %bitcast.11), channel_id=1, replica_groups=mesh['leaf'=16,'blk'=16] {'leaf'}, dimensions={0} | all-to-all | bytes 1179648 | tf_op jit(solution)/shard_map/all_to_all | solution.py:380
  123.1 2.2 %choose.1 = bf16[128,2176]{1,0:T(8,128)(2,1)} custom-call(bf16[128,2304]{1,0:T(8,128)(2,1)} %bitcast.8), custom_call_target="tpu_custom_call" | custom-call | tf_op jit(solution)/shard_map/choose/pallas_call | solution.py:282
  125.2 14.5 %all_to_all.23 = bf16[16,8,2176]{2,1,0:T(8,128)(2,1)} all-to-all(bf16[16,8,2176]{2,1,0:T(8,128)(2,1)} %bitcast.9), channel_id=1, replica_groups=mesh['leaf'=16,'blk'=16] {'leaf'}, dimensions={0} | all-to-all | bytes 1114112 | tf_op jit(solution)/shard_map/all_to_all | solution.py:382
  139.8 14.0 %couple.1 = (f32[8,1,64,64]{3,2,1,0:T(8,128)}, f32[8,64,64]{2,1,0:T(8,128)}) custom-call(bf16[8,64,512]{2,1,0:T(8,128)(2,1)} %get-tuple-element.13.basis_ref, f32[8,64,64]{2,1,0:T(8,128)} %get-tuple-element.14.upper_ref, bf16[128,2176]{1,0:T(8,128)(2,1)} %bitcast.10, bf16[8,1,512,512]{3,2,1,0:T(8,128)(2,1)} %tile_ref.3), custom_call_target="tpu_custom_call" | custom-call | tf_op jit(solution)/shard_map/couple/pallas_call | solution.py:327
  (2 shorter events, 0.0 us)
Async XLA Ops:
  2.4 24.8 %copy-start.7 = (s32[8]{0:T(128)S(1)}, s32[8]{0:T(128)}, u32[]{:S(2)}) copy-start(s32[8]{0:T(128)} %param.9) | copy-start | bytes 100
  2.4 24.8 %copy-start.8 = (s32[8,1]{0,1:T(1,128)S(1)}, s32[8,1]{0,1:T(1,128)}, u32[]{:S(2)}) copy-start(s32[8,1]{0,1:T(1,128)} %param.8) | copy-start | bytes 100
  6.7 14.9 %collective-permute-start = (f32[4,64,512]{2,1,0:T(8,128)}, f32[4,64,512]{2,1,0:T(8,128)S(1)}, u32[]{:S(2)}, u32[]{:S(2)}) collective-permute-start(f32[4,64,512]{2,1,0:T(8,128)} %mixed_probes.2.own_a), channel_id=1, source_target_pairs={{0,16},{16,32},{32,48},{48,64},{64,80},{80,96},{96,112},{112,128},... | collective-permute-start | bytes 1572872 | tf_op jit(solution)/shard_map/ppermute | solution.py:367
  10.7 14.6 %collective-permute-start.2 = (f32[4,64,512]{2,1,0:T(8,128)}, f32[4,64,512]{2,1,0:T(8,128)S(1)}, u32[]{:S(2)}, u32[]{:S(2)}) collective-permute-start(f32[4,64,512]{2,1,0:T(8,128)} %mixed_probes.2.own_a), channel_id=1, source_target_pairs={{16,0},{32,16},{48,32},{64,48},{80,64},{96,80},{112,96},{128,112},... | collective-permute-start | bytes 1572872 | tf_op jit(solution)/shard_map/ppermute | solution.py:368
  21.6 7.1 %copy-start.1 = (f32[4,64,512]{2,1,0:T(8,128)}, f32[4,64,512]{2,1,0:T(8,128)S(1)}, u32[]{:S(2)}) copy-start(f32[4,64,512]{2,1,0:T(8,128)S(1)} %collective-permute-done.before_a) | copy-start | bytes 1572868
  21.6 6.2 %collective-permute-start.1 = (f32[4,64,512]{2,1,0:T(8,128)S(1)}, f32[4,64,512]{2,1,0:T(8,128)S(1)}, u32[]{:S(2)}, u32[]{:S(2)}) collective-permute-start(f32[4,64,512]{2,1,0:T(8,128)S(1)} %collective-permute-done.before_a), channel_id=1, source_target_pairs={{0,1},{1,0},{2,3},{3,2},{4,5},{5,4},{6,7},{7,6},{8,9},{9,8},{10,11... | collective-permute-start | bytes 1572872 | tf_op jit(solution)/shard_map/ppermute | solution.py:370
  25.3 3.4 %copy-start.2 = (f32[4,64,512]{2,1,0:T(8,128)}, f32[4,64,512]{2,1,0:T(8,128)S(1)}, u32[]{:S(2)}) copy-start(f32[4,64,512]{2,1,0:T(8,128)S(1)} %collective-permute-done.2.after_a) | copy-start | bytes 1572868
  25.3 3.3 %collective-permute-start.3 = (f32[4,64,512]{2,1,0:T(8,128)S(1)}, f32[4,64,512]{2,1,0:T(8,128)S(1)}, u32[]{:S(2)}, u32[]{:S(2)}) collective-permute-start(f32[4,64,512]{2,1,0:T(8,128)S(1)} %collective-permute-done.2.after_a), channel_id=1, source_target_pairs={{0,1},{1,0},{2,3},{3,2},{4,5},{5,4},{6,7},{7,6},{8,9},{9,8},{10,11... | collective-permute-start | bytes 1572872 | tf_op jit(solution)/shard_map/ppermute | solution.py:371
  27.8 70.4 %copy-start.9 = (s32[8,1]{0,1:T(1,128)S(1)}, s32[8,1]{0,1:T(1,128)}, u32[]{:S(2)}) copy-start(s32[8,1]{0,1:T(1,128)} %param.13) | copy-start | bytes 100
  27.8 0.9 copy-start.3
  28.7 0.8 copy-start.4
  38.3 2.1 %collective-permute-start.4 = (f32[8,64,256]{2,1,0:T(8,128)}, f32[8,64,256]{2,1,0:T(8,128)S(1)}, u32[]{:S(2)}, u32[]{:S(2)}) collective-permute-start(f32[8,64,256]{2,1,0:T(8,128)} %get-tuple-element.10), channel_id=1, source_target_pairs={{0,1},{1,0},{2,3},{3,2},{4,5},{5,4},{6,7},{7,6},{8,9},{9,8},{10,11... | collective-permute-start | bytes 1572872 | tf_op jit(solution)/shard_map/ppermute | solution.py:373
  68.4 2.6 %collective-permute-start.5 = (f32[64,64]{1,0:T(8,128)}, f32[64,64]{1,0:T(8,128)S(1)}, u32[]{:S(2)}, u32[]{:S(2)}) collective-permute-start(f32[64,64]{1,0:T(8,128)} %get-tuple-element.12.gram_ref), channel_id=1, source_target_pairs={{0,1},{1,0},{2,3},{3,2},{4,5},{5,4},{6,7},{7,6},{8,9},{9,8},{10,11... | collective-permute-start | bytes 49160 | tf_op jit(solution)/shard_map/ppermute | solution.py:376
  71.0 0.6 copy-start.6
  97.7 1.8 %copy-start = (bf16[8,64,384]{2,1,0:T(8,128)(2,1)}, bf16[8,64,384]{2,1,0:T(8,128)(2,1)S(1)}, u32[]{:S(2)}) copy-start(bf16[8,64,384]{2,1,0:T(8,128)(2,1)S(1)} %all_to_all.21.own_ref) | copy-start | bytes 1179652
  97.7 1.8 %collective-permute-start.6 = (bf16[8,64,384]{2,1,0:T(8,128)(2,1)S(1)}, bf16[8,64,384]{2,1,0:T(8,128)(2,1)S(1)}, u32[]{:S(2)}, u32[]{:S(2)}) collective-permute-start(bf16[8,64,384]{2,1,0:T(8,128)(2,1)S(1)} %all_to_all.21.own_ref), channel_id=1, source_target_pairs={{0,1},{1,0},{2,3},{3,2},{4,5},{5,4},{6,7},{7,6},{8,9},{9,8},{10,11... | collective-permute-start | bytes 1179656 | tf_op jit(solution)/shard_map/ppermute | solution.py:378
  99.5 0.8 copy-start.5

commit v2 on v1

v2 whole, which is shorter than its diff:
```python
import functools
import math

import jax
import jax.numpy as jnp
from jax import lax
from jax.experimental import pallas as pl
from jax.experimental.pallas import tpu as pltpu
from jax.sharding import PartitionSpec as P

RANK = 64
REACH = 8
LANES = 128
PANEL = 8

f32 = jnp.float32
bf16 = jnp.bfloat16
highest = lax.Precision.HIGHEST

HBM = pl.BlockSpec(memory_space=pltpu.HBM)
SMEM = pl.BlockSpec(memory_space=pltpu.SMEM)
VMEM = pl.BlockSpec(memory_space=pltpu.VMEM)

LIMIT = pltpu.CompilerParams(vmem_limit_bytes=24 << 20)

NN = (((1,), (0,)), ((), ()))
NT = (((1,), (1,)), ((), ()))
TN = (((0,), (0,)), ((), ()))


def dot(a, b, dims, precision=None):
    return lax.dot_general(a, b, dims, precision=precision, preferred_element_type=f32)


def pieces(x):
    high = x.astype(bf16)
    rest = x - high.astype(f32)
    middle = rest.astype(bf16)
    low = (rest - middle.astype(f32)).astype(bf16)
    return high, middle, low


def in_vmem(x):
    return pltpu.with_memory_space_constraint(x, pltpu.VMEM)


def factor(gram):
    n = gram.shape[0]
    row = lax.broadcasted_iota(jnp.int32, (n, n), 0)
    col = lax.broadcasted_iota(jnp.int32, (n, n), 1)
    tall = lax.broadcasted_iota(jnp.int32, (PANEL, 2 * n), 0)
    work = jnp.concatenate([gram, (row == col).astype(f32)], axis=1)
    panels = [work[k : k + PANEL] for k in range(0, n, PANEL)]
    for k in range(len(panels)):
        columns = [
            [
                jnp.broadcast_to(panels[t][:, k * PANEL + j : k * PANEL + j + 1], (PANEL, 2 * n))
                for j in range(PANEL)
            ]
            for t in range(k, len(panels))
        ]
        scales = jnp.zeros((PANEL, 2 * n), f32)
        for j in range(PANEL):
            inverse = 1.0 / columns[0][j][j : j + 1]
            scales = jnp.where(tall == j, inverse, scales)
            entries = [columns[0][i][j : j + 1] for i in range(PANEL)]
            pivot_row = panels[k][j : j + 1]
            for t in range(k, len(panels)):
                multiplier = columns[t - k][j] * inverse
                if t == k:
                    if j == PANEL - 1:
                        continue
                    multiplier = jnp.where(tall > j, multiplier, 0.0)
                for i in range(j + 1, PANEL):
                    columns[t - k][i] = columns[t - k][i] - multiplier * entries[i]
                panels[t] = panels[t] - multiplier * pivot_row
        panels[k] = panels[k] * jnp.sqrt(scales)
    work = jnp.concatenate(panels, axis=0)
    upper = jnp.where(col >= row, work[:, :n], 0.0)
    return upper, work[:, n:]


def weights_of(x):
    high, middle, low = (piece.astype(f32) for piece in pieces(x))
    lane = lax.broadcasted_iota(jnp.int32, x.shape, 1)
    return jnp.concatenate([jnp.where(lane < RANK, high, middle), low], axis=1).astype(bf16)


def weighted(x, weights):
    terms = dot(x, weights, NN)
    first, last = terms[:, :LANES], terms[:, LANES:]
    return first + pltpu.roll(first, RANK, 1) + last


def folded(x):
    rows = x.shape[0] // 2
    lane = lax.broadcasted_iota(jnp.int32, (rows, LANES), 1)
    return jnp.where(lane < RANK, x[:rows], x[rows:])


def unfolded(x):
    lane = lax.broadcasted_iota(jnp.int32, x.shape, 1)
    turned = pltpu.roll(x, RANK, 1)
    return jnp.concatenate([jnp.where(lane < RANK, x, turned), jnp.where(lane < RANK, turned, x)], axis=0)


def mixed_probes_kernel(half_ref, mixing_hbm, probes_ref, out_ref, mixing_ref, tiles_ref, sems):
    part = out_ref.shape[0]
    start = half_ref[0] * part
    first = pltpu.make_async_copy(mixing_hbm, mixing_ref, sems.at[part])
    copies = [pltpu.make_async_copy(probes_ref.at[start + i], tiles_ref.at[i], sems.at[i]) for i in range(part)]
    for copy in [first] + copies:
        copy.start()
    first.wait()
    mixing = mixing_ref[...]
    weights = weights_of(jnp.concatenate([mixing, mixing], axis=0).T)
    for i, copy in enumerate(copies):
        copy.wait()
        out_ref[i] = folded(weighted(tiles_ref[i], weights))


def mixed_probes(half, mixing, probes):
    count, rows, width = probes.shape
    part = count // 2
    return pl.pallas_call(
        mixed_probes_kernel,
        out_shape=pltpu.VMEM((part, rows // 2, LANES), f32),
        in_specs=[SMEM, HBM, HBM],
        out_specs=VMEM,
        scratch_shapes=[
            pltpu.VMEM(mixing.shape, f32),
            pltpu.VMEM((part, rows, width), bf16),
            pltpu.SemaphoreType.DMA((part + 1,)),
        ],
        cost_estimate=pl.CostEstimate(
            flops=2 * part * rows * width * 3 * RANK,
            bytes_accessed=part * rows * (2 * width + 4 * RANK),
            transcendentals=0,
        ),
        compiler_params=LIMIT,
        name="mixed_probes",
    )(half, mixing, probes)


def sketch_kernel(
    meta_ref, own_a, own_b, before_a, before_b, after_a, after_b, near_ref, keep_ref, send_ref, pick_ref
):
    count = near_ref.shape[0]
    part = own_a.shape[0]
    core = meta_ref[2 * count]

    def pick(i):
        column = jnp.clip(meta_ref[i], 0, 6 * part - 1)
        group = column // part
        place = column % part
        for s, sides in enumerate(((before_a, before_b), (own_a, own_b), (after_a, after_b))):
            for h, side in enumerate(sides):

                @pl.when(group == 2 * s + (core if h == 0 else 1 - core))
                def _():
                    pick_ref[i] = side[place]

    for i in range(count):
        pick(i)
    for i in range(count):
        mixed = folded(weighted(near_ref[i, 0], weights_of(unfolded(pick_ref[i]))))
        mixed = jnp.where(meta_ref[count + i] > 0, mixed, 0.0)
        rows = mixed.shape[0] // 2
        keep_ref[i] = jnp.where(core == 0, mixed[:rows], mixed[rows:])
        send_ref[i] = jnp.where(core == 0, mixed[rows:], mixed[:rows])


def compress(meta, parts, near_tiles):
    count, _, rows, width = near_tiles.shape
    shape = pltpu.VMEM((count, rows // 4, LANES), f32)
    return pl.pallas_call(
        sketch_kernel,
        out_shape=(shape, shape),
        in_specs=[SMEM] + [VMEM] * 7,
        out_specs=(VMEM, VMEM),
        scratch_shapes=[pltpu.VMEM((count, rows // 2, LANES), f32)],
        cost_estimate=pl.CostEstimate(
            flops=2 * count * rows * width * 3 * RANK,
            bytes_accessed=count * rows * (2 * width + 16 * RANK),
            transcendentals=0,
        ),
        compiler_params=LIMIT,
        name="compress",
    )(meta, *[in_vmem(part) for part in parts], in_vmem(near_tiles))


def gram_kernel(terms_ref, mixed_ref, gram_ref):
    total = terms_ref[0]
    for k in range(1, terms_ref.shape[0]):
        total = total + terms_ref[k]
    mixed = total.T
    mixed_ref[...] = mixed
    first, second = mixed[:RANK], mixed[RANK:]
    gram_ref[...] = dot(first, first, NT, highest) + dot(second, second, NT, highest)


def gram_of(terms):
    return pl.pallas_call(
        gram_kernel,
        out_shape=(
            pltpu.VMEM((terms.shape[2], terms.shape[1]), f32),
            pltpu.VMEM((RANK, RANK), f32),
        ),
        in_specs=[VMEM],
        out_specs=(VMEM, VMEM),
        compiler_params=LIMIT,
        name="gram",
    )(in_vmem(terms))


def basis_kernel(core_ref, mixed_ref, gram_ref, other_ref, out_ref):
    upper, inverse = factor(gram_ref[...] + other_ref[...])
    basis = [dot(inverse, mixed_ref[k : k + RANK], NN, highest) for k in (0, RANK)]
    half = RANK // 2
    rows = jnp.where(core_ref[0] == 0, upper[:half], upper[half:])
    high, middle, low = (piece.astype(f32) for piece in pieces(rows))
    left = jnp.concatenate([high, middle], axis=0)
    right = jnp.concatenate([low, jnp.zeros_like(low)], axis=0)
    block = jnp.concatenate(basis + [left, right], axis=1).astype(bf16)
    for k in range(out_ref.shape[0]):
        out_ref[k] = block


def basis_of(core, mixed, gram, other, copies):
    return pl.pallas_call(
        basis_kernel,
        out_shape=pltpu.VMEM((copies, RANK, 2 * mixed.shape[1] + LANES), bf16),
        in_specs=[SMEM, VMEM, VMEM, VMEM],
        out_specs=VMEM,
        compiler_params=LIMIT,
        name="basis",
    )(core, in_vmem(mixed), in_vmem(gram), in_vmem(other))


def spread_kernel(meta_ref, own_ref, other_ref, out_ref, basis_ref, upper_ref, work_ref):
    count = own_ref.shape[0]
    groups = out_ref.shape[0] // count
    blocks = RANK // groups
    width = own_ref.shape[2] - LANES
    half = RANK // 2
    tiles = work_ref.shape[0]
    first = meta_ref[count] == 0
    total = jnp.zeros((RANK, RANK), f32)
    for r in range(count):
        mine, others = own_ref[r].astype(f32), other_ref[r].astype(f32)
        sides = (jnp.where(first, mine, others), jnp.where(first, others, mine))
        uppers = []
        for h, side in enumerate(sides):
            for t in range(width // LANES):
                strip = side[:, t * LANES : (t + 1) * LANES]
                place = 2 * t + h
                basis_ref[r, :, place * LANES : (place + 1) * LANES] = strip.astype(bf16)
                for q in range(blocks):
                    work_ref[2 * q * width // LANES + place, pl.ds(r, groups, stride=count), :] = strip[
                        q * groups : (q + 1) * groups
                    ]
            uppers.append(
                side[:half, width : width + RANK]
                + side[half:, width : width + RANK]
                + side[:half, width + RANK :]
            )
        upper = jnp.concatenate(uppers, axis=0)
        upper_ref[r] = upper
        total = total + dot(upper, upper, TN, highest)
        work_ref[tiles - 2, pl.ds(r, groups, stride=count), :] = jnp.full(
            (groups, LANES), meta_ref[r].astype(f32), f32
        )
    work_ref[tiles - 1] = jnp.zeros((groups * count, LANES), f32)
    for p in range(2):
        low_row = 2 * p * groups
        packed = jnp.concatenate(
            [total[low_row : low_row + groups], total[low_row + groups : low_row + 2 * groups]], axis=1
        )
        for k, piece in enumerate(pieces(packed)):
            work_ref[tiles - 1, pl.ds(2 * k + p, groups, stride=count), :] = piece.astype(f32)
    for t in range(tiles):
        out_ref[:, t * LANES : (t + 1) * LANES] = work_ref[t].astype(bf16)


def spread(meta, own, other, groups):
    count, _, width = own.shape
    rows = 2 * (width - LANES)
    total = RANK // groups * rows + 2 * LANES
    return pl.pallas_call(
        spread_kernel,
        out_shape=(
            pltpu.VMEM((groups * count, total), bf16),
            pltpu.VMEM((count, RANK, rows), bf16),
            pltpu.VMEM((count, RANK, RANK), f32),
        ),
        in_specs=[SMEM, VMEM, VMEM],
        out_specs=(VMEM, VMEM, VMEM),
        scratch_shapes=[pltpu.VMEM((total // LANES, groups * count, LANES), f32)],
        compiler_params=LIMIT,
        name="spread",
    )(meta, in_vmem(own), in_vmem(other))


def choose_kernel(count, in_ref, out_ref):
    clusters, total = in_ref.shape
    body = total - 2 * LANES
    wanted = in_ref[:, body : body + LANES].astype(f32)
    column = lax.broadcasted_iota(jnp.int32, (clusters, clusters), 1).astype(f32)
    select = (wanted == column).astype(bf16)
    out_ref[:, :body] = dot(select, in_ref[:, :body], NN).astype(bf16)
    row = lax.broadcasted_iota(jnp.int32, (count, clusters), 0)
    column = lax.broadcasted_iota(jnp.int32, (count, clusters), 1) % count
    gather = (((column == row) | (column == row + 2) | (column == row + 4)) & (row < 2)).astype(bf16)
    sums = dot(gather, in_ref[:, body + LANES :], NN)[:2]
    block = jnp.concatenate([piece.astype(f32) for piece in pieces(sums)] + [jnp.zeros((count - 6, LANES), f32)], axis=0)
    out_ref[:, body:] = jnp.concatenate([block] * (clusters // count), axis=0).astype(bf16)


def choose(received, count):
    rows, total = received.shape
    return pl.pallas_call(
        functools.partial(choose_kernel, count),
        out_shape=pltpu.VMEM((rows, total - LANES), bf16),
        in_specs=[VMEM],
        out_specs=VMEM,
        compiler_params=LIMIT,
        name="choose",
    )(in_vmem(received))


def couple_kernel(
    scale, basis_ref, upper_ref, received_ref, far_ref, coupling_ref, root_ref, work_ref
):
    count = upper_ref.shape[0]
    rows, total = received_ref.shape
    groups = rows // count
    blocks = RANK // groups
    wide = (total - LANES) // blocks // LANES
    tiles = work_ref.shape[0]
    for t in range(tiles):
        work_ref[t] = received_ref[:, t * LANES : (t + 1) * LANES].astype(f32)
    parts = []
    for p in range(2):
        packed = sum(work_ref[tiles - 1, pl.ds(2 * k + p, groups, stride=count), :] for k in range(3))
        parts += [packed[:, :RANK], packed[:, RANK:]]
    _, inverse = factor(jnp.concatenate(parts, axis=0))
    for i in range(count):
        far = [
            jnp.concatenate(
                [work_ref[q * wide + t, pl.ds(i, groups, stride=count), :] for t in range(wide)], axis=1
            )
            for q in range(blocks)
        ]
        far = jnp.concatenate(far, axis=0).astype(bf16)
        image = dot(far_ref[i, 0], far, NT)
        terms = dot(basis_ref[i], jnp.concatenate(pieces(image), axis=1), NN)
        coupling_ref[i, 0] = terms[:, :RANK] + terms[:, RANK : 2 * RANK] + terms[:, 2 * RANK :]
    for r in range(count):
        root_ref[r] = dot(upper_ref[r], inverse, NT, highest) * scale


def couple(basis, upper, received, far_tiles, scale):
    count = far_tiles.shape[0]
    return pl.pallas_call(
        functools.partial(couple_kernel, scale),
        out_shape=(
            jax.ShapeDtypeStruct((count, 1, RANK, RANK), f32),
            jax.ShapeDtypeStruct((count, RANK, RANK), f32),
        ),
        in_specs=[VMEM] * 4,
        out_specs=(VMEM, VMEM),
        scratch_shapes=[pltpu.VMEM((received.shape[1] // LANES, received.shape[0], LANES), f32)],
        compiler_params=LIMIT,
        name="couple",
    )(in_vmem(basis), in_vmem(upper), in_vmem(received), in_vmem(far_tiles))


def shards(near_tiles, near_cols, near_count, probes, mixing, far_tiles, far_cols):
    count = probes.shape[0]
    subtrees = lax.axis_size("leaf")
    members = lax.axis_size("blk")
    leaf_pos = lax.axis_index("leaf")
    blk_pos = lax.axis_index("blk")
    core = blk_pos % 2
    up = [(i, i + 1) for i in range(subtrees - 1)]
    down = [(j, i) for i, j in up]
    pair = [(i, i ^ 1) for i in range(members)]
    lanes = [list(range(c, members, 2)) for c in range(2)]

    core_vec = core.reshape(1).astype(jnp.int32)
    live = (blk_pos < near_count).astype(jnp.int32)
    near_meta = jnp.concatenate([near_cols[:, 0] - (leaf_pos * count - REACH), live, core_vec])
    far_meta = jnp.concatenate([far_cols[:, 0], core_vec])

    mixing, probes = (pltpu.with_memory_space_constraint(x, pltpu.HBM) for x in (mixing.T, probes))
    own_a = mixed_probes(core_vec, mixing, probes)
    before_a = lax.ppermute(own_a, "leaf", up)
    after_a = lax.ppermute(own_a, "leaf", down)
    own_b = mixed_probes(1 - core_vec, mixing, probes)
    before_b = lax.ppermute(before_a, "blk", pair)
    after_b = lax.ppermute(after_a, "blk", pair)
    keep, send = compress(near_meta, (own_a, own_b, before_a, before_b, after_a, after_b), near_tiles)
    halves = keep + lax.ppermute(send, "blk", pair)
    terms = lax.all_to_all(halves, "blk", 0, 0, tiled=True, axis_index_groups=lanes)
    mixed, gram = gram_of(terms)
    own = basis_of(core_vec, mixed, gram, lax.ppermute(gram, "blk", pair), count)
    own = lax.all_to_all(own, "blk", 0, 0, tiled=True, axis_index_groups=lanes)
    other = lax.ppermute(own, "blk", pair)
    payload, basis, upper = spread(far_meta, own, other, subtrees)
    slices = lax.all_to_all(payload.reshape(subtrees, count, -1), "leaf", 0, 0, tiled=True)
    chosen = choose(slices.reshape(payload.shape), count)
    received = lax.all_to_all(chosen.reshape(subtrees, count, -1), "leaf", 0, 0, tiled=True)
    scale = math.sqrt(subtrees * count * RANK)
    return couple(basis, upper, received.reshape(chosen.shape), far_tiles, scale)


def solution(mesh):
    in_specs = (
        P("leaf", "blk", None, None),
        P("leaf", "blk"),
        P("leaf"),
        P("leaf", None, None),
        P(),
        P("leaf", "blk", None, None),
        P("leaf", "blk"),
    )
    out_specs = (P("leaf", "blk", None, None), P("leaf", None, None))
    return jax.shard_map(shards, mesh=mesh, in_specs=in_specs, out_specs=out_specs, check_vma=False)
```

time: 155 us -> 120 us (0.77)
  Pallas kernels: 46.2 us -> 18.9 us
  local copies, waits for them, and re-layouts: 3.91 us -> 0.02 us
  blocking collectives: 77.6 us -> 75 us
  other arithmetic: 2.29 us -> 0.22 us
    pallas_call x7, Pallas kernels: 32.2 us -> 13.2 us  [the longest x2 6.38 us: mixed_probes(): pl.pallas_call(mixed_probes_kernel, out_shape=pltpu.VMEM((part, rows // 2...]
    pallas_call x1, Pallas kernels: 14 us -> 5.73 us  [couple(): pl.pallas_call(functools.partial(couple_kernel, scale), out_shape=(jax.Sh...]
    unnamed x21 -> x10, local copies, waits for them, and re-layouts: 3.91 us -> 0.02 us
  transfers between devices with their start and end apart: 7 -> 7, of which waited for: 6 -> 6; matrix products, arithmetic and copies ran while one was open for 1% -> 0% of each run, Pallas kernels for 3% -> 3%
where the time goes in v2:
time: 120 us
  blocking collectives  75 us (62%)
  Pallas kernels  18.9 us (16%)
  waiting for transfers between devices  13.4 us (11%)
  starting transfers between devices  11.5 us (10%)
    all_to_all x1, blocking collectives, shards(): lax.all_to_all(halves, 'blk', 0, 0, tiled=True, axis_index_groups=lanes)  25 us
    all_to_all x1, blocking collectives, shards(): lax.all_to_all(payload.reshape(subtrees, count, -1), 'leaf', 0, 0, tiled=...  19.2 us
    all_to_all x1, blocking collectives, shards(): own = lax.all_to_all(own, 'blk', 0, 0, tiled=True, axis_index_groups=lanes)  17.5 us
    all_to_all x1, blocking collectives, shards(): lax.all_to_all(chosen.reshape(subtrees, count, -1), 'leaf', 0, 0, tiled=T...  13.3 us
    pallas_call x2, Pallas kernels, mixed_probes(): pl.pallas_call(mixed_probes_kernel, out_shape=pltpu.VMEM((part, rows // 2...  6.38 us
    ppermute x1, waiting for transfers between devices, shards(): before_a = lax.ppermute(own_a, 'leaf', up)  5.97 us
    pallas_call x1, Pallas kernels, couple(): pl.pallas_call(functools.partial(couple_kernel, scale), out_shape=(jax.Sh...  5.73 us
    ppermute x1, starting transfers between devices, shards(): before_a = lax.ppermute(own_a, 'leaf', up)  4.05 us
  transfers between devices with their start and end apart: 7, of which 6 were waited for; matrix products, arithmetic and copies ran while one was open for 0% of the time, Pallas kernels for 3%

profile of v2, /device:TPU:1, one launch (start us, length us, event | category | flops | bytes accessed | tf_op | source)
XLA Modules:
  0.0 119.8 jit_solution(16023946252294175307)
XLA Ops:
  0.6 0.0 copy-start.2
  0.7 0.0 copy-start.3
  0.7 3.1 %mixed_probes.2.own_a = f32[4,256,128]{2,1,0:T(8,128)S(1)} custom-call(s32[1]{0:T(128)} %bitcast.1.half_ref.core_ref, f32[64,512]{1,0:T(8,128)} %bitcast.13, bf16[8,512,512]{2,1,0:T(8,128)(2,1)} %probes_ref.3), custom_call_target="tpu_custom_call" | custom-call | flops 402653184 | bytes 2621440 | tf_op jit(solution)/shard_map/mixed_probes/pallas_call | solution.py:125
  3.8 4.1 %collective-permute-start = (f32[4,256,128]{2,1,0:T(8,128)S(1)}, f32[4,256,128]{2,1,0:T(8,128)S(1)}, u32[]{:S(2)}, u32[]{:S(2)}) collective-permute-start(f32[4,256,128]{2,1,0:T(8,128)S(1)} %mixed_probes.2.own_a), channel_id=1, source_target_pairs={{0,16},{16,32},{32,48},{48,64},{64,80},{80,96},{96,112},{112,128},... | collective-permute-start | bytes 1572872 | tf_op jit(solution)/shard_map/ppermute | solution.py:397
  7.9 1.3 %collective-permute-start.2 = (f32[4,256,128]{2,1,0:T(8,128)S(1)}, f32[4,256,128]{2,1,0:T(8,128)S(1)}, u32[]{:S(2)}, u32[]{:S(2)}) collective-permute-start(f32[4,256,128]{2,1,0:T(8,128)S(1)} %mixed_probes.2.own_a), channel_id=1, source_target_pairs={{16,0},{32,16},{48,32},{64,48},{80,64},{96,80},{112,96},{128,112},... | collective-permute-start | bytes 1572872 | tf_op jit(solution)/shard_map/ppermute | solution.py:398
  9.2 0.0 copy-start
  9.2 3.3 %mixed_probes.3.own_b = f32[4,256,128]{2,1,0:T(8,128)S(1)} custom-call(s32[1]{0:T(128)S(6)} %sub.19.half_ref, f32[64,512]{1,0:T(8,128)} %bitcast.14, bf16[8,512,512]{2,1,0:T(8,128)(2,1)} %probes_ref.3), custom_call_target="tpu_custom_call" | custom-call | flops 402653184 | bytes 2621440 | tf_op jit(solution)/shard_map/mixed_probes/pallas_call | solution.py:125
  12.4 6.0 %collective-permute-done.before_a = f32[4,256,128]{2,1,0:T(8,128)S(1)} collective-permute-done((f32[4,256,128]{2,1,0:T(8,128)S(1)}, f32[4,256,128]{2,1,0:T(8,128)S(1)}, u32[]{:S(2)}, u32[]{:S(2)}) %collective-permute-start) | collective-permute-done | bytes 524320 | tf_op jit(solution)/shard_map/ppermute | solution.py:397
  18.4 1.5 %collective-permute-start.1 = (f32[4,256,128]{2,1,0:T(8,128)S(1)}, f32[4,256,128]{2,1,0:T(8,128)S(1)}, u32[]{:S(2)}, u32[]{:S(2)}) collective-permute-start(f32[4,256,128]{2,1,0:T(8,128)S(1)} %collective-permute-done.before_a), channel_id=1, source_target_pairs={{0,1},{1,0},{2,3},{3,2},{4,5},{5,4},{6,7},{7,6},{8,9},{9,8},{10,11... | collective-permute-start | bytes 1572872 | tf_op jit(solution)/shard_map/ppermute | solution.py:400
  19.9 2.3 %collective-permute-done.2.after_a = f32[4,256,128]{2,1,0:T(8,128)S(1)} collective-permute-done((f32[4,256,128]{2,1,0:T(8,128)S(1)}, f32[4,256,128]{2,1,0:T(8,128)S(1)}, u32[]{:S(2)}, u32[]{:S(2)}) %collective-permute-start.2) | collective-permute-done | bytes 524320 | tf_op jit(solution)/shard_map/ppermute | solution.py:398
  22.3 1.8 %collective-permute-start.3 = (f32[4,256,128]{2,1,0:T(8,128)S(1)}, f32[4,256,128]{2,1,0:T(8,128)S(1)}, u32[]{:S(2)}, u32[]{:S(2)}) collective-permute-start(f32[4,256,128]{2,1,0:T(8,128)S(1)} %collective-permute-done.2.after_a), channel_id=1, source_target_pairs={{0,1},{1,0},{2,3},{3,2},{4,5},{5,4},{6,7},{7,6},{8,9},{9,8},{10,11... | collective-permute-start | bytes 1572872 | tf_op jit(solution)/shard_map/ppermute | solution.py:401
  24.1 0.0 copy-done.2
  24.1 0.0 copy-done.3
  24.1 0.1 pad_add_fusion.1.meta_ref
  24.2 0.0 copy-start.4
  24.2 0.0 collective-permute-done.1.before_b
  24.2 1.4 %collective-permute-done.3.after_b = f32[4,256,128]{2,1,0:T(8,128)S(1)} collective-permute-done((f32[4,256,128]{2,1,0:T(8,128)S(1)}, f32[4,256,128]{2,1,0:T(8,128)S(1)}, u32[]{:S(2)}, u32[]{:S(2)}) %collective-permute-start.3) | collective-permute-done | bytes 524320 | tf_op jit(solution)/shard_map/ppermute | solution.py:401
  25.6 0.0 copy-done
  25.6 2.7 %compress.1 = (f32[8,128,128]{2,1,0:T(8,128)S(1)}, f32[8,128,128]{2,1,0:T(8,128)S(1)}) custom-call(s32[17]{0:T(128)S(1)} %pad_add_fusion.1.meta_ref, f32[4,256,128]{2,1,0:T(8,128)S(1)} %mixed_probes.2.own_a, f32[4,256,128]{2,1,0:T(8,128)S(1)} %mixed_probes.3.own_b, f32[4,256,128]{2,1,0:T(8,128)S(1)} %collective-permute-done.before_a, ...), custom_call_target="tpu_custom_call" | custom-call | flops 805306368 | bytes 8388608 | tf_op jit(solution)/shard_map/compress/pallas_call | solution.py:176
  28.4 0.5 collective-permute-start.4
  28.8 1.5 %collective-permute-done.4 = f32[8,128,128]{2,1,0:T(8,128)S(1)} collective-permute-done((f32[8,128,128]{2,1,0:T(8,128)S(1)}, f32[8,128,128]{2,1,0:T(8,128)S(1)}, u32[]{:S(2)}, u32[]{:S(2)}) %collective-permute-start.4) | collective-permute-done | bytes 524320 | tf_op jit(solution)/shard_map/ppermute | solution.py:403
  30.4 0.0 copy-start.1
  30.4 0.1 add.9
  30.4 25.0 %all_to_all.20.terms_ref = f32[8,128,128]{2,1,0:T(8,128)S(1)} all-to-all(f32[8,128,128]{2,1,0:T(8,128)S(1)} %add.9), channel_id=1, replica_groups={{0,2,4,6,8,10,12,14},{1,3,5,7,9,11,13,15},{16,18,20,22,24,26,28,30},{17..., dimensions={0} | all-to-all | bytes 1048576 | tf_op jit(solution)/shard_map/all_to_all | solution.py:404
  55.4 0.3 gram.1
  55.7 1.8 %collective-permute-start.5 = (f32[64,64]{1,0:T(8,128)S(1)}, f32[64,64]{1,0:T(8,128)S(1)}, u32[]{:S(2)}, u32[]{:S(2)}) collective-permute-start(f32[64,64]{1,0:T(8,128)S(1)} %get-tuple-element.12.gram_ref), channel_id=1, source_target_pairs={{0,1},{1,0},{2,3},{3,2},{4,5},{5,4},{6,7},{7,6},{8,9},{9,8},{10,11... | collective-permute-start | bytes 49160 | tf_op jit(solution)/shard_map/ppermute | solution.py:406
  57.5 0.9 collective-permute-done.5.other_ref
  58.4 2.0 %basis.1 = bf16[8,64,384]{2,1,0:T(8,128)(2,1)S(1)} custom-call(s32[1]{0:T(128)} %bitcast.1.half_ref.core_ref, f32[128,128]{1,0:T(8,128)S(1)} %get-tuple-element.11.mixed_ref, f32[64,64]{1,0:T(8,128)S(1)} %get-tuple-element.12.gram_ref, f32[64,64]{1,0:T(8,128)S(1)} %collective-permute-done.5.other_ref), custom_call_target="tpu_custom_call" | custom-call | tf_op jit(solution)/shard_map/basis/pallas_call | solution.py:230
  60.4 17.5 %all_to_all.21.own_ref = bf16[8,64,384]{2,1,0:T(8,128)(2,1)S(1)} all-to-all(bf16[8,64,384]{2,1,0:T(8,128)(2,1)S(1)} %basis.1), channel_id=1, replica_groups={{0,2,4,6,8,10,12,14},{1,3,5,7,9,11,13,15},{16,18,20,22,24,26,28,30},{17..., dimensions={0} | all-to-all | bytes 786432 | tf_op jit(solution)/shard_map/all_to_all | solution.py:407
  78.0 0.5 collective-permute-start.6
  78.5 0.0 copy-done.4
  78.5 0.1 pad_add_fusion.meta_ref
  78.5 1.3 %collective-permute-done.6.other_ref = bf16[8,64,384]{2,1,0:T(8,128)(2,1)S(1)} collective-permute-done((bf16[8,64,384]{2,1,0:T(8,128)(2,1)S(1)}, bf16[8,64,384]{2,1,0:T(8,128)(2,1)S(1)}, u32[]{:S(2)}, u32[]{:S(2)}) %collective-permute-start.6) | collective-permute-done | bytes 393248 | tf_op jit(solution)/shard_map/ppermute | solution.py:408
  79.8 1.5 %spread.1 = (bf16[128,2304]{1,0:T(8,128)(2,1)S(1)}, bf16[8,64,512]{2,1,0:T(8,128)(2,1)S(1)}, f32[8,64,64]{2,1,0:T(8,128)S(1)}) custom-call(s32[9]{0:T(128)S(1)} %pad_add_fusion.meta_ref, bf16[8,64,384]{2,1,0:T(8,128)(2,1)S(1)} %all_to_all.21.own_ref, bf16[8,64,384]{2,1,0:T(8,128)(2,1)S(1)} %collective-permute-done.6.other_ref), custom_call_target="tpu_custom_call" | custom-call | tf_op jit(solution)/shard_map/spread/pallas_call | solution.py:289
  81.3 19.2 %all_to_all.22 = bf16[16,8,2304]{2,1,0:T(8,128)(2,1)S(1)} all-to-all(bf16[16,8,2304]{2,1,0:T(8,128)(2,1)S(1)} %bitcast.12), channel_id=1, replica_groups=mesh['leaf'=16,'blk'=16] {'leaf'}, dimensions={0} | all-to-all | bytes 1179648 | tf_op jit(solution)/shard_map/all_to_all | solution.py:410
  100.5 0.3 choose.1
  100.8 13.3 %all_to_all.23 = bf16[16,8,2176]{2,1,0:T(8,128)(2,1)S(1)} all-to-all(bf16[16,8,2176]{2,1,0:T(8,128)(2,1)S(1)} %bitcast.10), channel_id=1, replica_groups=mesh['leaf'=16,'blk'=16] {'leaf'}, dimensions={0} | all-to-all | bytes 1114112 | tf_op jit(solution)/shard_map/all_to_all | solution.py:412
  114.1 0.0 copy-done.1
  114.1 5.7 %couple.1 = (f32[8,1,64,64]{3,2,1,0:T(8,128)}, f32[8,64,64]{2,1,0:T(8,128)}) custom-call(bf16[8,64,512]{2,1,0:T(8,128)(2,1)S(1)} %get-tuple-element.13.basis_ref, f32[8,64,64]{2,1,0:T(8,128)S(1)} %get-tuple-element.14.upper_ref, bf16[128,2176]{1,0:T(8,128)(2,1)S(1)} %bitcast.11, bf16[8,1,512,512]{3,2,1,0:T(8,128)(2,1)S(1)} %copy-done.1), custom_call_target="tpu_custom_call" | custom-call | tf_op jit(solution)/shard_map/couple/pallas_call | solution.py:364
  (2 shorter events, 0.0 us)
Async XLA Ops:
  0.6 23.4 %copy-start.2 = (s32[8]{0:T(128)S(1)}, s32[8]{0:T(128)}, u32[]{:S(2)}) copy-start(s32[8]{0:T(128)} %param.9) | copy-start | bytes 100
  0.7 23.4 %copy-start.3 = (s32[8,1]{0,1:T(1,128)S(1)}, s32[8,1]{0,1:T(1,128)}, u32[]{:S(2)}) copy-start(s32[8,1]{0,1:T(1,128)} %param.8) | copy-start | bytes 100
  3.8 14.6 %collective-permute-start = (f32[4,256,128]{2,1,0:T(8,128)S(1)}, f32[4,256,128]{2,1,0:T(8,128)S(1)}, u32[]{:S(2)}, u32[]{:S(2)}) collective-permute-start(f32[4,256,128]{2,1,0:T(8,128)S(1)} %mixed_probes.2.own_a), channel_id=1, source_target_pairs={{0,16},{16,32},{32,48},{48,64},{64,80},{80,96},{96,112},{112,128},... | collective-permute-start | bytes 1572872 | tf_op jit(solution)/shard_map/ppermute | solution.py:397
  7.9 14.4 %collective-permute-start.2 = (f32[4,256,128]{2,1,0:T(8,128)S(1)}, f32[4,256,128]{2,1,0:T(8,128)S(1)}, u32[]{:S(2)}, u32[]{:S(2)}) collective-permute-start(f32[4,256,128]{2,1,0:T(8,128)S(1)} %mixed_probes.2.own_a), channel_id=1, source_target_pairs={{16,0},{32,16},{48,32},{64,48},{80,64},{96,80},{112,96},{128,112},... | collective-permute-start | bytes 1572872 | tf_op jit(solution)/shard_map/ppermute | solution.py:398
  9.2 16.5 %copy-start = (bf16[8,1,512,512]{3,2,1,0:T(8,128)(2,1)S(1)}, bf16[8,1,512,512]{3,2,1,0:T(8,128)(2,1)}, u32[]{:S(2)}) copy-start(bf16[8,1,512,512]{3,2,1,0:T(8,128)(2,1)} %near_ref.1) | copy-start | bytes 12582916
  18.4 5.8 %collective-permute-start.1 = (f32[4,256,128]{2,1,0:T(8,128)S(1)}, f32[4,256,128]{2,1,0:T(8,128)S(1)}, u32[]{:S(2)}, u32[]{:S(2)}) collective-permute-start(f32[4,256,128]{2,1,0:T(8,128)S(1)} %collective-permute-done.before_a), channel_id=1, source_target_pairs={{0,1},{1,0},{2,3},{3,2},{4,5},{5,4},{6,7},{7,6},{8,9},{9,8},{10,11... | collective-permute-start | bytes 1572872 | tf_op jit(solution)/shard_map/ppermute | solution.py:400
  22.3 3.4 %collective-permute-start.3 = (f32[4,256,128]{2,1,0:T(8,128)S(1)}, f32[4,256,128]{2,1,0:T(8,128)S(1)}, u32[]{:S(2)}, u32[]{:S(2)}) collective-permute-start(f32[4,256,128]{2,1,0:T(8,128)S(1)} %collective-permute-done.2.after_a), channel_id=1, source_target_pairs={{0,1},{1,0},{2,3},{3,2},{4,5},{5,4},{6,7},{7,6},{8,9},{9,8},{10,11... | collective-permute-start | bytes 1572872 | tf_op jit(solution)/shard_map/ppermute | solution.py:401
  24.2 54.3 %copy-start.4 = (s32[8,1]{0,1:T(1,128)S(1)}, s32[8,1]{0,1:T(1,128)}, u32[]{:S(2)}) copy-start(s32[8,1]{0,1:T(1,128)} %param.13) | copy-start | bytes 100
  28.4 2.0 %collective-permute-start.4 = (f32[8,128,128]{2,1,0:T(8,128)S(1)}, f32[8,128,128]{2,1,0:T(8,128)S(1)}, u32[]{:S(2)}, u32[]{:S(2)}) collective-permute-start(f32[8,128,128]{2,1,0:T(8,128)S(1)} %get-tuple-element.10), channel_id=1, source_target_pairs={{0,1},{1,0},{2,3},{3,2},{4,5},{5,4},{6,7},{7,6},{8,9},{9,8},{10,11... | collective-permute-start | bytes 1572872 | tf_op jit(solution)/shard_map/ppermute | solution.py:403
  30.4 83.7 %copy-start.1 = (bf16[8,1,512,512]{3,2,1,0:T(8,128)(2,1)S(1)}, bf16[8,1,512,512]{3,2,1,0:T(8,128)(2,1)}, u32[]{:S(2)}) copy-start(bf16[8,1,512,512]{3,2,1,0:T(8,128)(2,1)} %far_ref.1) | copy-start | bytes 12582916
  55.7 2.7 %collective-permute-start.5 = (f32[64,64]{1,0:T(8,128)S(1)}, f32[64,64]{1,0:T(8,128)S(1)}, u32[]{:S(2)}, u32[]{:S(2)}) collective-permute-start(f32[64,64]{1,0:T(8,128)S(1)} %get-tuple-element.12.gram_ref), channel_id=1, source_target_pairs={{0,1},{1,0},{2,3},{3,2},{4,5},{5,4},{6,7},{7,6},{8,9},{9,8},{10,11... | collective-permute-start | bytes 49160 | tf_op jit(solution)/shard_map/ppermute | solution.py:406
  78.0 1.8 %collective-permute-start.6 = (bf16[8,64,384]{2,1,0:T(8,128)(2,1)S(1)}, bf16[8,64,384]{2,1,0:T(8,128)(2,1)S(1)}, u32[]{:S(2)}, u32[]{:S(2)}) collective-permute-start(bf16[8,64,384]{2,1,0:T(8,128)(2,1)S(1)} %all_to_all.21.own_ref), channel_id=1, source_target_pairs={{0,1},{1,0},{2,3},{3,2},{4,5},{5,4},{6,7},{7,6},{8,9},{9,8},{10,11... | collective-permute-start | bytes 1179656 | tf_op jit(solution)/shard_map/ppermute | solution.py:408

commit v3 on v2

--- a/solution.py
+++ b/solution.py
@@ -104,9 +104,8 @@
     return jnp.concatenate([jnp.where(lane < RANK, x, turned), jnp.where(lane < RANK, turned, x)], axis=0)
 
 
-def mixed_probes_kernel(half_ref, mixing_hbm, probes_ref, out_ref, mixing_ref, tiles_ref, sems):
+def mixed_probes_kernel(start, mixing_hbm, probes_ref, out_ref, mixing_ref, tiles_ref, sems):
     part = out_ref.shape[0]
-    start = half_ref[0] * part
     first = pltpu.make_async_copy(mixing_hbm, mixing_ref, sems.at[part])
     copies = [pltpu.make_async_copy(probes_ref.at[start + i], tiles_ref.at[i], sems.at[i]) for i in range(part)]
     for copy in [first] + copies:
@@ -119,13 +118,12 @@
         out_ref[i] = folded(weighted(tiles_ref[i], weights))
 
 
-def mixed_probes(half, mixing, probes):
-    count, rows, width = probes.shape
-    part = count // 2
-    return pl.pallas_call(
-        mixed_probes_kernel,
+def mixed_probes(start, part, mixing, probes):
+    _, rows, width = probes.shape
+    return pl.pallas_call(
+        functools.partial(mixed_probes_kernel, start),
         out_shape=pltpu.VMEM((part, rows // 2, LANES), f32),
-        in_specs=[SMEM, HBM, HBM],
+        in_specs=[HBM, HBM],
         out_specs=VMEM,
         scratch_shapes=[
             pltpu.VMEM(mixing.shape, f32),
@@ -139,26 +137,58 @@
         ),
         compiler_params=LIMIT,
         name="mixed_probes",
-    )(half, mixing, probes)
+    )(mixing, probes)
+
+
+def load_kernel(*refs):
+    count = len(refs) // 2
+    sems = refs[-1]
+    copies = [
+        pltpu.make_async_copy(refs[k], refs[count + k], sems.at[k]) for k in range(count)
+    ]
+    for copy in copies:
+        copy.start()
+    for copy in copies:
+        copy.wait()
+
+
+def load(after, *arrays):
+    def kernel(after_ref, *refs):
+        load_kernel(*refs)
+
+    arrays = [pltpu.with_memory_space_constraint(x, pltpu.HBM) for x in arrays]
+    return pl.pallas_call(
+        kernel,
+        out_shape=tuple(pltpu.VMEM(x.shape, x.dtype) for x in arrays),
+        in_specs=[VMEM] + [HBM] * len(arrays),
+        out_specs=(VMEM,) * len(arrays),
+        scratch_shapes=[pltpu.SemaphoreType.DMA((len(arrays),))],
+        cost_estimate=pl.CostEstimate(
+            flops=0, bytes_accessed=2 * sum(x.size * x.dtype.itemsize for x in arrays), transcendentals=0
+        ),
+        compiler_params=LIMIT,
+        name="load",
+    )(in_vmem(after), *arrays)
 
 
 def sketch_kernel(
-    meta_ref, own_a, own_b, before_a, before_b, after_a, after_b, near_ref, keep_ref, send_ref, pick_ref
+    meta_ref, own_a, own_b, moved_a, moved_b, other_a, other_b, near_ref, keep_ref, send_ref, pick_ref
 ):
     count = near_ref.shape[0]
     part = own_a.shape[0]
     core = meta_ref[2 * count]
+    sources = (
+        (own_a, 2), (own_b, 3), (moved_a, 4 * core), (moved_b, 4 * core + 1),
+        (other_a, 4 - 4 * core), (other_b, 5 - 4 * core),
+    )
 
     def pick(i):
         column = jnp.clip(meta_ref[i], 0, 6 * part - 1)
-        group = column // part
-        place = column % part
-        for s, sides in enumerate(((before_a, before_b), (own_a, own_b), (after_a, after_b))):
-            for h, side in enumerate(sides):
-
-                @pl.when(group == 2 * s + (core if h == 0 else 1 - core))
-                def _():
-                    pick_ref[i] = side[place]
+        for source, group in sources:
+
+            @pl.when(column // part == group)
+            def _():
+                pick_ref[i] = source[column % part]
 
     for i in range(count):
         pick(i)
@@ -237,38 +267,31 @@
     )(core, in_vmem(mixed), in_vmem(gram), in_vmem(other))
 
 
-def spread_kernel(meta_ref, own_ref, other_ref, out_ref, basis_ref, upper_ref, work_ref):
+def upper_half(block, width):
+    half = RANK // 2
+    left = block[:, width : width + RANK]
+    return left[:half] + left[half:] + block[:half, width + RANK :]
+
+
+def spread_kernel(far_ref, own_ref, out_ref, work_ref):
     count = own_ref.shape[0]
     groups = out_ref.shape[0] // count
     blocks = RANK // groups
     width = own_ref.shape[2] - LANES
-    half = RANK // 2
+    wide = width // LANES
     tiles = work_ref.shape[0]
-    first = meta_ref[count] == 0
     total = jnp.zeros((RANK, RANK), f32)
     for r in range(count):
-        mine, others = own_ref[r].astype(f32), other_ref[r].astype(f32)
-        sides = (jnp.where(first, mine, others), jnp.where(first, others, mine))
-        uppers = []
-        for h, side in enumerate(sides):
-            for t in range(width // LANES):
-                strip = side[:, t * LANES : (t + 1) * LANES]
-                place = 2 * t + h
-                basis_ref[r, :, place * LANES : (place + 1) * LANES] = strip.astype(bf16)
-                for q in range(blocks):
-                    work_ref[2 * q * width // LANES + place, pl.ds(r, groups, stride=count), :] = strip[
-                        q * groups : (q + 1) * groups
-                    ]
-            uppers.append(
-                side[:half, width : width + RANK]
-                + side[half:, width : width + RANK]
-                + side[:half, width + RANK :]
-            )
-        upper = jnp.concatenate(uppers, axis=0)
-        upper_ref[r] = upper
+        block = own_ref[r].astype(f32)
+        for q in range(blocks):
+            for t in range(wide):
+                work_ref[q * wide + t, pl.ds(r, groups, stride=count), :] = block[
+                    q * groups : (q + 1) * groups, t * LANES : (t + 1) * LANES
+                ]
+        upper = upper_half(block, width)
         total = total + dot(upper, upper, TN, highest)
         work_ref[tiles - 2, pl.ds(r, groups, stride=count), :] = jnp.full(
-            (groups, LANES), meta_ref[r].astype(f32), f32
+            (groups, LANES), far_ref[r].astype(f32), f32
         )
     work_ref[tiles - 1] = jnp.zeros((groups * count, LANES), f32)
     for p in range(2):
@@ -282,56 +305,88 @@
         out_ref[:, t * LANES : (t + 1) * LANES] = work_ref[t].astype(bf16)
 
 
-def spread(meta, own, other, groups):
+def spread(far, own, groups):
     count, _, width = own.shape
-    rows = 2 * (width - LANES)
-    total = RANK // groups * rows + 2 * LANES
+    total = RANK // groups * (width - LANES) + 2 * LANES
     return pl.pallas_call(
         spread_kernel,
-        out_shape=(
-            pltpu.VMEM((groups * count, total), bf16),
-            pltpu.VMEM((count, RANK, rows), bf16),
-            pltpu.VMEM((count, RANK, RANK), f32),
-        ),
-        in_specs=[SMEM, VMEM, VMEM],
-        out_specs=(VMEM, VMEM, VMEM),
+        out_shape=pltpu.VMEM((groups * count, total), bf16),
+        in_specs=[SMEM, VMEM],
+        out_specs=VMEM,
         scratch_shapes=[pltpu.VMEM((total // LANES, groups * count, LANES), f32)],
         compiler_params=LIMIT,
         name="spread",
-    )(meta, in_vmem(own), in_vmem(other))
-
-
-def choose_kernel(count, in_ref, out_ref):
-    clusters, total = in_ref.shape
+    )(far, in_vmem(own))
+
+
+def choose_kernel(count, core_ref, own_ref, other_ref, out_ref):
+    clusters, total = own_ref.shape
     body = total - 2 * LANES
-    wanted = in_ref[:, body : body + LANES].astype(f32)
+    first = core_ref[0] == 0
+    wanted = own_ref[:, body : body + LANES].astype(f32)
     column = lax.broadcasted_iota(jnp.int32, (clusters, clusters), 1).astype(f32)
     select = (wanted == column).astype(bf16)
-    out_ref[:, :body] = dot(select, in_ref[:, :body], NN).astype(bf16)
+    own = dot(select, own_ref[:, :body], NN)
+    other = dot(select, other_ref[:, :body], NN)
+    for t in range(body // LANES):
+        mine, others = own[:, t * LANES : (t + 1) * LANES], other[:, t * LANES : (t + 1) * LANES]
+        out_ref[:, 2 * t * LANES : (2 * t + 1) * LANES] = jnp.where(first, mine, others).astype(bf16)
+        out_ref[:, (2 * t + 1) * LANES : (2 * t + 2) * LANES] = jnp.where(first, others, mine).astype(bf16)
     row = lax.broadcasted_iota(jnp.int32, (count, clusters), 0)
     column = lax.broadcasted_iota(jnp.int32, (count, clusters), 1) % count
     gather = (((column == row) | (column == row + 2) | (column == row + 4)) & (row < 2)).astype(bf16)
-    sums = dot(gather, in_ref[:, body + LANES :], NN)[:2]
+    sums = (dot(gather, own_ref[:, body + LANES :], NN) + dot(gather, other_ref[:, body + LANES :], NN))[:2]
     block = jnp.concatenate([piece.astype(f32) for piece in pieces(sums)] + [jnp.zeros((count - 6, LANES), f32)], axis=0)
-    out_ref[:, body:] = jnp.concatenate([block] * (clusters // count), axis=0).astype(bf16)
-
-
-def choose(received, count):
-    rows, total = received.shape
+    out_ref[:, 2 * body :] = jnp.concatenate([block] * (clusters // count), axis=0).astype(bf16)
+
+
+def choose(core, own, other, count):
+    rows, total = own.shape
     return pl.pallas_call(
         functools.partial(choose_kernel, count),
-        out_shape=pltpu.VMEM((rows, total - LANES), bf16),
-        in_specs=[VMEM],
+        out_shape=pltpu.VMEM((rows, 2 * (total - 2 * LANES) + LANES), bf16),
+        in_specs=[SMEM, VMEM, VMEM],
         out_specs=VMEM,
         compiler_params=LIMIT,
         name="choose",
-    )(in_vmem(received))
-
-
-def couple_kernel(
-    scale, basis_ref, upper_ref, received_ref, far_ref, coupling_ref, root_ref, work_ref
-):
-    count = upper_ref.shape[0]
+    )(core, in_vmem(own), in_vmem(other))
+
+
+def project_kernel(core_ref, own_ref, other_ref, far_ref, out_ref, upper_ref):
+    count = own_ref.shape[0]
+    first = core_ref[0] == 0
+    half = own_ref.shape[2] - LANES
+    for i in range(count):
+        mine, others = own_ref[i].astype(f32), other_ref[i].astype(f32)
+        sides = (jnp.where(first, mine, others), jnp.where(first, others, mine))
+        basis = [side[:, t : t + LANES] for t in range(0, half, LANES) for side in sides]
+        image = dot(jnp.concatenate(basis, axis=1).astype(bf16), far_ref[i, 0], NN)
+        out_ref[i] = jnp.concatenate(pieces(image), axis=0)
+        upper_ref[i] = jnp.concatenate([upper_half(side, half) for side in sides], axis=0)
+
+
+def project(core, own, other, far_tiles):
+    count, _, rows, width = far_tiles.shape
+    return pl.pallas_call(
+        project_kernel,
+        out_shape=(
+            pltpu.VMEM((count, 3 * RANK, width), bf16),
+            pltpu.VMEM((count, RANK, RANK), f32),
+        ),
+        in_specs=[SMEM] + [VMEM] * 3,
+        out_specs=(VMEM, VMEM),
+        cost_estimate=pl.CostEstimate(
+            flops=2 * count * rows * width * RANK,
+            bytes_accessed=count * rows * width * 4,
+            transcendentals=0,
+        ),
+        compiler_params=LIMIT,
+        name="project",
+    )(core, *[in_vmem(x) for x in (own, other, far_tiles)])
+
+
+def couple_kernel(scale, image_ref, upper_ref, received_ref, coupling_ref, root_ref, work_ref):
+    count = image_ref.shape[0]
     rows, total = received_ref.shape
     groups = rows // count
     blocks = RANK // groups
@@ -351,28 +406,26 @@
             )
             for q in range(blocks)
         ]
-        far = jnp.concatenate(far, axis=0).astype(bf16)
-        image = dot(far_ref[i, 0], far, NT)
-        terms = dot(basis_ref[i], jnp.concatenate(pieces(image), axis=1), NN)
-        coupling_ref[i, 0] = terms[:, :RANK] + terms[:, RANK : 2 * RANK] + terms[:, 2 * RANK :]
-    for r in range(count):
-        root_ref[r] = dot(upper_ref[r], inverse, NT, highest) * scale
-
-
-def couple(basis, upper, received, far_tiles, scale):
-    count = far_tiles.shape[0]
+        terms = dot(image_ref[i], jnp.concatenate(far, axis=0).astype(bf16), NT)
+        coupling_ref[i, 0] = terms[:RANK] + terms[RANK : 2 * RANK] + terms[2 * RANK :]
+    for i in range(count):
+        root_ref[i] = dot(upper_ref[i], inverse, NT, highest) * scale
+
+
+def couple(image, upper, received, scale):
+    count = image.shape[0]
     return pl.pallas_call(
         functools.partial(couple_kernel, scale),
         out_shape=(
             jax.ShapeDtypeStruct((count, 1, RANK, RANK), f32),
             jax.ShapeDtypeStruct((count, RANK, RANK), f32),
         ),
-        in_specs=[VMEM] * 4,
+        in_specs=[VMEM] * 3,
         out_specs=(VMEM, VMEM),
         scratch_shapes=[pltpu.VMEM((received.shape[1] // LANES, received.shape[0], LANES), f32)],
         compiler_params=LIMIT,
         name="couple",
-    )(in_vmem(basis), in_vmem(upper), in_vmem(received), in_vmem(far_tiles))
+    )(*[in_vmem(x) for x in (image, upper, received)])
 
 
 def shards(near_tiles, near_cols, near_count, probes, mixing, far_tiles, far_cols):
@@ -382,36 +435,41 @@
     leaf_pos = lax.axis_index("leaf")
     blk_pos = lax.axis_index("blk")
     core = blk_pos % 2
-    up = [(i, i + 1) for i in range(subtrees - 1)]
-    down = [(j, i) for i, j in up]
     pair = [(i, i ^ 1) for i in range(members)]
     lanes = [list(range(c, members, 2)) for c in range(2)]
-
-    core_vec = core.reshape(1).astype(jnp.int32)
+    shift = [
+        (g * members + b, (g + step) * members + b)
+        for g in range(subtrees)
+        for b in range(members)
+        for step in [1 - 2 * (b % 2)]
+        if 0 <= g + step < subtrees
+    ]
+
+    core = core.reshape(1).astype(jnp.int32)
     live = (blk_pos < near_count).astype(jnp.int32)
-    near_meta = jnp.concatenate([near_cols[:, 0] - (leaf_pos * count - REACH), live, core_vec])
-    far_meta = jnp.concatenate([far_cols[:, 0], core_vec])
+    near_meta = jnp.concatenate([near_cols[:, 0] - (leaf_pos * count - REACH), live, core])
 
     mixing, probes = (pltpu.with_memory_space_constraint(x, pltpu.HBM) for x in (mixing.T, probes))
-    own_a = mixed_probes(core_vec, mixing, probes)
-    before_a = lax.ppermute(own_a, "leaf", up)
-    after_a = lax.ppermute(own_a, "leaf", down)
-    own_b = mixed_probes(1 - core_vec, mixing, probes)
-    before_b = lax.ppermute(before_a, "blk", pair)
-    after_b = lax.ppermute(after_a, "blk", pair)
-    keep, send = compress(near_meta, (own_a, own_b, before_a, before_b, after_a, after_b), near_tiles)
+    part = count // 2
+    own = [mixed_probes(start, part, mixing, probes) for start in (0, part)]
+    moved = [lax.ppermute(x, ("leaf", "blk"), shift) for x in own]
+    other = [lax.ppermute(x, "blk", pair) for x in moved]
+    (near_tiles,) = load(own[1], near_tiles)
+    keep, send = compress(near_meta, own + moved + other, near_tiles)
     halves = keep + lax.ppermute(send, "blk", pair)
     terms = lax.all_to_all(halves, "blk", 0, 0, tiled=True, axis_index_groups=lanes)
     mixed, gram = gram_of(terms)
-    own = basis_of(core_vec, mixed, gram, lax.ppermute(gram, "blk", pair), count)
+    own = basis_of(core, mixed, gram, lax.ppermute(gram, "blk", pair), count)
     own = lax.all_to_all(own, "blk", 0, 0, tiled=True, axis_index_groups=lanes)
     other = lax.ppermute(own, "blk", pair)
-    payload, basis, upper = spread(far_meta, own, other, subtrees)
+    payload = spread(far_cols[:, 0], own, subtrees)
     slices = lax.all_to_all(payload.reshape(subtrees, count, -1), "leaf", 0, 0, tiled=True)
-    chosen = choose(slices.reshape(payload.shape), count)
+    slices = slices.reshape(payload.shape)
+    image, upper = project(core, own, other, far_tiles)
+    chosen = choose(core, slices, lax.ppermute(slices, "blk", pair), count)
     received = lax.all_to_all(chosen.reshape(subtrees, count, -1), "leaf", 0, 0, tiled=True)
     scale = math.sqrt(subtrees * count * RANK)
-    return couple(basis, upper, received.reshape(chosen.shape), far_tiles, scale)
+    return couple(image, upper, received.reshape(chosen.shape), scale)
 
 
 def solution(mesh):

time: 120 us -> 117 us (0.975)
  blocking collectives: 75 us -> 57.3 us
  starting transfers between devices: 11.5 us -> 18.6 us
  local copies, waits for them, and re-layouts: 0.02 us -> 6.34 us
    all_to_all x1 -> x0, blocking collectives: 13.3 us -> none  [shards(): lax.all_to_all(chosen.reshape(subtrees, count, -1), 'leaf', 0, 0, tiled=T...]
    unnamed x10 -> x12, local copies, waits for them, and re-layouts: 0.02 us -> 6.34 us
    ppermute x5 -> x6, waiting for transfers between devices: 10.6 us -> 4.55 us  [the longest x2 1.42 us: shards(): other = [lax.ppermute(x, 'blk', pair) for x in moved]]
    all_to_all x0 -> x1, waiting for transfers between devices: none -> 5.69 us  [shards(): lax.all_to_all(chosen.reshape(subtrees, count, -1), 'leaf', 0, 0, tiled=T...]
    all_to_all x1, blocking collectives: 19.2 us -> 15 us  [shards(): lax.all_to_all(payload.reshape(subtrees, count, -1), 'leaf', 0, 0, tiled=...]
    all_to_all x0 -> x1, starting transfers between devices: none -> 3.58 us  [shards(): lax.all_to_all(chosen.reshape(subtrees, count, -1), 'leaf', 0, 0, tiled=T...]
    ppermute x5 -> x6, starting transfers between devices: 10.5 us -> 14 us  [the longest x2 7.33 us: shards(): other = [lax.ppermute(x, 'blk', pair) for x in moved]]
    pallas_call x3 -> x5, Pallas kernels: 7.84 us -> 10.6 us  [the longest x2 6.23 us: mixed_probes(): pl.pallas_call(functools.partial(mixed_probes_kernel, start), out_shape=p...]
  transfers between devices with their start and end apart: 7 -> 9, of which waited for: 6 -> 8; matrix products, arithmetic and copies ran while one was open for 0% -> 0% of each run, Pallas kernels for 3% -> 5%
where the time goes in v3:
time: 117 us; the launch traced here: 116 us
  blocking collectives  57.3 us (49%)
  Pallas kernels  19.8 us (17%)
  starting transfers between devices  18.6 us (16%)
  waiting for transfers between devices  13.1 us (11%)
  local copies, waits for them, and re-layouts  6.34 us (5%)
    all_to_all x1, blocking collectives, shards(): lax.all_to_all(halves, 'blk', 0, 0, tiled=True, axis_index_groups=lanes)  24.7 us
    all_to_all x1, blocking collectives, shards(): own = lax.all_to_all(own, 'blk', 0, 0, tiled=True, axis_index_groups=lanes)  17.5 us
    all_to_all x1, blocking collectives, shards(): lax.all_to_all(payload.reshape(subtrees, count, -1), 'leaf', 0, 0, tiled=...  15 us
    ppermute x2, starting transfers between devices, shards(): other = [lax.ppermute(x, 'blk', pair) for x in moved]  7.33 us
    unnamed x12, local copies, waits for them, and re-layouts  6.34 us
    pallas_call x2, Pallas kernels, mixed_probes(): pl.pallas_call(functools.partial(mixed_probes_kernel, start), out_shape=p...  6.23 us
    all_to_all x1, waiting for transfers between devices, shards(): lax.all_to_all(chosen.reshape(subtrees, count, -1), 'leaf', 0, 0, tiled=T...  5.69 us
    all_to_all x1, starting transfers between devices, shards(): lax.all_to_all(chosen.reshape(subtrees, count, -1), 'leaf', 0, 0, tiled=T...  3.58 us
  transfers between devices with their start and end apart: 9, of which 8 were waited for; matrix products, arithmetic and copies ran while one was open for 0% of the time, Pallas kernels for 5%

profile of v3, /device:TPU:1, one launch (start us, length us, event | category | flops | bytes accessed | tf_op | source)
XLA Modules:
  0.0 116.1 jit_solution(3118862987662600844)
XLA Ops:
  0.6 3.1 %mixed_probes.2.own_a = f32[4,256,128]{2,1,0:T(8,128)S(1)} custom-call(f32[64,512]{1,0:T(8,128)} %bitcast.14, bf16[8,512,512]{2,1,0:T(8,128)(2,1)} %probes_ref.3), custom_call_target="tpu_custom_call" | custom-call | flops 402653184 | bytes 2621440 | tf_op jit(solution)/shard_map/mixed_probes/pallas_call | solution.py:123
  3.8 1.3 %collective-permute-start = (f32[4,256,128]{2,1,0:T(8,128)S(1)}, f32[4,256,128]{2,1,0:T(8,128)S(1)}, u32[]{:S(2)}, u32[]{:S(2)}) collective-permute-start(f32[4,256,128]{2,1,0:T(8,128)S(1)} %mixed_probes.2.own_a), channel_id=1, source_target_pairs={{0,16},{2,18},{4,20},{6,22},{8,24},{10,26},{12,28},{14,30},{16,32}... | collective-permute-start | bytes 1572872 | tf_op jit(solution)/shard_map/ppermute | solution.py:455
  5.1 3.1 %mixed_probes.3.after_ref.own_b = f32[4,256,128]{2,1,0:T(8,128)S(1)} custom-call(f32[64,512]{1,0:T(8,128)} %bitcast.15, bf16[8,512,512]{2,1,0:T(8,128)(2,1)} %probes_ref.3), custom_call_target="tpu_custom_call" | custom-call | flops 402653184 | bytes 2621440 | tf_op jit(solution)/shard_map/mixed_probes/pallas_call | solution.py:123
  8.2 1.3 %collective-permute-start.1 = (f32[4,256,128]{2,1,0:T(8,128)S(1)}, f32[4,256,128]{2,1,0:T(8,128)S(1)}, u32[]{:S(2)}, u32[]{:S(2)}) collective-permute-start(f32[4,256,128]{2,1,0:T(8,128)S(1)} %mixed_probes.3.after_ref.own_b), channel_id=1, source_target_pairs={{0,16},{2,18},{4,20},{6,22},{8,24},{10,26},{12,28},{14,30},{16,32}... | collective-permute-start | bytes 1572872 | tf_op jit(solution)/shard_map/ppermute | solution.py:455
  9.5 0.0 copy-start.4
  9.5 0.0 copy-start.5
  9.5 2.2 %load.1.near_ref = bf16[8,1,512,512]{3,2,1,0:T(8,128)(2,1)S(1)} custom-call(f32[4,256,128]{2,1,0:T(8,128)S(1)} %mixed_probes.3.after_ref.own_b, bf16[8,1,512,512]{3,2,1,0:T(8,128)(2,1)} %refs_0_.1), custom_call_target="tpu_custom_call" | custom-call | bytes 8388608 | tf_op jit(solution)/shard_map/load/pallas_call | solution.py:160
  11.7 0.0 copy-start
  11.7 1.9 %copy-done = bf16[8,1,512,512]{3,2,1,0:T(8,128)(2,1)} copy-done((bf16[8,1,512,512]{3,2,1,0:T(8,128)(2,1)}, bf16[8,1,512,512]{3,2,1,0:T(8,128)(2,1)S(1)}, u32[]{:S(2)}) %copy-start) | copy-done | bytes 4194328
  13.7 0.7 collective-permute-done.moved_a
  14.3 5.3 %collective-permute-start.2 = (f32[4,256,128]{2,1,0:T(8,128)S(1)}, f32[4,256,128]{2,1,0:T(8,128)S(1)}, u32[]{:S(2)}, u32[]{:S(2)}) collective-permute-start(f32[4,256,128]{2,1,0:T(8,128)S(1)} %collective-permute-done.moved_a), channel_id=1, source_target_pairs={{0,1},{1,0},{2,3},{3,2},{4,5},{5,4},{6,7},{7,6},{8,9},{9,8},{10,11... | collective-permute-start | bytes 1572872 | tf_op jit(solution)/shard_map/ppermute | solution.py:456
  19.6 0.4 collective-permute-done.1.moved_b
  20.0 2.1 %collective-permute-start.3 = (f32[4,256,128]{2,1,0:T(8,128)S(1)}, f32[4,256,128]{2,1,0:T(8,128)S(1)}, u32[]{:S(2)}, u32[]{:S(2)}) collective-permute-start(f32[4,256,128]{2,1,0:T(8,128)S(1)} %collective-permute-done.1.moved_b), channel_id=1, source_target_pairs={{0,1},{1,0},{2,3},{3,2},{4,5},{5,4},{6,7},{7,6},{8,9},{9,8},{10,11... | collective-permute-start | bytes 1572872 | tf_op jit(solution)/shard_map/ppermute | solution.py:456
  22.0 0.0 copy-done.4
  22.0 0.0 copy-done.5
  22.1 0.0 copy-start.3
  22.1 0.1 pad_add_fusion.meta_ref
  22.1 0.0 collective-permute-done.2.other_a
  22.2 1.4 %collective-permute-done.3.other_b = f32[4,256,128]{2,1,0:T(8,128)S(1)} collective-permute-done((f32[4,256,128]{2,1,0:T(8,128)S(1)}, f32[4,256,128]{2,1,0:T(8,128)S(1)}, u32[]{:S(2)}, u32[]{:S(2)}) %collective-permute-start.3) | collective-permute-done | bytes 524320 | tf_op jit(solution)/shard_map/ppermute | solution.py:456
  23.6 0.0 copy-start.1
  23.6 2.2 %copy-done.1 = bf16[8,1,512,512]{3,2,1,0:T(8,128)(2,1)S(1)} copy-done((bf16[8,1,512,512]{3,2,1,0:T(8,128)(2,1)S(1)}, bf16[8,1,512,512]{3,2,1,0:T(8,128)(2,1)}, u32[]{:S(2)}) %copy-start.1) | copy-done | bytes 4194328
  25.8 2.6 %compress.1 = (f32[8,128,128]{2,1,0:T(8,128)S(1)}, f32[8,128,128]{2,1,0:T(8,128)S(1)}) custom-call(s32[17]{0:T(128)S(1)} %pad_add_fusion.meta_ref, f32[4,256,128]{2,1,0:T(8,128)S(1)} %mixed_probes.2.own_a, f32[4,256,128]{2,1,0:T(8,128)S(1)} %mixed_probes.3.after_ref.own_b, f32[4,256,128]{2,1,0:T(8,128)S(1)} %collective-permute-done.moved_a, ...), custom_call_target="tpu_custom_call" | custom-call | flops 805306368 | bytes 8388608 | tf_op jit(solution)/shard_map/compress/pallas_call | solution.py:206
  28.4 0.5 collective-permute-start.4
  28.8 1.5 %collective-permute-done.4 = f32[8,128,128]{2,1,0:T(8,128)S(1)} collective-permute-done((f32[8,128,128]{2,1,0:T(8,128)S(1)}, f32[8,128,128]{2,1,0:T(8,128)S(1)}, u32[]{:S(2)}, u32[]{:S(2)}) %collective-permute-start.4) | collective-permute-done | bytes 524320 | tf_op jit(solution)/shard_map/ppermute | solution.py:459
  30.4 0.1 add.9
  30.4 24.7 %all_to_all.20.terms_ref = f32[8,128,128]{2,1,0:T(8,128)S(1)} all-to-all(f32[8,128,128]{2,1,0:T(8,128)S(1)} %add.9), channel_id=1, replica_groups={{0,2,4,6,8,10,12,14},{1,3,5,7,9,11,13,15},{16,18,20,22,24,26,28,30},{17..., dimensions={0} | all-to-all | bytes 1048576 | tf_op jit(solution)/shard_map/all_to_all | solution.py:460
  55.2 0.3 gram.1
  55.5 1.8 %collective-permute-start.5 = (f32[64,64]{1,0:T(8,128)S(1)}, f32[64,64]{1,0:T(8,128)S(1)}, u32[]{:S(2)}, u32[]{:S(2)}) collective-permute-start(f32[64,64]{1,0:T(8,128)S(1)} %get-tuple-element.11.gram_ref), channel_id=1, source_target_pairs={{0,1},{1,0},{2,3},{3,2},{4,5},{5,4},{6,7},{7,6},{8,9},{9,8},{10,11... | collective-permute-start | bytes 49160 | tf_op jit(solution)/shard_map/ppermute | solution.py:462
  57.3 0.9 collective-permute-done.5.other_ref
  58.1 2.0 %basis.1 = bf16[8,64,384]{2,1,0:T(8,128)(2,1)S(1)} custom-call(s32[1]{0:T(128)} %bitcast.core_ref, f32[128,128]{1,0:T(8,128)S(1)} %get-tuple-element.10.mixed_ref, f32[64,64]{1,0:T(8,128)S(1)} %get-tuple-element.11.gram_ref, f32[64,64]{1,0:T(8,128)S(1)} %collective-permute-done.5.other_ref), custom_call_target="tpu_custom_call" | custom-call | tf_op jit(solution)/shard_map/basis/pallas_call | solution.py:260
  60.2 17.5 %all_to_all.21.own_ref = bf16[8,64,384]{2,1,0:T(8,128)(2,1)S(1)} all-to-all(bf16[8,64,384]{2,1,0:T(8,128)(2,1)S(1)} %basis.1), channel_id=1, replica_groups={{0,2,4,6,8,10,12,14},{1,3,5,7,9,11,13,15},{16,18,20,22,24,26,28,30},{17..., dimensions={0} | all-to-all | bytes 786432 | tf_op jit(solution)/shard_map/all_to_all | solution.py:463
  77.7 0.0 copy-done.3
  77.7 1.3 %spread.1 = bf16[128,1280]{1,0:T(8,128)(2,1)S(1)} custom-call(s32[8]{0:T(128)S(1)} %bitcast.13, bf16[8,64,384]{2,1,0:T(8,128)(2,1)S(1)} %all_to_all.21.own_ref), custom_call_target="tpu_custom_call" | custom-call | tf_op jit(solution)/shard_map/spread/pallas_call | solution.py:311
  79.0 15.0 %all_to_all.22 = bf16[16,8,1280]{2,1,0:T(8,128)(2,1)S(1)} all-to-all(bf16[16,8,1280]{2,1,0:T(8,128)(2,1)S(1)} %bitcast.10), channel_id=1, replica_groups=mesh['leaf'=16,'blk'=16] {'leaf'}, dimensions={0} | all-to-all | bytes 655360 | tf_op jit(solution)/shard_map/all_to_all | solution.py:466
  94.0 2.3 %collective-permute-start.7 = (bf16[128,1280]{1,0:T(8,128)(2,1)S(1)}, bf16[128,1280]{1,0:T(8,128)(2,1)S(1)}, u32[]{:S(2)}, u32[]{:S(2)}) collective-permute-start(bf16[128,1280]{1,0:T(8,128)(2,1)S(1)} %bitcast.11), channel_id=1, source_target_pairs={{0,1},{1,0},{2,3},{3,2},{4,5},{5,4},{6,7},{7,6},{8,9},{9,8},{10,11... | collective-permute-start | bytes 983048 | tf_op jit(solution)/shard_map/ppermute | solution.py:469
  96.3 1.3 %collective-permute-done.7.other_ref = bf16[128,1280]{1,0:T(8,128)(2,1)S(1)} collective-permute-done((bf16[128,1280]{1,0:T(8,128)(2,1)S(1)}, bf16[128,1280]{1,0:T(8,128)(2,1)S(1)}, u32[]{:S(2)}, u32[]{:S(2)}) %collective-permute-start.7) | collective-permute-done | bytes 327712 | tf_op jit(solution)/shard_map/ppermute | solution.py:469
  97.6 1.1 choose.1
  98.7 3.6 %all-to-all-start.3 = ((bf16[16,8,2176]{2,1,0:T(8,128)(2,1)}), bf16[16,8,2176]{2,1,0:T(8,128)(2,1)S(1)}, u32[]{:S(2)}, u32[]{:S(2)}) async-start(bf16[16,8,2176]{2,1,0:T(8,128)(2,1)} %bitcast.6), calls=%async_computation.3 | async-start | bytes 1114112 | tf_op jit(solution)/shard_map/all_to_all | solution.py:470
  102.3 0.6 collective-permute-start.6
  102.8 1.3 %collective-permute-done.6.other_ref = bf16[8,64,384]{2,1,0:T(8,128)(2,1)S(1)} collective-permute-done((bf16[8,64,384]{2,1,0:T(8,128)(2,1)S(1)}, bf16[8,64,384]{2,1,0:T(8,128)(2,1)S(1)}, u32[]{:S(2)}, u32[]{:S(2)}) %collective-permute-start.6) | collective-permute-done | bytes 393248 | tf_op jit(solution)/shard_map/ppermute | solution.py:464
  104.2 0.0 copy-start.2
  104.2 2.2 %copy-done.2 = bf16[8,1,512,512]{3,2,1,0:T(8,128)(2,1)S(1)} copy-done((bf16[8,1,512,512]{3,2,1,0:T(8,128)(2,1)S(1)}, bf16[8,1,512,512]{3,2,1,0:T(8,128)(2,1)}, u32[]{:S(2)}) %copy-start.2) | copy-done | bytes 4194328
  106.4 0.9 project.1
  107.2 5.7 %all-to-all-done.3 = bf16[16,8,2176]{2,1,0:T(8,128)(2,1)S(1)} async-done(((bf16[16,8,2176]{2,1,0:T(8,128)(2,1)}), bf16[16,8,2176]{2,1,0:T(8,128)(2,1)S(1)}, u32[]{:S(2)}, u32[]{:S(2)}) %all-to-all-start.3) | async-done | bytes 557088 | tf_op jit(solution)/shard_map/all_to_all | solution.py:470
  112.9 3.1 %couple.1 = (f32[8,1,64,64]{3,2,1,0:T(8,128)}, f32[8,64,64]{2,1,0:T(8,128)}) custom-call(bf16[8,192,512]{2,1,0:T(8,128)(2,1)S(1)} %get-tuple-element.12.image_ref, f32[8,64,64]{2,1,0:T(8,128)S(1)} %get-tuple-element.13.upper_ref, bf16[128,2176]{1,0:T(8,128)(2,1)S(1)} %bitcast.9), custom_call_target="tpu_custom_call" | custom-call | tf_op jit(solution)/shard_map/couple/pallas_call | solution.py:417
  (2 shorter events, 0.0 us)
Async XLA Ops:
  3.8 10.6 %collective-permute-start = (f32[4,256,128]{2,1,0:T(8,128)S(1)}, f32[4,256,128]{2,1,0:T(8,128)S(1)}, u32[]{:S(2)}, u32[]{:S(2)}) collective-permute-start(f32[4,256,128]{2,1,0:T(8,128)S(1)} %mixed_probes.2.own_a), channel_id=1, source_target_pairs={{0,16},{2,18},{4,20},{6,22},{8,24},{10,26},{12,28},{14,30},{16,32}... | collective-permute-start | bytes 1572872 | tf_op jit(solution)/shard_map/ppermute | solution.py:455
  8.2 11.8 %collective-permute-start.1 = (f32[4,256,128]{2,1,0:T(8,128)S(1)}, f32[4,256,128]{2,1,0:T(8,128)S(1)}, u32[]{:S(2)}, u32[]{:S(2)}) collective-permute-start(f32[4,256,128]{2,1,0:T(8,128)S(1)} %mixed_probes.3.after_ref.own_b), channel_id=1, source_target_pairs={{0,16},{2,18},{4,20},{6,22},{8,24},{10,26},{12,28},{14,30},{16,32}... | collective-permute-start | bytes 1572872 | tf_op jit(solution)/shard_map/ppermute | solution.py:455
  9.5 12.5 %copy-start.4 = (s32[8]{0:T(128)S(1)}, s32[8]{0:T(128)}, u32[]{:S(2)}) copy-start(s32[8]{0:T(128)} %param.9) | copy-start | bytes 100
  9.5 12.5 %copy-start.5 = (s32[8,1]{0,1:T(1,128)S(1)}, s32[8,1]{0,1:T(1,128)}, u32[]{:S(2)}) copy-start(s32[8,1]{0,1:T(1,128)} %param.8) | copy-start | bytes 100
  11.7 2.0 %copy-start = (bf16[8,1,512,512]{3,2,1,0:T(8,128)(2,1)}, bf16[8,1,512,512]{3,2,1,0:T(8,128)(2,1)S(1)}, u32[]{:S(2)}) copy-start(bf16[8,1,512,512]{3,2,1,0:T(8,128)(2,1)S(1)} %load.1.near_ref) | copy-start | bytes 12582916
  14.3 7.8 %collective-permute-start.2 = (f32[4,256,128]{2,1,0:T(8,128)S(1)}, f32[4,256,128]{2,1,0:T(8,128)S(1)}, u32[]{:S(2)}, u32[]{:S(2)}) collective-permute-start(f32[4,256,128]{2,1,0:T(8,128)S(1)} %collective-permute-done.moved_a), channel_id=1, source_target_pairs={{0,1},{1,0},{2,3},{3,2},{4,5},{5,4},{6,7},{7,6},{8,9},{9,8},{10,11... | collective-permute-start | bytes 1572872 | tf_op jit(solution)/shard_map/ppermute | solution.py:456
  20.0 3.6 %collective-permute-start.3 = (f32[4,256,128]{2,1,0:T(8,128)S(1)}, f32[4,256,128]{2,1,0:T(8,128)S(1)}, u32[]{:S(2)}, u32[]{:S(2)}) collective-permute-start(f32[4,256,128]{2,1,0:T(8,128)S(1)} %collective-permute-done.1.moved_b), channel_id=1, source_target_pairs={{0,1},{1,0},{2,3},{3,2},{4,5},{5,4},{6,7},{7,6},{8,9},{9,8},{10,11... | collective-permute-start | bytes 1572872 | tf_op jit(solution)/shard_map/ppermute | solution.py:456
  22.1 55.7 %copy-start.3 = (s32[8,1]{0,1:T(1,128)S(1)}, s32[8,1]{0,1:T(1,128)}, u32[]{:S(2)}) copy-start(s32[8,1]{0,1:T(1,128)} %param.13) | copy-start | bytes 100
  23.6 2.2 %copy-start.1 = (bf16[8,1,512,512]{3,2,1,0:T(8,128)(2,1)S(1)}, bf16[8,1,512,512]{3,2,1,0:T(8,128)(2,1)}, u32[]{:S(2)}) copy-start(bf16[8,1,512,512]{3,2,1,0:T(8,128)(2,1)} %copy-done) | copy-start | bytes 12582916
  28.4 2.0 %collective-permute-start.4 = (f32[8,128,128]{2,1,0:T(8,128)S(1)}, f32[8,128,128]{2,1,0:T(8,128)S(1)}, u32[]{:S(2)}, u32[]{:S(2)}) collective-permute-start(f32[8,128,128]{2,1,0:T(8,128)S(1)} %get-tuple-element.9), channel_id=1, source_target_pairs={{0,1},{1,0},{2,3},{3,2},{4,5},{5,4},{6,7},{7,6},{8,9},{9,8},{10,11... | collective-permute-start | bytes 1572872 | tf_op jit(solution)/shard_map/ppermute | solution.py:459
  55.5 2.7 %collective-permute-start.5 = (f32[64,64]{1,0:T(8,128)S(1)}, f32[64,64]{1,0:T(8,128)S(1)}, u32[]{:S(2)}, u32[]{:S(2)}) collective-permute-start(f32[64,64]{1,0:T(8,128)S(1)} %get-tuple-element.11.gram_ref), channel_id=1, source_target_pairs={{0,1},{1,0},{2,3},{3,2},{4,5},{5,4},{6,7},{7,6},{8,9},{9,8},{10,11... | collective-permute-start | bytes 49160 | tf_op jit(solution)/shard_map/ppermute | solution.py:462
  94.0 3.5 %collective-permute-start.7 = (bf16[128,1280]{1,0:T(8,128)(2,1)S(1)}, bf16[128,1280]{1,0:T(8,128)(2,1)S(1)}, u32[]{:S(2)}, u32[]{:S(2)}) collective-permute-start(bf16[128,1280]{1,0:T(8,128)(2,1)S(1)} %bitcast.11), channel_id=1, source_target_pairs={{0,1},{1,0},{2,3},{3,2},{4,5},{5,4},{6,7},{7,6},{8,9},{9,8},{10,11... | collective-permute-start | bytes 983048 | tf_op jit(solution)/shard_map/ppermute | solution.py:469
  98.7 14.2 %all-to-all-start.3 = ((bf16[16,8,2176]{2,1,0:T(8,128)(2,1)}), bf16[16,8,2176]{2,1,0:T(8,128)(2,1)S(1)}, u32[]{:S(2)}, u32[]{:S(2)}) async-start(bf16[16,8,2176]{2,1,0:T(8,128)(2,1)} %bitcast.6), calls=%async_computation.3 | async-start | bytes 1114112 | tf_op jit(solution)/shard_map/all_to_all | solution.py:470
  102.3 1.9 %collective-permute-start.6 = (bf16[8,64,384]{2,1,0:T(8,128)(2,1)S(1)}, bf16[8,64,384]{2,1,0:T(8,128)(2,1)S(1)}, u32[]{:S(2)}, u32[]{:S(2)}) collective-permute-start(bf16[8,64,384]{2,1,0:T(8,128)(2,1)S(1)} %all_to_all.21.own_ref), channel_id=1, source_target_pairs={{0,1},{1,0},{2,3},{3,2},{4,5},{5,4},{6,7},{7,6},{8,9},{9,8},{10,11... | collective-permute-start | bytes 1179656 | tf_op jit(solution)/shard_map/ppermute | solution.py:464
  104.2 2.2 %copy-start.2 = (bf16[8,1,512,512]{3,2,1,0:T(8,128)(2,1)S(1)}, bf16[8,1,512,512]{3,2,1,0:T(8,128)(2,1)}, u32[]{:S(2)}) copy-start(bf16[8,1,512,512]{3,2,1,0:T(8,128)(2,1)} %far_ref.1) | copy-start | bytes 12582916

commit v4 on v3

--- a/solution.py
+++ b/solution.py
@@ -80,28 +80,8 @@
     return upper, work[:, n:]
 
 
-def weights_of(x):
-    high, middle, low = (piece.astype(f32) for piece in pieces(x))
-    lane = lax.broadcasted_iota(jnp.int32, x.shape, 1)
-    return jnp.concatenate([jnp.where(lane < RANK, high, middle), low], axis=1).astype(bf16)
-
-
-def weighted(x, weights):
-    terms = dot(x, weights, NN)
-    first, last = terms[:, :LANES], terms[:, LANES:]
-    return first + pltpu.roll(first, RANK, 1) + last
-
-
-def folded(x):
-    rows = x.shape[0] // 2
-    lane = lax.broadcasted_iota(jnp.int32, (rows, LANES), 1)
-    return jnp.where(lane < RANK, x[:rows], x[rows:])
-
-
-def unfolded(x):
-    lane = lax.broadcasted_iota(jnp.int32, x.shape, 1)
-    turned = pltpu.roll(x, RANK, 1)
-    return jnp.concatenate([jnp.where(lane < RANK, x, turned), jnp.where(lane < RANK, turned, x)], axis=0)
+def doubled(terms):
+    return terms + pltpu.roll(terms, RANK, 1)
 
 
 def mixed_probes_kernel(start, mixing_hbm, probes_ref, out_ref, mixing_ref, tiles_ref, sems):
@@ -111,18 +91,22 @@
     for copy in [first] + copies:
         copy.start()
     first.wait()
-    mixing = mixing_ref[...]
-    weights = weights_of(jnp.concatenate([mixing, mixing], axis=0).T)
+    high, middle, low = pieces(mixing_ref[...])
+    weights = jnp.concatenate([piece.astype(f32) for piece in (high, middle, low, low)], axis=0).T.astype(bf16)
     for i, copy in enumerate(copies):
         copy.wait()
-        out_ref[i] = folded(weighted(tiles_ref[i], weights))
+        terms = dot(tiles_ref[i], weights, NN)
+        mixed = doubled(terms[:, :LANES]) + terms[:, LANES:]
+        lane = lax.broadcasted_iota(jnp.int32, mixed.shape, 1)
+        high = mixed.astype(bf16).astype(f32)
+        out_ref[i] = jnp.where(lane < RANK, high, mixed - high).astype(bf16)
 
 
 def mixed_probes(start, part, mixing, probes):
     _, rows, width = probes.shape
     return pl.pallas_call(
         functools.partial(mixed_probes_kernel, start),
-        out_shape=pltpu.VMEM((part, rows // 2, LANES), f32),
+        out_shape=pltpu.VMEM((part, rows, LANES), bf16),
         in_specs=[HBM, HBM],
         out_specs=VMEM,
         scratch_shapes=[
@@ -140,43 +124,16 @@
     )(mixing, probes)
 
 
-def load_kernel(*refs):
-    count = len(refs) // 2
-    sems = refs[-1]
-    copies = [
-        pltpu.make_async_copy(refs[k], refs[count + k], sems.at[k]) for k in range(count)
-    ]
-    for copy in copies:
-        copy.start()
-    for copy in copies:
-        copy.wait()
-
-
-def load(after, *arrays):
-    def kernel(after_ref, *refs):
-        load_kernel(*refs)
-
-    arrays = [pltpu.with_memory_space_constraint(x, pltpu.HBM) for x in arrays]
-    return pl.pallas_call(
-        kernel,
-        out_shape=tuple(pltpu.VMEM(x.shape, x.dtype) for x in arrays),
-        in_specs=[VMEM] + [HBM] * len(arrays),
-        out_specs=(VMEM,) * len(arrays),
-        scratch_shapes=[pltpu.SemaphoreType.DMA((len(arrays),))],
-        cost_estimate=pl.CostEstimate(
-            flops=0, bytes_accessed=2 * sum(x.size * x.dtype.itemsize for x in arrays), transcendentals=0
-        ),
-        compiler_params=LIMIT,
-        name="load",
-    )(in_vmem(after), *arrays)
-
-
 def sketch_kernel(
-    meta_ref, own_a, own_b, moved_a, moved_b, other_a, other_b, near_ref, keep_ref, send_ref, pick_ref
+    meta_ref, own_a, own_b, moved_a, moved_b, other_a, other_b, near_ref, keep_ref, send_ref,
+    pick_ref, tiles_ref, sems
 ):
     count = near_ref.shape[0]
     part = own_a.shape[0]
     core = meta_ref[2 * count]
+    copies = [pltpu.make_async_copy(near_ref.at[i, 0], tiles_ref.at[i], sems.at[i]) for i in range(count)]
+    for copy in copies:
+        copy.start()
     sources = (
         (own_a, 2), (own_b, 3), (moved_a, 4 * core), (moved_b, 4 * core + 1),
         (other_a, 4 - 4 * core), (other_b, 5 - 4 * core),
@@ -192,31 +149,41 @@
 
     for i in range(count):
         pick(i)
-    for i in range(count):
-        mixed = folded(weighted(near_ref[i, 0], weights_of(unfolded(pick_ref[i]))))
-        mixed = jnp.where(meta_ref[count + i] > 0, mixed, 0.0)
-        rows = mixed.shape[0] // 2
-        keep_ref[i] = jnp.where(core == 0, mixed[:rows], mixed[rows:])
-        send_ref[i] = jnp.where(core == 0, mixed[rows:], mixed[:rows])
+    for i, copy in enumerate(copies):
+        copy.wait()
+        mixed = doubled(dot(tiles_ref[i], pick_ref[i], NN))
+        rows = mixed.shape[0] // 4
+        lane = lax.broadcasted_iota(jnp.int32, (rows, LANES), 1)
+        live = meta_ref[count + i] > 0
+        quarters = [jnp.where(live, mixed[k * rows : (k + 1) * rows], 0.0) for k in range(4)]
+        left = jnp.where(lane < RANK, quarters[0], quarters[2])
+        right = jnp.where(lane < RANK, quarters[1], quarters[3])
+        keep_ref[i] = jnp.where(core == 0, left, right)
+        send_ref[i] = jnp.where(core == 0, right, left)
 
 
 def compress(meta, parts, near_tiles):
     count, _, rows, width = near_tiles.shape
     shape = pltpu.VMEM((count, rows // 4, LANES), f32)
+    near_tiles = pltpu.with_memory_space_constraint(near_tiles, pltpu.HBM)
     return pl.pallas_call(
         sketch_kernel,
         out_shape=(shape, shape),
-        in_specs=[SMEM] + [VMEM] * 7,
+        in_specs=[SMEM] + [VMEM] * 6 + [HBM],
         out_specs=(VMEM, VMEM),
-        scratch_shapes=[pltpu.VMEM((count, rows // 2, LANES), f32)],
+        scratch_shapes=[
+            pltpu.VMEM((count, rows, LANES), bf16),
+            pltpu.VMEM((count, rows, width), bf16),
+            pltpu.SemaphoreType.DMA((count,)),
+        ],
         cost_estimate=pl.CostEstimate(
-            flops=2 * count * rows * width * 3 * RANK,
+            flops=2 * count * rows * width * LANES,
             bytes_accessed=count * rows * (2 * width + 16 * RANK),
             transcendentals=0,
         ),
         compiler_params=LIMIT,
         name="compress",
-    )(meta, *[in_vmem(part) for part in parts], in_vmem(near_tiles))
+    )(meta, *[in_vmem(part) for part in parts], near_tiles)
 
 
 def gram_kernel(terms_ref, mixed_ref, gram_ref):
@@ -454,7 +421,6 @@
     own = [mixed_probes(start, part, mixing, probes) for start in (0, part)]
     moved = [lax.ppermute(x, ("leaf", "blk"), shift) for x in own]
     other = [lax.ppermute(x, "blk", pair) for x in moved]
-    (near_tiles,) = load(own[1], near_tiles)
     keep, send = compress(near_meta, own + moved + other, near_tiles)
     halves = keep + lax.ppermute(send, "blk", pair)
     terms = lax.all_to_all(halves, "blk", 0, 0, tiled=True, axis_index_groups=lanes)

time: 117 us -> 117 us (level)
  waiting for transfers between devices: 13.1 us -> 21.4 us
  local copies, waits for them, and re-layouts: 6.34 us -> 2.2 us
  starting transfers between devices: 18.6 us -> 14.5 us
    ppermute x2, waiting for transfers between devices: 1.01 us -> 9.27 us  [shards(): moved = [lax.ppermute(x, ('leaf', 'blk'), shift) for x in own]]
    unnamed x12 -> x8, local copies, waits for them, and re-layouts: 6.34 us -> 2.2 us
    ppermute x2, starting transfers between devices: 7.33 us -> 3.27 us  [shards(): other = [lax.ppermute(x, 'blk', pair) for x in moved]]
    pallas_call x1, Pallas kernels: 2.59 us -> 5.57 us  [compress(): pl.pallas_call(sketch_kernel, out_shape=(shape, shape), in_specs=[SMEM] +...]
    pallas_call x1 -> x0, Pallas kernels: 2.21 us -> none  [load(): pl.pallas_call(kernel, out_shape=tuple((pltpu.VMEM(x.shape, x.dtype) for...]
  transfers between devices with their start and end apart: 9 -> 9, of which waited for: 8 -> 8; matrix products, arithmetic and copies ran while one was open for 0% -> 0% of each run, Pallas kernels for 5% -> 3%
where the time goes in v4:
time: 117 us
  blocking collectives  57.3 us (49%)
  waiting for transfers between devices  21.4 us (18%)
  Pallas kernels  20.6 us (18%)
  starting transfers between devices  14.5 us (12%)
  local copies, waits for them, and re-layouts  2.2 us (2%)
    all_to_all x1, blocking collectives, shards(): lax.all_to_all(halves, 'blk', 0, 0, tiled=True, axis_index_groups=lanes)  24.7 us
    all_to_all x1, blocking collectives, shards(): own = lax.all_to_all(own, 'blk', 0, 0, tiled=True, axis_index_groups=lanes)  17.5 us
    all_to_all x1, blocking collectives, shards(): lax.all_to_all(payload.reshape(subtrees, count, -1), 'leaf', 0, 0, tiled=...  15 us
    ppermute x2, waiting for transfers between devices, shards(): moved = [lax.ppermute(x, ('leaf', 'blk'), shift) for x in own]  9.27 us
    pallas_call x2, Pallas kernels, mixed_probes(): pl.pallas_call(functools.partial(mixed_probes_kernel, start), out_shape=p...  6.28 us
    all_to_all x1, waiting for transfers between devices, shards(): lax.all_to_all(chosen.reshape(subtrees, count, -1), 'leaf', 0, 0, tiled=T...  5.69 us
    pallas_call x1, Pallas kernels, compress(): pl.pallas_call(sketch_kernel, out_shape=(shape, shape), in_specs=[SMEM] +...  5.57 us
    all_to_all x1, starting transfers between devices, shards(): lax.all_to_all(chosen.reshape(subtrees, count, -1), 'leaf', 0, 0, tiled=T...  3.58 us
  transfers between devices with their start and end apart: 9, of which 8 were waited for; matrix products, arithmetic and copies ran while one was open for 0% of the time, Pallas kernels for 3%

profile of v4, /device:TPU:1, one launch (start us, length us, event | category | flops | bytes accessed | tf_op | source)
XLA Modules:
  0.0 116.9 jit_solution(15453482012581730519)
XLA Ops:
  0.6 0.0 copy-start.2
  0.6 0.0 copy-start.3
  0.6 3.1 %mixed_probes.2.own_a = bf16[4,512,128]{2,1,0:T(8,128)(2,1)S(1)} custom-call(f32[64,512]{1,0:T(8,128)} %bitcast.14, bf16[8,512,512]{2,1,0:T(8,128)(2,1)} %probes_ref.3), custom_call_target="tpu_custom_call" | custom-call | flops 402653184 | bytes 2621440 | tf_op jit(solution)/shard_map/mixed_probes/pallas_call | solution.py:107
  3.8 1.3 %collective-permute-start = (bf16[4,512,128]{2,1,0:T(8,128)(2,1)S(1)}, bf16[4,512,128]{2,1,0:T(8,128)(2,1)S(1)}, u32[]{:S(2)}, u32[]{:S(2)}) collective-permute-start(bf16[4,512,128]{2,1,0:T(8,128)(2,1)S(1)} %mixed_probes.2.own_a), channel_id=1, source_target_pairs={{0,16},{2,18},{4,20},{6,22},{8,24},{10,26},{12,28},{14,30},{16,32}... | collective-permute-start | bytes 1572872 | tf_op jit(solution)/shard_map/ppermute | solution.py:422
  5.1 3.1 %mixed_probes.3.own_b = bf16[4,512,128]{2,1,0:T(8,128)(2,1)S(1)} custom-call(f32[64,512]{1,0:T(8,128)} %bitcast.15, bf16[8,512,512]{2,1,0:T(8,128)(2,1)} %probes_ref.3), custom_call_target="tpu_custom_call" | custom-call | flops 402653184 | bytes 2621440 | tf_op jit(solution)/shard_map/mixed_probes/pallas_call | solution.py:107
  8.2 1.3 %collective-permute-start.1 = (bf16[4,512,128]{2,1,0:T(8,128)(2,1)S(1)}, bf16[4,512,128]{2,1,0:T(8,128)(2,1)S(1)}, u32[]{:S(2)}, u32[]{:S(2)}) collective-permute-start(bf16[4,512,128]{2,1,0:T(8,128)(2,1)S(1)} %mixed_probes.3.own_b), channel_id=1, source_target_pairs={{0,16},{2,18},{4,20},{6,22},{8,24},{10,26},{12,28},{14,30},{16,32}... | collective-permute-start | bytes 1572872 | tf_op jit(solution)/shard_map/ppermute | solution.py:422
  9.6 4.8 %collective-permute-done.moved_a = bf16[4,512,128]{2,1,0:T(8,128)(2,1)S(1)} collective-permute-done((bf16[4,512,128]{2,1,0:T(8,128)(2,1)S(1)}, bf16[4,512,128]{2,1,0:T(8,128)(2,1)S(1)}, u32[]{:S(2)}, u32[]{:S(2)}) %collective-permute-start) | collective-permute-done | bytes 524320 | tf_op jit(solution)/shard_map/ppermute | solution.py:422
  14.4 1.2 %collective-permute-start.2 = (bf16[4,512,128]{2,1,0:T(8,128)(2,1)S(1)}, bf16[4,512,128]{2,1,0:T(8,128)(2,1)S(1)}, u32[]{:S(2)}, u32[]{:S(2)}) collective-permute-start(bf16[4,512,128]{2,1,0:T(8,128)(2,1)S(1)} %collective-permute-done.moved_a), channel_id=1, source_target_pairs={{0,1},{1,0},{2,3},{3,2},{4,5},{5,4},{6,7},{7,6},{8,9},{9,8},{10,11... | collective-permute-start | bytes 1572872 | tf_op jit(solution)/shard_map/ppermute | solution.py:423
  15.6 4.4 %collective-permute-done.1.moved_b = bf16[4,512,128]{2,1,0:T(8,128)(2,1)S(1)} collective-permute-done((bf16[4,512,128]{2,1,0:T(8,128)(2,1)S(1)}, bf16[4,512,128]{2,1,0:T(8,128)(2,1)S(1)}, u32[]{:S(2)}, u32[]{:S(2)}) %collective-permute-start.1) | collective-permute-done | bytes 524320 | tf_op jit(solution)/shard_map/ppermute | solution.py:422
  20.0 2.1 %collective-permute-start.3 = (bf16[4,512,128]{2,1,0:T(8,128)(2,1)S(1)}, bf16[4,512,128]{2,1,0:T(8,128)(2,1)S(1)}, u32[]{:S(2)}, u32[]{:S(2)}) collective-permute-start(bf16[4,512,128]{2,1,0:T(8,128)(2,1)S(1)} %collective-permute-done.1.moved_b), channel_id=1, source_target_pairs={{0,1},{1,0},{2,3},{3,2},{4,5},{5,4},{6,7},{7,6},{8,9},{9,8},{10,11... | collective-permute-start | bytes 1572872 | tf_op jit(solution)/shard_map/ppermute | solution.py:423
  22.1 0.0 copy-done.2
  22.1 0.0 copy-done.3
  22.1 0.1 pad_add_fusion.meta_ref
  22.2 0.0 copy-start.1
  22.2 0.0 collective-permute-done.2.other_a
  22.2 1.4 %collective-permute-done.3.other_b = bf16[4,512,128]{2,1,0:T(8,128)(2,1)S(1)} collective-permute-done((bf16[4,512,128]{2,1,0:T(8,128)(2,1)S(1)}, bf16[4,512,128]{2,1,0:T(8,128)(2,1)S(1)}, u32[]{:S(2)}, u32[]{:S(2)}) %collective-permute-start.3) | collective-permute-done | bytes 524320 | tf_op jit(solution)/shard_map/ppermute | solution.py:423
  23.6 5.6 %compress.1 = (f32[8,128,128]{2,1,0:T(8,128)S(1)}, f32[8,128,128]{2,1,0:T(8,128)S(1)}) custom-call(s32[17]{0:T(128)S(1)} %pad_add_fusion.meta_ref, bf16[4,512,128]{2,1,0:T(8,128)(2,1)S(1)} %mixed_probes.2.own_a, bf16[4,512,128]{2,1,0:T(8,128)(2,1)S(1)} %mixed_probes.3.own_b, bf16[4,512,128]{2,1,0:T(8,128)(2,1)S(1)} %collective-permute-done.moved_a, ...), custom_call_target="tpu_custom_call" | custom-call | flops 536870912 | bytes 8388608 | tf_op jit(solution)/shard_map/compress/pallas_call | solution.py:169
  29.2 0.5 collective-permute-start.4
  29.7 1.5 %collective-permute-done.4 = f32[8,128,128]{2,1,0:T(8,128)S(1)} collective-permute-done((f32[8,128,128]{2,1,0:T(8,128)S(1)}, f32[8,128,128]{2,1,0:T(8,128)S(1)}, u32[]{:S(2)}, u32[]{:S(2)}) %collective-permute-start.4) | collective-permute-done | bytes 524320 | tf_op jit(solution)/shard_map/ppermute | solution.py:425
  31.2 0.1 add.9
  31.3 24.7 %all_to_all.20.terms_ref = f32[8,128,128]{2,1,0:T(8,128)S(1)} all-to-all(f32[8,128,128]{2,1,0:T(8,128)S(1)} %add.9), channel_id=1, replica_groups={{0,2,4,6,8,10,12,14},{1,3,5,7,9,11,13,15},{16,18,20,22,24,26,28,30},{17..., dimensions={0} | all-to-all | bytes 1048576 | tf_op jit(solution)/shard_map/all_to_all | solution.py:426
  56.0 0.3 gram.1
  56.3 1.8 %collective-permute-start.5 = (f32[64,64]{1,0:T(8,128)S(1)}, f32[64,64]{1,0:T(8,128)S(1)}, u32[]{:S(2)}, u32[]{:S(2)}) collective-permute-start(f32[64,64]{1,0:T(8,128)S(1)} %get-tuple-element.11.gram_ref), channel_id=1, source_target_pairs={{0,1},{1,0},{2,3},{3,2},{4,5},{5,4},{6,7},{7,6},{8,9},{9,8},{10,11... | collective-permute-start | bytes 49160 | tf_op jit(solution)/shard_map/ppermute | solution.py:428
  58.1 0.9 collective-permute-done.5.other_ref
  59.0 2.0 %basis.1 = bf16[8,64,384]{2,1,0:T(8,128)(2,1)S(1)} custom-call(s32[1]{0:T(128)} %bitcast.core_ref, f32[128,128]{1,0:T(8,128)S(1)} %get-tuple-element.10.mixed_ref, f32[64,64]{1,0:T(8,128)S(1)} %get-tuple-element.11.gram_ref, f32[64,64]{1,0:T(8,128)S(1)} %collective-permute-done.5.other_ref), custom_call_target="tpu_custom_call" | custom-call | tf_op jit(solution)/shard_map/basis/pallas_call | solution.py:227
  61.0 17.5 %all_to_all.21.own_ref = bf16[8,64,384]{2,1,0:T(8,128)(2,1)S(1)} all-to-all(bf16[8,64,384]{2,1,0:T(8,128)(2,1)S(1)} %basis.1), channel_id=1, replica_groups={{0,2,4,6,8,10,12,14},{1,3,5,7,9,11,13,15},{16,18,20,22,24,26,28,30},{17..., dimensions={0} | all-to-all | bytes 786432 | tf_op jit(solution)/shard_map/all_to_all | solution.py:429
  78.6 0.0 copy-done.1
  78.6 1.3 %spread.1 = bf16[128,1280]{1,0:T(8,128)(2,1)S(1)} custom-call(s32[8]{0:T(128)S(1)} %bitcast.13, bf16[8,64,384]{2,1,0:T(8,128)(2,1)S(1)} %all_to_all.21.own_ref), custom_call_target="tpu_custom_call" | custom-call | tf_op jit(solution)/shard_map/spread/pallas_call | solution.py:278
  79.9 15.0 %all_to_all.22 = bf16[16,8,1280]{2,1,0:T(8,128)(2,1)S(1)} all-to-all(bf16[16,8,1280]{2,1,0:T(8,128)(2,1)S(1)} %bitcast.10), channel_id=1, replica_groups=mesh['leaf'=16,'blk'=16] {'leaf'}, dimensions={0} | all-to-all | bytes 655360 | tf_op jit(solution)/shard_map/all_to_all | solution.py:432
  94.9 2.3 %collective-permute-start.7 = (bf16[128,1280]{1,0:T(8,128)(2,1)S(1)}, bf16[128,1280]{1,0:T(8,128)(2,1)S(1)}, u32[]{:S(2)}, u32[]{:S(2)}) collective-permute-start(bf16[128,1280]{1,0:T(8,128)(2,1)S(1)} %bitcast.11), channel_id=1, source_target_pairs={{0,1},{1,0},{2,3},{3,2},{4,5},{5,4},{6,7},{7,6},{8,9},{9,8},{10,11... | collective-permute-start | bytes 983048 | tf_op jit(solution)/shard_map/ppermute | solution.py:435
  97.2 1.3 %collective-permute-done.7.other_ref = bf16[128,1280]{1,0:T(8,128)(2,1)S(1)} collective-permute-done((bf16[128,1280]{1,0:T(8,128)(2,1)S(1)}, bf16[128,1280]{1,0:T(8,128)(2,1)S(1)}, u32[]{:S(2)}, u32[]{:S(2)}) %collective-permute-start.7) | collective-permute-done | bytes 327712 | tf_op jit(solution)/shard_map/ppermute | solution.py:435
  98.4 1.1 choose.1
  99.6 3.6 %all-to-all-start.3 = ((bf16[16,8,2176]{2,1,0:T(8,128)(2,1)}), bf16[16,8,2176]{2,1,0:T(8,128)(2,1)S(1)}, u32[]{:S(2)}, u32[]{:S(2)}) async-start(bf16[16,8,2176]{2,1,0:T(8,128)(2,1)} %bitcast.6), calls=%async_computation.3 | async-start | bytes 1114112 | tf_op jit(solution)/shard_map/all_to_all | solution.py:436
  103.1 0.6 collective-permute-start.6
  103.7 1.3 %collective-permute-done.6.other_ref = bf16[8,64,384]{2,1,0:T(8,128)(2,1)S(1)} collective-permute-done((bf16[8,64,384]{2,1,0:T(8,128)(2,1)S(1)}, bf16[8,64,384]{2,1,0:T(8,128)(2,1)S(1)}, u32[]{:S(2)}, u32[]{:S(2)}) %collective-permute-start.6) | collective-permute-done | bytes 393248 | tf_op jit(solution)/shard_map/ppermute | solution.py:430
  105.0 0.0 copy-start
  105.0 2.2 %copy-done = bf16[8,1,512,512]{3,2,1,0:T(8,128)(2,1)S(1)} copy-done((bf16[8,1,512,512]{3,2,1,0:T(8,128)(2,1)S(1)}, bf16[8,1,512,512]{3,2,1,0:T(8,128)(2,1)}, u32[]{:S(2)}) %copy-start) | copy-done | bytes 4194328
  107.2 0.9 project.1
  108.1 5.7 %all-to-all-done.3 = bf16[16,8,2176]{2,1,0:T(8,128)(2,1)S(1)} async-done(((bf16[16,8,2176]{2,1,0:T(8,128)(2,1)}), bf16[16,8,2176]{2,1,0:T(8,128)(2,1)S(1)}, u32[]{:S(2)}, u32[]{:S(2)}) %all-to-all-start.3) | async-done | bytes 557088 | tf_op jit(solution)/shard_map/all_to_all | solution.py:436
  113.8 3.1 %couple.1 = (f32[8,1,64,64]{3,2,1,0:T(8,128)}, f32[8,64,64]{2,1,0:T(8,128)}) custom-call(bf16[8,192,512]{2,1,0:T(8,128)(2,1)S(1)} %get-tuple-element.12.image_ref, f32[8,64,64]{2,1,0:T(8,128)S(1)} %get-tuple-element.13.upper_ref, bf16[128,2176]{1,0:T(8,128)(2,1)S(1)} %bitcast.9), custom_call_target="tpu_custom_call" | custom-call | tf_op jit(solution)/shard_map/couple/pallas_call | solution.py:384
  (2 shorter events, 0.0 us)
Async XLA Ops:
  0.6 21.5 %copy-start.2 = (s32[8]{0:T(128)S(1)}, s32[8]{0:T(128)}, u32[]{:S(2)}) copy-start(s32[8]{0:T(128)} %param.9) | copy-start | bytes 100
  0.6 21.5 %copy-start.3 = (s32[8,1]{0,1:T(1,128)S(1)}, s32[8,1]{0,1:T(1,128)}, u32[]{:S(2)}) copy-start(s32[8,1]{0,1:T(1,128)} %param.8) | copy-start | bytes 100
  3.8 10.6 %collective-permute-start = (bf16[4,512,128]{2,1,0:T(8,128)(2,1)S(1)}, bf16[4,512,128]{2,1,0:T(8,128)(2,1)S(1)}, u32[]{:S(2)}, u32[]{:S(2)}) collective-permute-start(bf16[4,512,128]{2,1,0:T(8,128)(2,1)S(1)} %mixed_probes.2.own_a), channel_id=1, source_target_pairs={{0,16},{2,18},{4,20},{6,22},{8,24},{10,26},{12,28},{14,30},{16,32}... | collective-permute-start | bytes 1572872 | tf_op jit(solution)/shard_map/ppermute | solution.py:422
  8.2 11.8 %collective-permute-start.1 = (bf16[4,512,128]{2,1,0:T(8,128)(2,1)S(1)}, bf16[4,512,128]{2,1,0:T(8,128)(2,1)S(1)}, u32[]{:S(2)}, u32[]{:S(2)}) collective-permute-start(bf16[4,512,128]{2,1,0:T(8,128)(2,1)S(1)} %mixed_probes.3.own_b), channel_id=1, source_target_pairs={{0,16},{2,18},{4,20},{6,22},{8,24},{10,26},{12,28},{14,30},{16,32}... | collective-permute-start | bytes 1572872 | tf_op jit(solution)/shard_map/ppermute | solution.py:422
  14.4 7.8 %collective-permute-start.2 = (bf16[4,512,128]{2,1,0:T(8,128)(2,1)S(1)}, bf16[4,512,128]{2,1,0:T(8,128)(2,1)S(1)}, u32[]{:S(2)}, u32[]{:S(2)}) collective-permute-start(bf16[4,512,128]{2,1,0:T(8,128)(2,1)S(1)} %collective-permute-done.moved_a), channel_id=1, source_target_pairs={{0,1},{1,0},{2,3},{3,2},{4,5},{5,4},{6,7},{7,6},{8,9},{9,8},{10,11... | collective-permute-start | bytes 1572872 | tf_op jit(solution)/shard_map/ppermute | solution.py:423
  20.0 3.6 %collective-permute-start.3 = (bf16[4,512,128]{2,1,0:T(8,128)(2,1)S(1)}, bf16[4,512,128]{2,1,0:T(8,128)(2,1)S(1)}, u32[]{:S(2)}, u32[]{:S(2)}) collective-permute-start(bf16[4,512,128]{2,1,0:T(8,128)(2,1)S(1)} %collective-permute-done.1.moved_b), channel_id=1, source_target_pairs={{0,1},{1,0},{2,3},{3,2},{4,5},{5,4},{6,7},{7,6},{8,9},{9,8},{10,11... | collective-permute-start | bytes 1572872 | tf_op jit(solution)/shard_map/ppermute | solution.py:423
  22.2 56.4 %copy-start.1 = (s32[8,1]{0,1:T(1,128)S(1)}, s32[8,1]{0,1:T(1,128)}, u32[]{:S(2)}) copy-start(s32[8,1]{0,1:T(1,128)} %param.13) | copy-start | bytes 100
  29.2 2.0 %collective-permute-start.4 = (f32[8,128,128]{2,1,0:T(8,128)S(1)}, f32[8,128,128]{2,1,0:T(8,128)S(1)}, u32[]{:S(2)}, u32[]{:S(2)}) collective-permute-start(f32[8,128,128]{2,1,0:T(8,128)S(1)} %get-tuple-element.9), channel_id=1, source_target_pairs={{0,1},{1,0},{2,3},{3,2},{4,5},{5,4},{6,7},{7,6},{8,9},{9,8},{10,11... | collective-permute-start | bytes 1572872 | tf_op jit(solution)/shard_map/ppermute | solution.py:425
  56.3 2.7 %collective-permute-start.5 = (f32[64,64]{1,0:T(8,128)S(1)}, f32[64,64]{1,0:T(8,128)S(1)}, u32[]{:S(2)}, u32[]{:S(2)}) collective-permute-start(f32[64,64]{1,0:T(8,128)S(1)} %get-tuple-element.11.gram_ref), channel_id=1, source_target_pairs={{0,1},{1,0},{2,3},{3,2},{4,5},{5,4},{6,7},{7,6},{8,9},{9,8},{10,11... | collective-permute-start | bytes 49160 | tf_op jit(solution)/shard_map/ppermute | solution.py:428
  94.9 3.5 %collective-permute-start.7 = (bf16[128,1280]{1,0:T(8,128)(2,1)S(1)}, bf16[128,1280]{1,0:T(8,128)(2,1)S(1)}, u32[]{:S(2)}, u32[]{:S(2)}) collective-permute-start(bf16[128,1280]{1,0:T(8,128)(2,1)S(1)} %bitcast.11), channel_id=1, source_target_pairs={{0,1},{1,0},{2,3},{3,2},{4,5},{5,4},{6,7},{7,6},{8,9},{9,8},{10,11... | collective-permute-start | bytes 983048 | tf_op jit(solution)/shard_map/ppermute | solution.py:435
  99.6 14.2 %all-to-all-start.3 = ((bf16[16,8,2176]{2,1,0:T(8,128)(2,1)}), bf16[16,8,2176]{2,1,0:T(8,128)(2,1)S(1)}, u32[]{:S(2)}, u32[]{:S(2)}) async-start(bf16[16,8,2176]{2,1,0:T(8,128)(2,1)} %bitcast.6), calls=%async_computation.3 | async-start | bytes 1114112 | tf_op jit(solution)/shard_map/all_to_all | solution.py:436
  103.1 1.9 %collective-permute-start.6 = (bf16[8,64,384]{2,1,0:T(8,128)(2,1)S(1)}, bf16[8,64,384]{2,1,0:T(8,128)(2,1)S(1)}, u32[]{:S(2)}, u32[]{:S(2)}) collective-permute-start(bf16[8,64,384]{2,1,0:T(8,128)(2,1)S(1)} %all_to_all.21.own_ref), channel_id=1, source_target_pairs={{0,1},{1,0},{2,3},{3,2},{4,5},{5,4},{6,7},{7,6},{8,9},{9,8},{10,11... | collective-permute-start | bytes 1179656 | tf_op jit(solution)/shard_map/ppermute | solution.py:430
  105.0 2.2 %copy-start = (bf16[8,1,512,512]{3,2,1,0:T(8,128)(2,1)S(1)}, bf16[8,1,512,512]{3,2,1,0:T(8,128)(2,1)}, u32[]{:S(2)}) copy-start(bf16[8,1,512,512]{3,2,1,0:T(8,128)(2,1)} %far_ref.1) | copy-start | bytes 12582916

commit v5 on v3

--- a/solution.py
+++ b/solution.py
@@ -44,7 +44,7 @@
     return pltpu.with_memory_space_constraint(x, pltpu.VMEM)
 
 
-def factor(gram):
+def factor(gram, beside=lambda k: None):
     n = gram.shape[0]
     row = lax.broadcasted_iota(jnp.int32, (n, n), 0)
     col = lax.broadcasted_iota(jnp.int32, (n, n), 1)
@@ -74,6 +74,8 @@
                 for i in range(j + 1, PANEL):
                     columns[t - k][i] = columns[t - k][i] - multiplier * entries[i]
                 panels[t] = panels[t] - multiplier * pivot_row
+            if j == PANEL // 2:
+                beside(k)
         panels[k] = panels[k] * jnp.sqrt(scales)
     work = jnp.concatenate(panels, axis=0)
     upper = jnp.where(col >= row, work[:, :n], 0.0)
@@ -108,13 +110,15 @@
     part = out_ref.shape[0]
     first = pltpu.make_async_copy(mixing_hbm, mixing_ref, sems.at[part])
     copies = [pltpu.make_async_copy(probes_ref.at[start + i], tiles_ref.at[i], sems.at[i]) for i in range(part)]
-    for copy in [first] + copies:
+    for copy in [first] + copies[:2]:
         copy.start()
     first.wait()
     mixing = mixing_ref[...]
     weights = weights_of(jnp.concatenate([mixing, mixing], axis=0).T)
     for i, copy in enumerate(copies):
         copy.wait()
+        if i + 2 < part:
+            copies[i + 2].start()
         out_ref[i] = folded(weighted(tiles_ref[i], weights))
 
 
@@ -140,41 +144,43 @@
     )(mixing, probes)
 
 
-def load_kernel(*refs):
-    count = len(refs) // 2
-    sems = refs[-1]
-    copies = [
-        pltpu.make_async_copy(refs[k], refs[count + k], sems.at[k]) for k in range(count)
-    ]
+def load_kernel(meta_ref, after_ref, tiles_ref, out_ref, sems):
+    del meta_ref, after_ref
+    part = out_ref.shape[0]
+    copies = [pltpu.make_async_copy(tiles_ref.at[i, 0], out_ref.at[i], sems.at[i]) for i in range(part)]
     for copy in copies:
         copy.start()
     for copy in copies:
         copy.wait()
 
 
-def load(after, *arrays):
-    def kernel(after_ref, *refs):
-        load_kernel(*refs)
-
-    arrays = [pltpu.with_memory_space_constraint(x, pltpu.HBM) for x in arrays]
-    return pl.pallas_call(
-        kernel,
-        out_shape=tuple(pltpu.VMEM(x.shape, x.dtype) for x in arrays),
-        in_specs=[VMEM] + [HBM] * len(arrays),
-        out_specs=(VMEM,) * len(arrays),
-        scratch_shapes=[pltpu.SemaphoreType.DMA((len(arrays),))],
+def load(meta, after, tiles, part):
+    _, _, rows, width = tiles.shape
+    return pl.pallas_call(
+        load_kernel,
+        out_shape=pltpu.VMEM((part, rows, width), tiles.dtype),
+        in_specs=[SMEM, VMEM, HBM],
+        out_specs=VMEM,
+        scratch_shapes=[pltpu.SemaphoreType.DMA((part,))],
         cost_estimate=pl.CostEstimate(
-            flops=0, bytes_accessed=2 * sum(x.size * x.dtype.itemsize for x in arrays), transcendentals=0
+            flops=0, bytes_accessed=4 * part * rows * width, transcendentals=0
         ),
         compiler_params=LIMIT,
         name="load",
-    )(in_vmem(after), *arrays)
+    )(meta, in_vmem(after), tiles)
 
 
 def sketch_kernel(
-    meta_ref, own_a, own_b, moved_a, moved_b, other_a, other_b, near_ref, keep_ref, send_ref, pick_ref
+    meta_ref, own_a, own_b, moved_a, moved_b, other_a, other_b, ready_ref, near_ref, keep_ref, send_ref,
+    pick_ref, tiles_ref, sems
 ):
     count = near_ref.shape[0]
+    ready = ready_ref.shape[0]
+    copies = [
+        pltpu.make_async_copy(near_ref.at[ready + i, 0], tiles_ref.at[i], sems.at[i]) for i in range(count - ready)
+    ]
+    for copy in copies:
+        copy.start()
     part = own_a.shape[0]
     core = meta_ref[2 * count]
     sources = (
@@ -193,22 +199,29 @@
     for i in range(count):
         pick(i)
     for i in range(count):
-        mixed = folded(weighted(near_ref[i, 0], weights_of(unfolded(pick_ref[i]))))
+        if i >= ready:
+            copies[i - ready].wait()
+        tile = ready_ref[i] if i < ready else tiles_ref[i - ready]
+        mixed = folded(weighted(tile, weights_of(unfolded(pick_ref[i]))))
         mixed = jnp.where(meta_ref[count + i] > 0, mixed, 0.0)
         rows = mixed.shape[0] // 2
         keep_ref[i] = jnp.where(core == 0, mixed[:rows], mixed[rows:])
         send_ref[i] = jnp.where(core == 0, mixed[rows:], mixed[:rows])
 
 
-def compress(meta, parts, near_tiles):
+def compress(meta, parts, ready, near_tiles):
     count, _, rows, width = near_tiles.shape
     shape = pltpu.VMEM((count, rows // 4, LANES), f32)
     return pl.pallas_call(
         sketch_kernel,
         out_shape=(shape, shape),
-        in_specs=[SMEM] + [VMEM] * 7,
+        in_specs=[SMEM] + [VMEM] * 7 + [HBM],
         out_specs=(VMEM, VMEM),
-        scratch_shapes=[pltpu.VMEM((count, rows // 2, LANES), f32)],
+        scratch_shapes=[
+            pltpu.VMEM((count, rows // 2, LANES), f32),
+            pltpu.VMEM((count - ready.shape[0], rows, width), bf16),
+            pltpu.SemaphoreType.DMA((count - ready.shape[0],)),
+        ],
         cost_estimate=pl.CostEstimate(
             flops=2 * count * rows * width * 3 * RANK,
             bytes_accessed=count * rows * (2 * width + 16 * RANK),
@@ -216,7 +229,7 @@
         ),
         compiler_params=LIMIT,
         name="compress",
-    )(meta, *[in_vmem(part) for part in parts], in_vmem(near_tiles))
+    )(meta, *[in_vmem(x) for x in (*parts, ready)], near_tiles)
 
 
 def gram_kernel(terms_ref, mixed_ref, gram_ref):
@@ -398,8 +411,8 @@
     for p in range(2):
         packed = sum(work_ref[tiles - 1, pl.ds(2 * k + p, groups, stride=count), :] for k in range(3))
         parts += [packed[:, :RANK], packed[:, RANK:]]
-    _, inverse = factor(jnp.concatenate(parts, axis=0))
-    for i in range(count):
+
+    def coupling(i):
         far = [
             jnp.concatenate(
                 [work_ref[q * wide + t, pl.ds(i, groups, stride=count), :] for t in range(wide)], axis=1
@@ -408,6 +421,8 @@
         ]
         terms = dot(image_ref[i], jnp.concatenate(far, axis=0).astype(bf16), NT)
         coupling_ref[i, 0] = terms[:RANK] + terms[RANK : 2 * RANK] + terms[2 * RANK :]
+
+    _, inverse = factor(jnp.concatenate(parts, axis=0), coupling)
     for i in range(count):
         root_ref[i] = dot(upper_ref[i], inverse, NT, highest) * scale
 
@@ -454,8 +469,9 @@
     own = [mixed_probes(start, part, mixing, probes) for start in (0, part)]
     moved = [lax.ppermute(x, ("leaf", "blk"), shift) for x in own]
     other = [lax.ppermute(x, "blk", pair) for x in moved]
-    (near_tiles,) = load(own[1], near_tiles)
-    keep, send = compress(near_meta, own + moved + other, near_tiles)
+    near_tiles = pltpu.with_memory_space_constraint(near_tiles, pltpu.HBM)
+    ready = load(near_meta, own[1], near_tiles, part)
+    keep, send = compress(near_meta, own + moved + other, ready, near_tiles)
     halves = keep + lax.ppermute(send, "blk", pair)
     terms = lax.all_to_all(halves, "blk", 0, 0, tiled=True, axis_index_groups=lanes)
     mixed, gram = gram_of(terms)

time: 117 us -> 117 us (level)
  waiting for transfers between devices: 13.1 us -> 20.2 us
  starting transfers between devices: 18.6 us -> 13.2 us
  local copies, waits for them, and re-layouts: 6.34 us -> 2.2 us
  Pallas kernels: 19.8 us -> 21.7 us
    ppermute x2, waiting for transfers between devices: 1.01 us -> 9.11 us  [shards(): moved = [lax.ppermute(x, ('leaf', 'blk'), shift) for x in own]]
    unnamed x12 -> x8, local copies, waits for them, and re-layouts: 6.34 us -> 2.2 us
    ppermute x2, starting transfers between devices: 7.33 us -> 3.44 us  [shards(): other = [lax.ppermute(x, 'blk', pair) for x in moved]]
    pallas_call x1, Pallas kernels: 2.59 us -> 4.42 us  [compress(): pl.pallas_call(sketch_kernel, out_shape=(shape, shape), in_specs=[SMEM] +...]
    ppermute x2, waiting for transfers between devices: 1.42 us -> 0.01 us  [shards(): other = [lax.ppermute(x, 'blk', pair) for x in moved]]
  transfers between devices with their start and end apart: 9 -> 9, of which waited for: 8 -> 7; matrix products, arithmetic and copies ran while one was open for 0% -> 0% of each run, Pallas kernels for 5% -> 5%
where the time goes in v5:
time: 117 us
  blocking collectives  58.4 us (50%)
  Pallas kernels  21.7 us (19%)
  waiting for transfers between devices  20.2 us (17%)
  starting transfers between devices  13.2 us (11%)
  local copies, waits for them, and re-layouts  2.2 us (2%)
    all_to_all x1, blocking collectives, shards(): lax.all_to_all(halves, 'blk', 0, 0, tiled=True, axis_index_groups=lanes)  25.9 us
    all_to_all x1, blocking collectives, shards(): own = lax.all_to_all(own, 'blk', 0, 0, tiled=True, axis_index_groups=lanes)  17.5 us
    all_to_all x1, blocking collectives, shards(): lax.all_to_all(payload.reshape(subtrees, count, -1), 'leaf', 0, 0, tiled=...  15 us
    ppermute x2, waiting for transfers between devices, shards(): moved = [lax.ppermute(x, ('leaf', 'blk'), shift) for x in own]  9.11 us
    pallas_call x2, Pallas kernels, mixed_probes(): pl.pallas_call(functools.partial(mixed_probes_kernel, start), out_shape=p...  6.44 us
    all_to_all x1, waiting for transfers between devices, shards(): lax.all_to_all(chosen.reshape(subtrees, count, -1), 'leaf', 0, 0, tiled=T...  5.69 us
    pallas_call x1, Pallas kernels, compress(): pl.pallas_call(sketch_kernel, out_shape=(shape, shape), in_specs=[SMEM] +...  4.42 us
    all_to_all x1, starting transfers between devices, shards(): lax.all_to_all(chosen.reshape(subtrees, count, -1), 'leaf', 0, 0, tiled=T...  3.58 us
  transfers between devices with their start and end apart: 9, of which 7 were waited for; matrix products, arithmetic and copies ran while one was open for 0% of the time, Pallas kernels for 5%

profile of v5, /device:TPU:1, one launch (start us, length us, event | category | flops | bytes accessed | tf_op | source)
XLA Modules:
  0.0 116.7 jit_solution(10113762011096602944)
XLA Ops:
  0.6 0.0 copy-start.2
  0.6 0.0 copy-start.3
  0.6 3.2 %mixed_probes.2.own_a = f32[4,256,128]{2,1,0:T(8,128)S(1)} custom-call(f32[64,512]{1,0:T(8,128)} %bitcast.14, bf16[8,512,512]{2,1,0:T(8,128)(2,1)} %probes_ref.3), custom_call_target="tpu_custom_call" | custom-call | flops 402653184 | bytes 2621440 | tf_op jit(solution)/shard_map/mixed_probes/pallas_call | solution.py:127
  3.9 1.3 %collective-permute-start = (f32[4,256,128]{2,1,0:T(8,128)S(1)}, f32[4,256,128]{2,1,0:T(8,128)S(1)}, u32[]{:S(2)}, u32[]{:S(2)}) collective-permute-start(f32[4,256,128]{2,1,0:T(8,128)S(1)} %mixed_probes.2.own_a), channel_id=1, source_target_pairs={{0,16},{2,18},{4,20},{6,22},{8,24},{10,26},{12,28},{14,30},{16,32}... | collective-permute-start | bytes 1572872 | tf_op jit(solution)/shard_map/ppermute | solution.py:470
  5.2 3.2 %mixed_probes.3.after_ref.own_b = f32[4,256,128]{2,1,0:T(8,128)S(1)} custom-call(f32[64,512]{1,0:T(8,128)} %bitcast.15, bf16[8,512,512]{2,1,0:T(8,128)(2,1)} %probes_ref.3), custom_call_target="tpu_custom_call" | custom-call | flops 402653184 | bytes 2621440 | tf_op jit(solution)/shard_map/mixed_probes/pallas_call | solution.py:127
  8.4 1.3 %collective-permute-start.1 = (f32[4,256,128]{2,1,0:T(8,128)S(1)}, f32[4,256,128]{2,1,0:T(8,128)S(1)}, u32[]{:S(2)}, u32[]{:S(2)}) collective-permute-start(f32[4,256,128]{2,1,0:T(8,128)S(1)} %mixed_probes.3.after_ref.own_b), channel_id=1, source_target_pairs={{0,16},{2,18},{4,20},{6,22},{8,24},{10,26},{12,28},{14,30},{16,32}... | collective-permute-start | bytes 1572872 | tf_op jit(solution)/shard_map/ppermute | solution.py:470
  9.7 4.7 %collective-permute-done.moved_a = f32[4,256,128]{2,1,0:T(8,128)S(1)} collective-permute-done((f32[4,256,128]{2,1,0:T(8,128)S(1)}, f32[4,256,128]{2,1,0:T(8,128)S(1)}, u32[]{:S(2)}, u32[]{:S(2)}) %collective-permute-start) | collective-permute-done | bytes 524320 | tf_op jit(solution)/shard_map/ppermute | solution.py:470
  14.5 1.3 %collective-permute-start.2 = (f32[4,256,128]{2,1,0:T(8,128)S(1)}, f32[4,256,128]{2,1,0:T(8,128)S(1)}, u32[]{:S(2)}, u32[]{:S(2)}) collective-permute-start(f32[4,256,128]{2,1,0:T(8,128)S(1)} %collective-permute-done.moved_a), channel_id=1, source_target_pairs={{0,1},{1,0},{2,3},{3,2},{4,5},{5,4},{6,7},{7,6},{8,9},{9,8},{10,11... | collective-permute-start | bytes 1572872 | tf_op jit(solution)/shard_map/ppermute | solution.py:471
  15.7 4.4 %collective-permute-done.1.moved_b = f32[4,256,128]{2,1,0:T(8,128)S(1)} collective-permute-done((f32[4,256,128]{2,1,0:T(8,128)S(1)}, f32[4,256,128]{2,1,0:T(8,128)S(1)}, u32[]{:S(2)}, u32[]{:S(2)}) %collective-permute-start.1) | collective-permute-done | bytes 524320 | tf_op jit(solution)/shard_map/ppermute | solution.py:470
  20.1 2.2 %collective-permute-start.3 = (f32[4,256,128]{2,1,0:T(8,128)S(1)}, f32[4,256,128]{2,1,0:T(8,128)S(1)}, u32[]{:S(2)}, u32[]{:S(2)}) collective-permute-start(f32[4,256,128]{2,1,0:T(8,128)S(1)} %collective-permute-done.1.moved_b), channel_id=1, source_target_pairs={{0,1},{1,0},{2,3},{3,2},{4,5},{5,4},{6,7},{7,6},{8,9},{9,8},{10,11... | collective-permute-start | bytes 1572872 | tf_op jit(solution)/shard_map/ppermute | solution.py:471
  22.3 0.0 copy-done.2
  22.3 0.0 copy-done.3
  22.3 0.1 pad_add_fusion.meta_ref
  22.4 2.1 %load.1.ready_ref = bf16[4,512,512]{2,1,0:T(8,128)(2,1)S(1)} custom-call(s32[17]{0:T(128)S(1)} %pad_add_fusion.meta_ref, f32[4,256,128]{2,1,0:T(8,128)S(1)} %mixed_probes.3.after_ref.own_b, bf16[8,1,512,512]{3,2,1,0:T(8,128)(2,1)} %near_ref.1), custom_call_target="tpu_custom_call" | custom-call | bytes 4194304 | tf_op jit(solution)/shard_map/load/pallas_call | solution.py:159
  24.5 0.0 collective-permute-done.2.other_a
  24.5 0.0 collective-permute-done.3.other_b
  24.5 4.4 %compress.1 = (f32[8,128,128]{2,1,0:T(8,128)S(1)}, f32[8,128,128]{2,1,0:T(8,128)S(1)}) custom-call(s32[17]{0:T(128)S(1)} %pad_add_fusion.meta_ref, f32[4,256,128]{2,1,0:T(8,128)S(1)} %mixed_probes.2.own_a, f32[4,256,128]{2,1,0:T(8,128)S(1)} %mixed_probes.3.after_ref.own_b, f32[4,256,128]{2,1,0:T(8,128)S(1)} %collective-permute-done.moved_a, ...), custom_call_target="tpu_custom_call" | custom-call | flops 805306368 | bytes 8388608 | tf_op jit(solution)/shard_map/compress/pallas_call | solution.py:215
  28.9 0.0 copy-start.1
  28.9 0.1 collective-permute-start.4
  29.0 1.9 %collective-permute-done.4 = f32[8,128,128]{2,1,0:T(8,128)S(1)} collective-permute-done((f32[8,128,128]{2,1,0:T(8,128)S(1)}, f32[8,128,128]{2,1,0:T(8,128)S(1)}, u32[]{:S(2)}, u32[]{:S(2)}) %collective-permute-start.4) | collective-permute-done | bytes 524320 | tf_op jit(solution)/shard_map/ppermute | solution.py:475
  30.9 0.1 add.9
  31.0 25.9 %all_to_all.20.terms_ref = f32[8,128,128]{2,1,0:T(8,128)S(1)} all-to-all(f32[8,128,128]{2,1,0:T(8,128)S(1)} %add.9), channel_id=1, replica_groups={{0,2,4,6,8,10,12,14},{1,3,5,7,9,11,13,15},{16,18,20,22,24,26,28,30},{17..., dimensions={0} | all-to-all | bytes 1048576 | tf_op jit(solution)/shard_map/all_to_all | solution.py:476
  56.9 0.3 gram.1
  57.2 0.7 collective-permute-start.5
  57.8 0.9 collective-permute-done.5.other_ref
  58.7 2.0 %basis.1 = bf16[8,64,384]{2,1,0:T(8,128)(2,1)S(1)} custom-call(s32[1]{0:T(128)} %bitcast.core_ref, f32[128,128]{1,0:T(8,128)S(1)} %get-tuple-element.10.mixed_ref, f32[64,64]{1,0:T(8,128)S(1)} %get-tuple-element.11.gram_ref, f32[64,64]{1,0:T(8,128)S(1)} %collective-permute-done.5.other_ref), custom_call_target="tpu_custom_call" | custom-call | tf_op jit(solution)/shard_map/basis/pallas_call | solution.py:273
  60.8 17.5 %all_to_all.21.own_ref = bf16[8,64,384]{2,1,0:T(8,128)(2,1)S(1)} all-to-all(bf16[8,64,384]{2,1,0:T(8,128)(2,1)S(1)} %basis.1), channel_id=1, replica_groups={{0,2,4,6,8,10,12,14},{1,3,5,7,9,11,13,15},{16,18,20,22,24,26,28,30},{17..., dimensions={0} | all-to-all | bytes 786432 | tf_op jit(solution)/shard_map/all_to_all | solution.py:479
  78.3 0.0 copy-done.1
  78.3 1.3 %spread.1 = bf16[128,1280]{1,0:T(8,128)(2,1)S(1)} custom-call(s32[8]{0:T(128)S(1)} %bitcast.13, bf16[8,64,384]{2,1,0:T(8,128)(2,1)S(1)} %all_to_all.21.own_ref), custom_call_target="tpu_custom_call" | custom-call | tf_op jit(solution)/shard_map/spread/pallas_call | solution.py:324
  79.6 15.0 %all_to_all.22 = bf16[16,8,1280]{2,1,0:T(8,128)(2,1)S(1)} all-to-all(bf16[16,8,1280]{2,1,0:T(8,128)(2,1)S(1)} %bitcast.10), channel_id=1, replica_groups=mesh['leaf'=16,'blk'=16] {'leaf'}, dimensions={0} | all-to-all | bytes 655360 | tf_op jit(solution)/shard_map/all_to_all | solution.py:482
  94.6 2.3 %collective-permute-start.7 = (bf16[128,1280]{1,0:T(8,128)(2,1)S(1)}, bf16[128,1280]{1,0:T(8,128)(2,1)S(1)}, u32[]{:S(2)}, u32[]{:S(2)}) collective-permute-start(bf16[128,1280]{1,0:T(8,128)(2,1)S(1)} %bitcast.11), channel_id=1, source_target_pairs={{0,1},{1,0},{2,3},{3,2},{4,5},{5,4},{6,7},{7,6},{8,9},{9,8},{10,11... | collective-permute-start | bytes 983048 | tf_op jit(solution)/shard_map/ppermute | solution.py:485
  96.9 1.3 %collective-permute-done.7.other_ref = bf16[128,1280]{1,0:T(8,128)(2,1)S(1)} collective-permute-done((bf16[128,1280]{1,0:T(8,128)(2,1)S(1)}, bf16[128,1280]{1,0:T(8,128)(2,1)S(1)}, u32[]{:S(2)}, u32[]{:S(2)}) %collective-permute-start.7) | collective-permute-done | bytes 327712 | tf_op jit(solution)/shard_map/ppermute | solution.py:485
  98.1 1.1 choose.1
  99.3 3.6 %all-to-all-start.3 = ((bf16[16,8,2176]{2,1,0:T(8,128)(2,1)}), bf16[16,8,2176]{2,1,0:T(8,128)(2,1)S(1)}, u32[]{:S(2)}, u32[]{:S(2)}) async-start(bf16[16,8,2176]{2,1,0:T(8,128)(2,1)} %bitcast.6), calls=%async_computation.3 | async-start | bytes 1114112 | tf_op jit(solution)/shard_map/all_to_all | solution.py:486
  102.9 0.6 collective-permute-start.6
  103.4 1.3 %collective-permute-done.6.other_ref = bf16[8,64,384]{2,1,0:T(8,128)(2,1)S(1)} collective-permute-done((bf16[8,64,384]{2,1,0:T(8,128)(2,1)S(1)}, bf16[8,64,384]{2,1,0:T(8,128)(2,1)S(1)}, u32[]{:S(2)}, u32[]{:S(2)}) %collective-permute-start.6) | collective-permute-done | bytes 393248 | tf_op jit(solution)/shard_map/ppermute | solution.py:480
  104.8 0.0 copy-start
  104.8 2.2 %copy-done = bf16[8,1,512,512]{3,2,1,0:T(8,128)(2,1)S(1)} copy-done((bf16[8,1,512,512]{3,2,1,0:T(8,128)(2,1)S(1)}, bf16[8,1,512,512]{3,2,1,0:T(8,128)(2,1)}, u32[]{:S(2)}) %copy-start) | copy-done | bytes 4194328
  106.9 0.9 project.1
  107.8 5.7 %all-to-all-done.3 = bf16[16,8,2176]{2,1,0:T(8,128)(2,1)S(1)} async-done(((bf16[16,8,2176]{2,1,0:T(8,128)(2,1)}), bf16[16,8,2176]{2,1,0:T(8,128)(2,1)S(1)}, u32[]{:S(2)}, u32[]{:S(2)}) %all-to-all-start.3) | async-done | bytes 557088 | tf_op jit(solution)/shard_map/all_to_all | solution.py:486
  113.5 3.1 %couple.1 = (f32[8,1,64,64]{3,2,1,0:T(8,128)}, f32[8,64,64]{2,1,0:T(8,128)}) custom-call(bf16[8,192,512]{2,1,0:T(8,128)(2,1)S(1)} %get-tuple-element.12.image_ref, f32[8,64,64]{2,1,0:T(8,128)S(1)} %get-tuple-element.13.upper_ref, bf16[128,2176]{1,0:T(8,128)(2,1)S(1)} %bitcast.9), custom_call_target="tpu_custom_call" | custom-call | tf_op jit(solution)/shard_map/couple/pallas_call | solution.py:432
  (2 shorter events, 0.0 us)
Async XLA Ops:
  0.6 21.6 %copy-start.2 = (s32[8]{0:T(128)S(1)}, s32[8]{0:T(128)}, u32[]{:S(2)}) copy-start(s32[8]{0:T(128)} %param.9) | copy-start | bytes 100
  0.6 21.6 %copy-start.3 = (s32[8,1]{0,1:T(1,128)S(1)}, s32[8,1]{0,1:T(1,128)}, u32[]{:S(2)}) copy-start(s32[8,1]{0,1:T(1,128)} %param.8) | copy-start | bytes 100
  3.9 10.6 %collective-permute-start = (f32[4,256,128]{2,1,0:T(8,128)S(1)}, f32[4,256,128]{2,1,0:T(8,128)S(1)}, u32[]{:S(2)}, u32[]{:S(2)}) collective-permute-start(f32[4,256,128]{2,1,0:T(8,128)S(1)} %mixed_probes.2.own_a), channel_id=1, source_target_pairs={{0,16},{2,18},{4,20},{6,22},{8,24},{10,26},{12,28},{14,30},{16,32}... | collective-permute-start | bytes 1572872 | tf_op jit(solution)/shard_map/ppermute | solution.py:470
  8.4 11.7 %collective-permute-start.1 = (f32[4,256,128]{2,1,0:T(8,128)S(1)}, f32[4,256,128]{2,1,0:T(8,128)S(1)}, u32[]{:S(2)}, u32[]{:S(2)}) collective-permute-start(f32[4,256,128]{2,1,0:T(8,128)S(1)} %mixed_probes.3.after_ref.own_b), channel_id=1, source_target_pairs={{0,16},{2,18},{4,20},{6,22},{8,24},{10,26},{12,28},{14,30},{16,32}... | collective-permute-start | bytes 1572872 | tf_op jit(solution)/shard_map/ppermute | solution.py:470
  14.5 10.0 %collective-permute-start.2 = (f32[4,256,128]{2,1,0:T(8,128)S(1)}, f32[4,256,128]{2,1,0:T(8,128)S(1)}, u32[]{:S(2)}, u32[]{:S(2)}) collective-permute-start(f32[4,256,128]{2,1,0:T(8,128)S(1)} %collective-permute-done.moved_a), channel_id=1, source_target_pairs={{0,1},{1,0},{2,3},{3,2},{4,5},{5,4},{6,7},{7,6},{8,9},{9,8},{10,11... | collective-permute-start | bytes 1572872 | tf_op jit(solution)/shard_map/ppermute | solution.py:471
  20.1 4.4 %collective-permute-start.3 = (f32[4,256,128]{2,1,0:T(8,128)S(1)}, f32[4,256,128]{2,1,0:T(8,128)S(1)}, u32[]{:S(2)}, u32[]{:S(2)}) collective-permute-start(f32[4,256,128]{2,1,0:T(8,128)S(1)} %collective-permute-done.1.moved_b), channel_id=1, source_target_pairs={{0,1},{1,0},{2,3},{3,2},{4,5},{5,4},{6,7},{7,6},{8,9},{9,8},{10,11... | collective-permute-start | bytes 1572872 | tf_op jit(solution)/shard_map/ppermute | solution.py:471
  28.9 49.4 %copy-start.1 = (s32[8,1]{0,1:T(1,128)S(1)}, s32[8,1]{0,1:T(1,128)}, u32[]{:S(2)}) copy-start(s32[8,1]{0,1:T(1,128)} %param.13) | copy-start | bytes 100
  28.9 2.0 %collective-permute-start.4 = (f32[8,128,128]{2,1,0:T(8,128)S(1)}, f32[8,128,128]{2,1,0:T(8,128)S(1)}, u32[]{:S(2)}, u32[]{:S(2)}) collective-permute-start(f32[8,128,128]{2,1,0:T(8,128)S(1)} %get-tuple-element.9), channel_id=1, source_target_pairs={{0,1},{1,0},{2,3},{3,2},{4,5},{5,4},{6,7},{7,6},{8,9},{9,8},{10,11... | collective-permute-start | bytes 1572872 | tf_op jit(solution)/shard_map/ppermute | solution.py:475
  57.2 1.5 %collective-permute-start.5 = (f32[64,64]{1,0:T(8,128)S(1)}, f32[64,64]{1,0:T(8,128)S(1)}, u32[]{:S(2)}, u32[]{:S(2)}) collective-permute-start(f32[64,64]{1,0:T(8,128)S(1)} %get-tuple-element.11.gram_ref), channel_id=1, source_target_pairs={{0,1},{1,0},{2,3},{3,2},{4,5},{5,4},{6,7},{7,6},{8,9},{9,8},{10,11... | collective-permute-start | bytes 49160 | tf_op jit(solution)/shard_map/ppermute | solution.py:478
  94.6 3.5 %collective-permute-start.7 = (bf16[128,1280]{1,0:T(8,128)(2,1)S(1)}, bf16[128,1280]{1,0:T(8,128)(2,1)S(1)}, u32[]{:S(2)}, u32[]{:S(2)}) collective-permute-start(bf16[128,1280]{1,0:T(8,128)(2,1)S(1)} %bitcast.11), channel_id=1, source_target_pairs={{0,1},{1,0},{2,3},{3,2},{4,5},{5,4},{6,7},{7,6},{8,9},{9,8},{10,11... | collective-permute-start | bytes 983048 | tf_op jit(solution)/shard_map/ppermute | solution.py:485
  99.3 14.2 %all-to-all-start.3 = ((bf16[16,8,2176]{2,1,0:T(8,128)(2,1)}), bf16[16,8,2176]{2,1,0:T(8,128)(2,1)S(1)}, u32[]{:S(2)}, u32[]{:S(2)}) async-start(bf16[16,8,2176]{2,1,0:T(8,128)(2,1)} %bitcast.6), calls=%async_computation.3 | async-start | bytes 1114112 | tf_op jit(solution)/shard_map/all_to_all | solution.py:486
  102.9 1.9 %collective-permute-start.6 = (bf16[8,64,384]{2,1,0:T(8,128)(2,1)S(1)}, bf16[8,64,384]{2,1,0:T(8,128)(2,1)S(1)}, u32[]{:S(2)}, u32[]{:S(2)}) collective-permute-start(bf16[8,64,384]{2,1,0:T(8,128)(2,1)S(1)} %all_to_all.21.own_ref), channel_id=1, source_target_pairs={{0,1},{1,0},{2,3},{3,2},{4,5},{5,4},{6,7},{7,6},{8,9},{9,8},{10,11... | collective-permute-start | bytes 1179656 | tf_op jit(solution)/shard_map/ppermute | solution.py:480
  104.8 2.2 %copy-start = (bf16[8,1,512,512]{3,2,1,0:T(8,128)(2,1)S(1)}, bf16[8,1,512,512]{3,2,1,0:T(8,128)(2,1)}, u32[]{:S(2)}) copy-start(bf16[8,1,512,512]{3,2,1,0:T(8,128)(2,1)} %far_ref.1) | copy-start | bytes 12582916

commit v6 on v5

--- a/solution.py
+++ b/solution.py
@@ -106,19 +106,34 @@
     return jnp.concatenate([jnp.where(lane < RANK, x, turned), jnp.where(lane < RANK, turned, x)], axis=0)
 
 
+class Tile:
+    def __init__(self, source, target, sem, strips=8):
+        self.whole = pltpu.make_async_copy(source, target, sem)
+        rows = source.shape[0] // strips
+        self.strips = [
+            pltpu.make_async_copy(source.at[pl.ds(k * rows, rows)], target.at[pl.ds(k * rows, rows)], sem)
+            for k in range(strips)
+        ]
+
+    def start(self):
+        for strip in self.strips:
+            strip.start()
+
+    def wait(self):
+        self.whole.wait()
+
+
 def mixed_probes_kernel(start, mixing_hbm, probes_ref, out_ref, mixing_ref, tiles_ref, sems):
     part = out_ref.shape[0]
-    first = pltpu.make_async_copy(mixing_hbm, mixing_ref, sems.at[part])
-    copies = [pltpu.make_async_copy(probes_ref.at[start + i], tiles_ref.at[i], sems.at[i]) for i in range(part)]
-    for copy in [first] + copies[:2]:
+    first = Tile(mixing_hbm, mixing_ref, sems.at[part])
+    copies = [Tile(probes_ref.at[start + i], tiles_ref.at[i], sems.at[i]) for i in range(part)]
+    for copy in [first] + copies:
         copy.start()
     first.wait()
     mixing = mixing_ref[...]
     weights = weights_of(jnp.concatenate([mixing, mixing], axis=0).T)
     for i, copy in enumerate(copies):
         copy.wait()
-        if i + 2 < part:
-            copies[i + 2].start()
         out_ref[i] = folded(weighted(tiles_ref[i], weights))
 
 
@@ -147,7 +162,7 @@
 def load_kernel(meta_ref, after_ref, tiles_ref, out_ref, sems):
     del meta_ref, after_ref
     part = out_ref.shape[0]
-    copies = [pltpu.make_async_copy(tiles_ref.at[i, 0], out_ref.at[i], sems.at[i]) for i in range(part)]
+    copies = [Tile(tiles_ref.at[i, 0], out_ref.at[i], sems.at[i]) for i in range(part)]
     for copy in copies:
         copy.start()
     for copy in copies:
@@ -176,9 +191,7 @@
 ):
     count = near_ref.shape[0]
     ready = ready_ref.shape[0]
-    copies = [
-        pltpu.make_async_copy(near_ref.at[ready + i, 0], tiles_ref.at[i], sems.at[i]) for i in range(count - ready)
-    ]
+    copies = [Tile(near_ref.at[ready + i, 0], tiles_ref.at[i], sems.at[i]) for i in range(count - ready)]
     for copy in copies:
         copy.start()
     part = own_a.shape[0]

time: 117 us -> 117 us (level)
  no operation moved by 1% of the time
where the time goes in v6:
time: 117 us
  blocking collectives  58.4 us (50%)
  Pallas kernels  21.7 us (19%)
  waiting for transfers between devices  20.2 us (17%)
  starting transfers between devices  13.1 us (11%)
  local copies, waits for them, and re-layouts  2.2 us (2%)
    all_to_all x1, blocking collectives, shards(): lax.all_to_all(halves, 'blk', 0, 0, tiled=True, axis_index_groups=lanes)  25.9 us
    all_to_all x1, blocking collectives, shards(): own = lax.all_to_all(own, 'blk', 0, 0, tiled=True, axis_index_groups=lanes)  17.5 us
    all_to_all x1, blocking collectives, shards(): lax.all_to_all(payload.reshape(subtrees, count, -1), 'leaf', 0, 0, tiled=...  15 us
    ppermute x2, waiting for transfers between devices, shards(): moved = [lax.ppermute(x, ('leaf', 'blk'), shift) for x in own]  9.18 us
    pallas_call x2, Pallas kernels, mixed_probes(): pl.pallas_call(functools.partial(mixed_probes_kernel, start), out_shape=p...  6.38 us
    all_to_all x1, waiting for transfers between devices, shards(): lax.all_to_all(chosen.reshape(subtrees, count, -1), 'leaf', 0, 0, tiled=T...  5.69 us
    pallas_call x1, Pallas kernels, compress(): pl.pallas_call(sketch_kernel, out_shape=(shape, shape), in_specs=[SMEM] +...  4.45 us
    all_to_all x1, starting transfers between devices, shards(): lax.all_to_all(chosen.reshape(subtrees, count, -1), 'leaf', 0, 0, tiled=T...  3.58 us
  transfers between devices with their start and end apart: 9, of which 7 were waited for; matrix products, arithmetic and copies ran while one was open for 0% of the time, Pallas kernels for 5%

profile of v6, /device:TPU:1, one launch (start us, length us, event | category | flops | bytes accessed | tf_op | source)
XLA Modules:
  0.0 116.7 jit_solution(16034936132935310901)
XLA Ops:
  0.6 0.0 copy-start.2
  0.6 0.0 copy-start.3
  0.6 3.2 %mixed_probes.2.own_a = f32[4,256,128]{2,1,0:T(8,128)S(1)} custom-call(f32[64,512]{1,0:T(8,128)} %bitcast.14, bf16[8,512,512]{2,1,0:T(8,128)(2,1)} %probes_ref.3), custom_call_target="tpu_custom_call" | custom-call | flops 402653184 | bytes 2621440 | tf_op jit(solution)/shard_map/mixed_probes/pallas_call | solution.py:142
  3.8 1.3 %collective-permute-start = (f32[4,256,128]{2,1,0:T(8,128)S(1)}, f32[4,256,128]{2,1,0:T(8,128)S(1)}, u32[]{:S(2)}, u32[]{:S(2)}) collective-permute-start(f32[4,256,128]{2,1,0:T(8,128)S(1)} %mixed_probes.2.own_a), channel_id=1, source_target_pairs={{0,16},{2,18},{4,20},{6,22},{8,24},{10,26},{12,28},{14,30},{16,32}... | collective-permute-start | bytes 1572872 | tf_op jit(solution)/shard_map/ppermute | solution.py:483
  5.1 3.2 %mixed_probes.3.after_ref.own_b = f32[4,256,128]{2,1,0:T(8,128)S(1)} custom-call(f32[64,512]{1,0:T(8,128)} %bitcast.15, bf16[8,512,512]{2,1,0:T(8,128)(2,1)} %probes_ref.3), custom_call_target="tpu_custom_call" | custom-call | flops 402653184 | bytes 2621440 | tf_op jit(solution)/shard_map/mixed_probes/pallas_call | solution.py:142
  8.3 1.3 %collective-permute-start.1 = (f32[4,256,128]{2,1,0:T(8,128)S(1)}, f32[4,256,128]{2,1,0:T(8,128)S(1)}, u32[]{:S(2)}, u32[]{:S(2)}) collective-permute-start(f32[4,256,128]{2,1,0:T(8,128)S(1)} %mixed_probes.3.after_ref.own_b), channel_id=1, source_target_pairs={{0,16},{2,18},{4,20},{6,22},{8,24},{10,26},{12,28},{14,30},{16,32}... | collective-permute-start | bytes 1572872 | tf_op jit(solution)/shard_map/ppermute | solution.py:483
  9.7 4.8 %collective-permute-done.moved_a = f32[4,256,128]{2,1,0:T(8,128)S(1)} collective-permute-done((f32[4,256,128]{2,1,0:T(8,128)S(1)}, f32[4,256,128]{2,1,0:T(8,128)S(1)}, u32[]{:S(2)}, u32[]{:S(2)}) %collective-permute-start) | collective-permute-done | bytes 524320 | tf_op jit(solution)/shard_map/ppermute | solution.py:483
  14.4 1.2 %collective-permute-start.2 = (f32[4,256,128]{2,1,0:T(8,128)S(1)}, f32[4,256,128]{2,1,0:T(8,128)S(1)}, u32[]{:S(2)}, u32[]{:S(2)}) collective-permute-start(f32[4,256,128]{2,1,0:T(8,128)S(1)} %collective-permute-done.moved_a), channel_id=1, source_target_pairs={{0,1},{1,0},{2,3},{3,2},{4,5},{5,4},{6,7},{7,6},{8,9},{9,8},{10,11... | collective-permute-start | bytes 1572872 | tf_op jit(solution)/shard_map/ppermute | solution.py:484
  15.7 4.4 %collective-permute-done.1.moved_b = f32[4,256,128]{2,1,0:T(8,128)S(1)} collective-permute-done((f32[4,256,128]{2,1,0:T(8,128)S(1)}, f32[4,256,128]{2,1,0:T(8,128)S(1)}, u32[]{:S(2)}, u32[]{:S(2)}) %collective-permute-start.1) | collective-permute-done | bytes 524320 | tf_op jit(solution)/shard_map/ppermute | solution.py:483
  20.1 2.1 %collective-permute-start.3 = (f32[4,256,128]{2,1,0:T(8,128)S(1)}, f32[4,256,128]{2,1,0:T(8,128)S(1)}, u32[]{:S(2)}, u32[]{:S(2)}) collective-permute-start(f32[4,256,128]{2,1,0:T(8,128)S(1)} %collective-permute-done.1.moved_b), channel_id=1, source_target_pairs={{0,1},{1,0},{2,3},{3,2},{4,5},{5,4},{6,7},{7,6},{8,9},{9,8},{10,11... | collective-permute-start | bytes 1572872 | tf_op jit(solution)/shard_map/ppermute | solution.py:484
  22.2 0.0 copy-done.2
  22.2 0.0 copy-done.3
  22.2 0.1 pad_add_fusion.meta_ref
  22.3 2.1 %load.1.ready_ref = bf16[4,512,512]{2,1,0:T(8,128)(2,1)S(1)} custom-call(s32[17]{0:T(128)S(1)} %pad_add_fusion.meta_ref, f32[4,256,128]{2,1,0:T(8,128)S(1)} %mixed_probes.3.after_ref.own_b, bf16[8,1,512,512]{3,2,1,0:T(8,128)(2,1)} %near_ref.1), custom_call_target="tpu_custom_call" | custom-call | bytes 4194304 | tf_op jit(solution)/shard_map/load/pallas_call | solution.py:174
  24.4 0.0 collective-permute-done.2.other_a
  24.4 0.0 collective-permute-done.3.other_b
  24.5 4.5 %compress.1 = (f32[8,128,128]{2,1,0:T(8,128)S(1)}, f32[8,128,128]{2,1,0:T(8,128)S(1)}) custom-call(s32[17]{0:T(128)S(1)} %pad_add_fusion.meta_ref, f32[4,256,128]{2,1,0:T(8,128)S(1)} %mixed_probes.2.own_a, f32[4,256,128]{2,1,0:T(8,128)S(1)} %mixed_probes.3.after_ref.own_b, f32[4,256,128]{2,1,0:T(8,128)S(1)} %collective-permute-done.moved_a, ...), custom_call_target="tpu_custom_call" | custom-call | flops 805306368 | bytes 8388608 | tf_op jit(solution)/shard_map/compress/pallas_call | solution.py:228
  28.9 0.0 copy-start.1
  28.9 0.1 collective-permute-start.4
  29.0 1.9 %collective-permute-done.4 = f32[8,128,128]{2,1,0:T(8,128)S(1)} collective-permute-done((f32[8,128,128]{2,1,0:T(8,128)S(1)}, f32[8,128,128]{2,1,0:T(8,128)S(1)}, u32[]{:S(2)}, u32[]{:S(2)}) %collective-permute-start.4) | collective-permute-done | bytes 524320 | tf_op jit(solution)/shard_map/ppermute | solution.py:488
  30.9 0.1 add.9
  31.0 25.9 %all_to_all.20.terms_ref = f32[8,128,128]{2,1,0:T(8,128)S(1)} all-to-all(f32[8,128,128]{2,1,0:T(8,128)S(1)} %add.9), channel_id=1, replica_groups={{0,2,4,6,8,10,12,14},{1,3,5,7,9,11,13,15},{16,18,20,22,24,26,28,30},{17..., dimensions={0} | all-to-all | bytes 1048576 | tf_op jit(solution)/shard_map/all_to_all | solution.py:489
  56.9 0.3 gram.1
  57.2 0.7 collective-permute-start.5
  57.8 0.9 collective-permute-done.5.other_ref
  58.7 2.0 %basis.1 = bf16[8,64,384]{2,1,0:T(8,128)(2,1)S(1)} custom-call(s32[1]{0:T(128)} %bitcast.core_ref, f32[128,128]{1,0:T(8,128)S(1)} %get-tuple-element.10.mixed_ref, f32[64,64]{1,0:T(8,128)S(1)} %get-tuple-element.11.gram_ref, f32[64,64]{1,0:T(8,128)S(1)} %collective-permute-done.5.other_ref), custom_call_target="tpu_custom_call" | custom-call | tf_op jit(solution)/shard_map/basis/pallas_call | solution.py:286
  60.8 17.5 %all_to_all.21.own_ref = bf16[8,64,384]{2,1,0:T(8,128)(2,1)S(1)} all-to-all(bf16[8,64,384]{2,1,0:T(8,128)(2,1)S(1)} %basis.1), channel_id=1, replica_groups={{0,2,4,6,8,10,12,14},{1,3,5,7,9,11,13,15},{16,18,20,22,24,26,28,30},{17..., dimensions={0} | all-to-all | bytes 786432 | tf_op jit(solution)/shard_map/all_to_all | solution.py:492
  78.3 0.0 copy-done.1
  78.3 1.3 %spread.1 = bf16[128,1280]{1,0:T(8,128)(2,1)S(1)} custom-call(s32[8]{0:T(128)S(1)} %bitcast.13, bf16[8,64,384]{2,1,0:T(8,128)(2,1)S(1)} %all_to_all.21.own_ref), custom_call_target="tpu_custom_call" | custom-call | tf_op jit(solution)/shard_map/spread/pallas_call | solution.py:337
  79.6 15.0 %all_to_all.22 = bf16[16,8,1280]{2,1,0:T(8,128)(2,1)S(1)} all-to-all(bf16[16,8,1280]{2,1,0:T(8,128)(2,1)S(1)} %bitcast.10), channel_id=1, replica_groups=mesh['leaf'=16,'blk'=16] {'leaf'}, dimensions={0} | all-to-all | bytes 655360 | tf_op jit(solution)/shard_map/all_to_all | solution.py:495
  94.6 2.3 %collective-permute-start.7 = (bf16[128,1280]{1,0:T(8,128)(2,1)S(1)}, bf16[128,1280]{1,0:T(8,128)(2,1)S(1)}, u32[]{:S(2)}, u32[]{:S(2)}) collective-permute-start(bf16[128,1280]{1,0:T(8,128)(2,1)S(1)} %bitcast.11), channel_id=1, source_target_pairs={{0,1},{1,0},{2,3},{3,2},{4,5},{5,4},{6,7},{7,6},{8,9},{9,8},{10,11... | collective-permute-start | bytes 983048 | tf_op jit(solution)/shard_map/ppermute | solution.py:498
  96.9 1.3 %collective-permute-done.7.other_ref = bf16[128,1280]{1,0:T(8,128)(2,1)S(1)} collective-permute-done((bf16[128,1280]{1,0:T(8,128)(2,1)S(1)}, bf16[128,1280]{1,0:T(8,128)(2,1)S(1)}, u32[]{:S(2)}, u32[]{:S(2)}) %collective-permute-start.7) | collective-permute-done | bytes 327712 | tf_op jit(solution)/shard_map/ppermute | solution.py:498
  98.1 1.1 choose.1
  99.3 3.6 %all-to-all-start.3 = ((bf16[16,8,2176]{2,1,0:T(8,128)(2,1)}), bf16[16,8,2176]{2,1,0:T(8,128)(2,1)S(1)}, u32[]{:S(2)}, u32[]{:S(2)}) async-start(bf16[16,8,2176]{2,1,0:T(8,128)(2,1)} %bitcast.6), calls=%async_computation.3 | async-start | bytes 1114112 | tf_op jit(solution)/shard_map/all_to_all | solution.py:499
  102.9 0.6 collective-permute-start.6
  103.4 1.3 %collective-permute-done.6.other_ref = bf16[8,64,384]{2,1,0:T(8,128)(2,1)S(1)} collective-permute-done((bf16[8,64,384]{2,1,0:T(8,128)(2,1)S(1)}, bf16[8,64,384]{2,1,0:T(8,128)(2,1)S(1)}, u32[]{:S(2)}, u32[]{:S(2)}) %collective-permute-start.6) | collective-permute-done | bytes 393248 | tf_op jit(solution)/shard_map/ppermute | solution.py:493
  104.8 0.0 copy-start
  104.8 2.2 %copy-done = bf16[8,1,512,512]{3,2,1,0:T(8,128)(2,1)S(1)} copy-done((bf16[8,1,512,512]{3,2,1,0:T(8,128)(2,1)S(1)}, bf16[8,1,512,512]{3,2,1,0:T(8,128)(2,1)}, u32[]{:S(2)}) %copy-start) | copy-done | bytes 4194328
  106.9 0.9 project.1
  107.8 5.7 %all-to-all-done.3 = bf16[16,8,2176]{2,1,0:T(8,128)(2,1)S(1)} async-done(((bf16[16,8,2176]{2,1,0:T(8,128)(2,1)}), bf16[16,8,2176]{2,1,0:T(8,128)(2,1)S(1)}, u32[]{:S(2)}, u32[]{:S(2)}) %all-to-all-start.3) | async-done | bytes 557088 | tf_op jit(solution)/shard_map/all_to_all | solution.py:499
  113.5 3.1 %couple.1 = (f32[8,1,64,64]{3,2,1,0:T(8,128)}, f32[8,64,64]{2,1,0:T(8,128)}) custom-call(bf16[8,192,512]{2,1,0:T(8,128)(2,1)S(1)} %get-tuple-element.12.image_ref, f32[8,64,64]{2,1,0:T(8,128)S(1)} %get-tuple-element.13.upper_ref, bf16[128,2176]{1,0:T(8,128)(2,1)S(1)} %bitcast.9), custom_call_target="tpu_custom_call" | custom-call | tf_op jit(solution)/shard_map/couple/pallas_call | solution.py:445
  (2 shorter events, 0.0 us)
Async XLA Ops:
  0.6 21.6 %copy-start.2 = (s32[8]{0:T(128)S(1)}, s32[8]{0:T(128)}, u32[]{:S(2)}) copy-start(s32[8]{0:T(128)} %param.9) | copy-start | bytes 100
  0.6 21.6 %copy-start.3 = (s32[8,1]{0,1:T(1,128)S(1)}, s32[8,1]{0,1:T(1,128)}, u32[]{:S(2)}) copy-start(s32[8,1]{0,1:T(1,128)} %param.8) | copy-start | bytes 100
  3.8 10.6 %collective-permute-start = (f32[4,256,128]{2,1,0:T(8,128)S(1)}, f32[4,256,128]{2,1,0:T(8,128)S(1)}, u32[]{:S(2)}, u32[]{:S(2)}) collective-permute-start(f32[4,256,128]{2,1,0:T(8,128)S(1)} %mixed_probes.2.own_a), channel_id=1, source_target_pairs={{0,16},{2,18},{4,20},{6,22},{8,24},{10,26},{12,28},{14,30},{16,32}... | collective-permute-start | bytes 1572872 | tf_op jit(solution)/shard_map/ppermute | solution.py:483
  8.3 11.7 %collective-permute-start.1 = (f32[4,256,128]{2,1,0:T(8,128)S(1)}, f32[4,256,128]{2,1,0:T(8,128)S(1)}, u32[]{:S(2)}, u32[]{:S(2)}) collective-permute-start(f32[4,256,128]{2,1,0:T(8,128)S(1)} %mixed_probes.3.after_ref.own_b), channel_id=1, source_target_pairs={{0,16},{2,18},{4,20},{6,22},{8,24},{10,26},{12,28},{14,30},{16,32}... | collective-permute-start | bytes 1572872 | tf_op jit(solution)/shard_map/ppermute | solution.py:483
  14.4 10.0 %collective-permute-start.2 = (f32[4,256,128]{2,1,0:T(8,128)S(1)}, f32[4,256,128]{2,1,0:T(8,128)S(1)}, u32[]{:S(2)}, u32[]{:S(2)}) collective-permute-start(f32[4,256,128]{2,1,0:T(8,128)S(1)} %collective-permute-done.moved_a), channel_id=1, source_target_pairs={{0,1},{1,0},{2,3},{3,2},{4,5},{5,4},{6,7},{7,6},{8,9},{9,8},{10,11... | collective-permute-start | bytes 1572872 | tf_op jit(solution)/shard_map/ppermute | solution.py:484
  20.1 4.4 %collective-permute-start.3 = (f32[4,256,128]{2,1,0:T(8,128)S(1)}, f32[4,256,128]{2,1,0:T(8,128)S(1)}, u32[]{:S(2)}, u32[]{:S(2)}) collective-permute-start(f32[4,256,128]{2,1,0:T(8,128)S(1)} %collective-permute-done.1.moved_b), channel_id=1, source_target_pairs={{0,1},{1,0},{2,3},{3,2},{4,5},{5,4},{6,7},{7,6},{8,9},{9,8},{10,11... | collective-permute-start | bytes 1572872 | tf_op jit(solution)/shard_map/ppermute | solution.py:484
  28.9 49.4 %copy-start.1 = (s32[8,1]{0,1:T(1,128)S(1)}, s32[8,1]{0,1:T(1,128)}, u32[]{:S(2)}) copy-start(s32[8,1]{0,1:T(1,128)} %param.13) | copy-start | bytes 100
  28.9 2.0 %collective-permute-start.4 = (f32[8,128,128]{2,1,0:T(8,128)S(1)}, f32[8,128,128]{2,1,0:T(8,128)S(1)}, u32[]{:S(2)}, u32[]{:S(2)}) collective-permute-start(f32[8,128,128]{2,1,0:T(8,128)S(1)} %get-tuple-element.9), channel_id=1, source_target_pairs={{0,1},{1,0},{2,3},{3,2},{4,5},{5,4},{6,7},{7,6},{8,9},{9,8},{10,11... | collective-permute-start | bytes 1572872 | tf_op jit(solution)/shard_map/ppermute | solution.py:488
  57.2 1.5 %collective-permute-start.5 = (f32[64,64]{1,0:T(8,128)S(1)}, f32[64,64]{1,0:T(8,128)S(1)}, u32[]{:S(2)}, u32[]{:S(2)}) collective-permute-start(f32[64,64]{1,0:T(8,128)S(1)} %get-tuple-element.11.gram_ref), channel_id=1, source_target_pairs={{0,1},{1,0},{2,3},{3,2},{4,5},{5,4},{6,7},{7,6},{8,9},{9,8},{10,11... | collective-permute-start | bytes 49160 | tf_op jit(solution)/shard_map/ppermute | solution.py:491
  94.6 3.5 %collective-permute-start.7 = (bf16[128,1280]{1,0:T(8,128)(2,1)S(1)}, bf16[128,1280]{1,0:T(8,128)(2,1)S(1)}, u32[]{:S(2)}, u32[]{:S(2)}) collective-permute-start(bf16[128,1280]{1,0:T(8,128)(2,1)S(1)} %bitcast.11), channel_id=1, source_target_pairs={{0,1},{1,0},{2,3},{3,2},{4,5},{5,4},{6,7},{7,6},{8,9},{9,8},{10,11... | collective-permute-start | bytes 983048 | tf_op jit(solution)/shard_map/ppermute | solution.py:498
  99.3 14.2 %all-to-all-start.3 = ((bf16[16,8,2176]{2,1,0:T(8,128)(2,1)}), bf16[16,8,2176]{2,1,0:T(8,128)(2,1)S(1)}, u32[]{:S(2)}, u32[]{:S(2)}) async-start(bf16[16,8,2176]{2,1,0:T(8,128)(2,1)} %bitcast.6), calls=%async_computation.3 | async-start | bytes 1114112 | tf_op jit(solution)/shard_map/all_to_all | solution.py:499
  102.9 1.9 %collective-permute-start.6 = (bf16[8,64,384]{2,1,0:T(8,128)(2,1)S(1)}, bf16[8,64,384]{2,1,0:T(8,128)(2,1)S(1)}, u32[]{:S(2)}, u32[]{:S(2)}) collective-permute-start(bf16[8,64,384]{2,1,0:T(8,128)(2,1)S(1)} %all_to_all.21.own_ref), channel_id=1, source_target_pairs={{0,1},{1,0},{2,3},{3,2},{4,5},{5,4},{6,7},{7,6},{8,9},{9,8},{10,11... | collective-permute-start | bytes 1179656 | tf_op jit(solution)/shard_map/ppermute | solution.py:493
  104.8 2.2 %copy-start = (bf16[8,1,512,512]{3,2,1,0:T(8,128)(2,1)S(1)}, bf16[8,1,512,512]{3,2,1,0:T(8,128)(2,1)}, u32[]{:S(2)}) copy-start(bf16[8,1,512,512]{3,2,1,0:T(8,128)(2,1)} %far_ref.1) | copy-start | bytes 12582916

commit v7 on v3

--- a/solution.py
+++ b/solution.py
@@ -104,40 +104,69 @@
     return jnp.concatenate([jnp.where(lane < RANK, x, turned), jnp.where(lane < RANK, turned, x)], axis=0)
 
 
-def mixed_probes_kernel(start, mixing_hbm, probes_ref, out_ref, mixing_ref, tiles_ref, sems):
+def first_probes_kernel(mixing_hbm, probes_ref, out_ref, rest_ref, weights_ref, mixing_ref, tiles_ref, sems):
     part = out_ref.shape[0]
-    first = pltpu.make_async_copy(mixing_hbm, mixing_ref, sems.at[part])
-    copies = [pltpu.make_async_copy(probes_ref.at[start + i], tiles_ref.at[i], sems.at[i]) for i in range(part)]
-    for copy in [first] + copies:
+    first = pltpu.make_async_copy(mixing_hbm, mixing_ref, sems.at[2 * part])
+    copies = [pltpu.make_async_copy(probes_ref.at[i], tiles_ref.at[i], sems.at[i]) for i in range(part)]
+    later = [
+        pltpu.make_async_copy(probes_ref.at[part + i], rest_ref.at[i], sems.at[part + i])
+        for i in range(rest_ref.shape[0])
+    ]
+    for copy in [first] + copies + later:
         copy.start()
     first.wait()
     mixing = mixing_ref[...]
     weights = weights_of(jnp.concatenate([mixing, mixing], axis=0).T)
+    weights_ref[...] = weights
     for i, copy in enumerate(copies):
         copy.wait()
         out_ref[i] = folded(weighted(tiles_ref[i], weights))
-
-
-def mixed_probes(start, part, mixing, probes):
-    _, rows, width = probes.shape
-    return pl.pallas_call(
-        functools.partial(mixed_probes_kernel, start),
-        out_shape=pltpu.VMEM((part, rows // 2, LANES), f32),
+    for copy in later:
+        copy.wait()
+
+
+def rest_probes_kernel(rest_ref, weights_ref, out_ref):
+    for i in range(out_ref.shape[0]):
+        out_ref[i] = folded(weighted(rest_ref[i], weights_ref[...]))
+
+
+def mixed_probes(mixing, probes):
+    count, rows, width = probes.shape
+    part = count // 2
+    half = pltpu.VMEM((part, rows // 2, LANES), f32)
+    cost = pl.CostEstimate(
+        flops=2 * part * rows * width * 3 * RANK,
+        bytes_accessed=part * rows * (2 * width + 4 * RANK),
+        transcendentals=0,
+    )
+    first, rest, weights = pl.pallas_call(
+        first_probes_kernel,
+        out_shape=(
+            half,
+            pltpu.VMEM((count - part, rows, width), bf16),
+            pltpu.VMEM((width, 2 * LANES), bf16),
+        ),
         in_specs=[HBM, HBM],
-        out_specs=VMEM,
+        out_specs=(VMEM, VMEM, VMEM),
         scratch_shapes=[
             pltpu.VMEM(mixing.shape, f32),
             pltpu.VMEM((part, rows, width), bf16),
-            pltpu.SemaphoreType.DMA((part + 1,)),
+            pltpu.SemaphoreType.DMA((2 * part + 1,)),
         ],
-        cost_estimate=pl.CostEstimate(
-            flops=2 * part * rows * width * 3 * RANK,
-            bytes_accessed=part * rows * (2 * width + 4 * RANK),
-            transcendentals=0,
-        ),
-        compiler_params=LIMIT,
-        name="mixed_probes",
+        cost_estimate=cost,
+        compiler_params=LIMIT,
+        name="first_probes",
     )(mixing, probes)
+    second = pl.pallas_call(
+        rest_probes_kernel,
+        out_shape=half,
+        in_specs=[VMEM, VMEM],
+        out_specs=VMEM,
+        cost_estimate=cost,
+        compiler_params=LIMIT,
+        name="rest_probes",
+    )(in_vmem(rest), in_vmem(weights))
+    return [first, second]
 
 
 def load_kernel(*refs):
@@ -152,15 +181,15 @@
         copy.wait()
 
 
-def load(after, *arrays):
-    def kernel(after_ref, *refs):
+def load(meta, after, *arrays):
+    def kernel(meta_ref, after_ref, *refs):
         load_kernel(*refs)
 
     arrays = [pltpu.with_memory_space_constraint(x, pltpu.HBM) for x in arrays]
     return pl.pallas_call(
         kernel,
         out_shape=tuple(pltpu.VMEM(x.shape, x.dtype) for x in arrays),
-        in_specs=[VMEM] + [HBM] * len(arrays),
+        in_specs=[SMEM, VMEM] + [HBM] * len(arrays),
         out_specs=(VMEM,) * len(arrays),
         scratch_shapes=[pltpu.SemaphoreType.DMA((len(arrays),))],
         cost_estimate=pl.CostEstimate(
@@ -168,7 +197,7 @@
         ),
         compiler_params=LIMIT,
         name="load",
-    )(in_vmem(after), *arrays)
+    )(meta, in_vmem(after), *arrays)
 
 
 def sketch_kernel(
@@ -450,11 +479,12 @@
     near_meta = jnp.concatenate([near_cols[:, 0] - (leaf_pos * count - REACH), live, core])
 
     mixing, probes = (pltpu.with_memory_space_constraint(x, pltpu.HBM) for x in (mixing.T, probes))
-    part = count // 2
-    own = [mixed_probes(start, part, mixing, probes) for start in (0, part)]
+    own = mixed_probes(mixing, probes)
     moved = [lax.ppermute(x, ("leaf", "blk"), shift) for x in own]
-    other = [lax.ppermute(x, "blk", pair) for x in moved]
-    (near_tiles,) = load(own[1], near_tiles)
+    other = [lax.ppermute(moved[0], "blk", pair)]
+    (near_tiles,) = load(near_meta, other[0], near_tiles)
+    moved[1], near_tiles = lax.optimization_barrier((moved[1], near_tiles))
+    other.append(lax.ppermute(moved[1], "blk", pair))
     keep, send = compress(near_meta, own + moved + other, near_tiles)
     halves = keep + lax.ppermute(send, "blk", pair)
     terms = lax.all_to_all(halves, "blk", 0, 0, tiled=True, axis_index_groups=lanes)

time: 117 us -> 114 us (0.974)
  waiting for transfers between devices: 13.1 us -> 21.1 us
  starting transfers between devices: 18.6 us -> 13.4 us
  local copies, waits for them, and re-layouts: 6.34 us -> 2.2 us
  Pallas kernels: 19.8 us -> 18.2 us
    ppermute x2, waiting for transfers between devices: 1.01 us -> 7.43 us  [shards(): moved = [lax.ppermute(x, ('leaf', 'blk'), shift) for x in own]]
    ppermute x2, starting transfers between devices: 7.33 us -> 2.15 us  [the longest x1 1.08 us: shards(): other = [lax.ppermute(moved[0], 'blk', pair)]]
    unnamed x12 -> x8, local copies, waits for them, and re-layouts: 6.34 us -> 2.2 us
    pallas_call x2, Pallas kernels: 6.23 us -> 3.94 us  [the longest x1 3.17 us: mixed_probes(): pl.pallas_call(first_probes_kernel, out_shape=(half, pltpu.VMEM((count -...]
    ppermute x2, waiting for transfers between devices: 1.42 us -> 2.97 us  [the longest x1 1.54 us: shards(): other.append(lax.ppermute(moved[1], 'blk', pair))]
  transfers between devices with their start and end apart: 9 -> 9, of which waited for: 8 -> 9; matrix products, arithmetic and copies ran while one was open for 0% -> 0% of each run, Pallas kernels for 5% -> 4%
where the time goes in v7:
time: 114 us
  blocking collectives  58 us (51%)
  waiting for transfers between devices  21.1 us (19%)
  Pallas kernels  18.2 us (16%)
  starting transfers between devices  13.4 us (12%)
  local copies, waits for them, and re-layouts  2.2 us (2%)
    all_to_all x1, blocking collectives, shards(): lax.all_to_all(halves, 'blk', 0, 0, tiled=True, axis_index_groups=lanes)  24.7 us
    all_to_all x1, blocking collectives, shards(): own = lax.all_to_all(own, 'blk', 0, 0, tiled=True, axis_index_groups=lanes)  17.5 us
    all_to_all x1, blocking collectives, shards(): lax.all_to_all(payload.reshape(subtrees, count, -1), 'leaf', 0, 0, tiled=...  15.8 us
    ppermute x2, waiting for transfers between devices, shards(): moved = [lax.ppermute(x, ('leaf', 'blk'), shift) for x in own]  7.43 us
    all_to_all x1, waiting for transfers between devices, shards(): lax.all_to_all(chosen.reshape(subtrees, count, -1), 'leaf', 0, 0, tiled=T...  5.69 us
    all_to_all x1, starting transfers between devices, shards(): lax.all_to_all(chosen.reshape(subtrees, count, -1), 'leaf', 0, 0, tiled=T...  3.58 us
    pallas_call x1, Pallas kernels, mixed_probes(): pl.pallas_call(first_probes_kernel, out_shape=(half, pltpu.VMEM((count -...  3.17 us
    pallas_call x1, Pallas kernels, couple(): pl.pallas_call(functools.partial(couple_kernel, scale), out_shape=(jax.Sh...  3.14 us
  transfers between devices with their start and end apart: 9, of which 9 were waited for; matrix products, arithmetic and copies ran while one was open for 0% of the time, Pallas kernels for 4%

profile of v7, /device:TPU:1, one launch (start us, length us, event | category | flops | bytes accessed | tf_op | source)
XLA Modules:
  0.0 113.9 jit_solution(14175756214687444364)
XLA Ops:
  0.6 0.0 copy-start.2
  0.6 0.0 copy-start.3
  0.7 3.2 %first_probes.1 = (f32[4,256,128]{2,1,0:T(8,128)S(1)}, bf16[4,512,512]{2,1,0:T(8,128)(2,1)S(1)}, bf16[512,256]{1,0:T(8,128)(2,1)S(1)}) custom-call(f32[64,512]{1,0:T(8,128)} %bitcast.14, bf16[8,512,512]{2,1,0:T(8,128)(2,1)} %probes_ref.1), custom_call_target="tpu_custom_call" | custom-call | flops 402653184 | bytes 2621440 | tf_op jit(solution)/shard_map/first_probes/pallas_call | solution.py:142
  3.8 1.3 %collective-permute-start = (f32[4,256,128]{2,1,0:T(8,128)S(1)}, f32[4,256,128]{2,1,0:T(8,128)S(1)}, u32[]{:S(2)}, u32[]{:S(2)}) collective-permute-start(f32[4,256,128]{2,1,0:T(8,128)S(1)} %get-tuple-element.13.own_a), channel_id=1, source_target_pairs={{0,16},{2,18},{4,20},{6,22},{8,24},{10,26},{12,28},{14,30},{16,32}... | collective-permute-start | bytes 1572872 | tf_op jit(solution)/shard_map/ppermute | solution.py:483
  5.1 0.8 rest_probes.1.own_b
  5.9 1.3 %collective-permute-start.1 = (f32[4,256,128]{2,1,0:T(8,128)S(1)}, f32[4,256,128]{2,1,0:T(8,128)S(1)}, u32[]{:S(2)}, u32[]{:S(2)}) collective-permute-start(f32[4,256,128]{2,1,0:T(8,128)S(1)} %rest_probes.1.own_b), channel_id=1, source_target_pairs={{0,16},{2,18},{4,20},{6,22},{8,24},{10,26},{12,28},{14,30},{16,32}... | collective-permute-start | bytes 1572872 | tf_op jit(solution)/shard_map/ppermute | solution.py:483
  7.2 7.2 %collective-permute-done.moved_a = f32[4,256,128]{2,1,0:T(8,128)S(1)} collective-permute-done((f32[4,256,128]{2,1,0:T(8,128)S(1)}, f32[4,256,128]{2,1,0:T(8,128)S(1)}, u32[]{:S(2)}, u32[]{:S(2)}) %collective-permute-start) | collective-permute-done | bytes 524320 | tf_op jit(solution)/shard_map/ppermute | solution.py:483
  14.4 1.1 collective-permute-start.2
  15.5 0.0 copy-done.2
  15.5 0.0 copy-done.3
  15.5 0.1 pad_add_fusion.meta_ref
  15.6 1.4 %collective-permute-done.2.after_ref.other_a = f32[4,256,128]{2,1,0:T(8,128)S(1)} collective-permute-done((f32[4,256,128]{2,1,0:T(8,128)S(1)}, f32[4,256,128]{2,1,0:T(8,128)S(1)}, u32[]{:S(2)}, u32[]{:S(2)}) %collective-permute-start.2) | collective-permute-done | bytes 524320 | tf_op jit(solution)/shard_map/ppermute | solution.py:484
  17.0 2.7 %load.1.near_ref = bf16[8,1,512,512]{3,2,1,0:T(8,128)(2,1)S(1)} custom-call(s32[17]{0:T(128)S(1)} %pad_add_fusion.meta_ref, f32[4,256,128]{2,1,0:T(8,128)S(1)} %collective-permute-done.2.after_ref.other_a, bf16[8,1,512,512]{3,2,1,0:T(8,128)(2,1)} %refs_0_.1), custom_call_target="tpu_custom_call" | custom-call | bytes 8388608 | tf_op jit(solution)/shard_map/load/pallas_call | solution.py:189
  19.8 0.0 copy-start.1
  19.8 0.2 collective-permute-done.1.moved_b
  20.0 1.1 collective-permute-start.3
  21.1 1.5 %collective-permute-done.3.other_b = f32[4,256,128]{2,1,0:T(8,128)S(1)} collective-permute-done((f32[4,256,128]{2,1,0:T(8,128)S(1)}, f32[4,256,128]{2,1,0:T(8,128)S(1)}, u32[]{:S(2)}, u32[]{:S(2)}) %collective-permute-start.3) | collective-permute-done | bytes 524320 | tf_op jit(solution)/shard_map/ppermute | solution.py:487
  22.6 2.8 %compress.1 = (f32[8,128,128]{2,1,0:T(8,128)S(1)}, f32[8,128,128]{2,1,0:T(8,128)S(1)}) custom-call(s32[17]{0:T(128)S(1)} %pad_add_fusion.meta_ref, f32[4,256,128]{2,1,0:T(8,128)S(1)} %get-tuple-element.13.own_a, f32[4,256,128]{2,1,0:T(8,128)S(1)} %rest_probes.1.own_b, f32[4,256,128]{2,1,0:T(8,128)S(1)} %collective-permute-done.moved_a, ...), custom_call_target="tpu_custom_call" | custom-call | flops 805306368 | bytes 8388608 | tf_op jit(solution)/shard_map/compress/pallas_call | solution.py:235
  25.4 0.5 collective-permute-start.4
  25.9 1.5 %collective-permute-done.4 = f32[8,128,128]{2,1,0:T(8,128)S(1)} collective-permute-done((f32[8,128,128]{2,1,0:T(8,128)S(1)}, f32[8,128,128]{2,1,0:T(8,128)S(1)}, u32[]{:S(2)}, u32[]{:S(2)}) %collective-permute-start.4) | collective-permute-done | bytes 524320 | tf_op jit(solution)/shard_map/ppermute | solution.py:489
  27.4 0.1 add.9
  27.5 24.7 %all_to_all.20.terms_ref = f32[8,128,128]{2,1,0:T(8,128)S(1)} all-to-all(f32[8,128,128]{2,1,0:T(8,128)S(1)} %add.9), channel_id=1, replica_groups={{0,2,4,6,8,10,12,14},{1,3,5,7,9,11,13,15},{16,18,20,22,24,26,28,30},{17..., dimensions={0} | all-to-all | bytes 1048576 | tf_op jit(solution)/shard_map/all_to_all | solution.py:490
  52.2 0.3 gram.1
  52.5 1.8 %collective-permute-start.5 = (f32[64,64]{1,0:T(8,128)S(1)}, f32[64,64]{1,0:T(8,128)S(1)}, u32[]{:S(2)}, u32[]{:S(2)}) collective-permute-start(f32[64,64]{1,0:T(8,128)S(1)} %get-tuple-element.21.gram_ref), channel_id=1, source_target_pairs={{0,1},{1,0},{2,3},{3,2},{4,5},{5,4},{6,7},{7,6},{8,9},{9,8},{10,11... | collective-permute-start | bytes 49160 | tf_op jit(solution)/shard_map/ppermute | solution.py:492
  54.3 0.9 collective-permute-done.5.other_ref
  55.2 2.0 %basis.1 = bf16[8,64,384]{2,1,0:T(8,128)(2,1)S(1)} custom-call(s32[1]{0:T(128)} %bitcast.core_ref, f32[128,128]{1,0:T(8,128)S(1)} %get-tuple-element.20.mixed_ref, f32[64,64]{1,0:T(8,128)S(1)} %get-tuple-element.21.gram_ref, f32[64,64]{1,0:T(8,128)S(1)} %collective-permute-done.5.other_ref), custom_call_target="tpu_custom_call" | custom-call | tf_op jit(solution)/shard_map/basis/pallas_call | solution.py:289
  57.2 17.5 %all_to_all.21.own_ref = bf16[8,64,384]{2,1,0:T(8,128)(2,1)S(1)} all-to-all(bf16[8,64,384]{2,1,0:T(8,128)(2,1)S(1)} %basis.1), channel_id=1, replica_groups={{0,2,4,6,8,10,12,14},{1,3,5,7,9,11,13,15},{16,18,20,22,24,26,28,30},{17..., dimensions={0} | all-to-all | bytes 786432 | tf_op jit(solution)/shard_map/all_to_all | solution.py:493
  74.8 0.0 copy-done.1
  74.8 1.3 %spread.1 = bf16[128,1280]{1,0:T(8,128)(2,1)S(1)} custom-call(s32[8]{0:T(128)S(1)} %bitcast.13, bf16[8,64,384]{2,1,0:T(8,128)(2,1)S(1)} %all_to_all.21.own_ref), custom_call_target="tpu_custom_call" | custom-call | tf_op jit(solution)/shard_map/spread/pallas_call | solution.py:340
  76.1 15.8 %all_to_all.22 = bf16[16,8,1280]{2,1,0:T(8,128)(2,1)S(1)} all-to-all(bf16[16,8,1280]{2,1,0:T(8,128)(2,1)S(1)} %bitcast.10), channel_id=1, replica_groups=mesh['leaf'=16,'blk'=16] {'leaf'}, dimensions={0} | all-to-all | bytes 655360 | tf_op jit(solution)/shard_map/all_to_all | solution.py:496
  91.9 2.3 %collective-permute-start.7 = (bf16[128,1280]{1,0:T(8,128)(2,1)S(1)}, bf16[128,1280]{1,0:T(8,128)(2,1)S(1)}, u32[]{:S(2)}, u32[]{:S(2)}) collective-permute-start(bf16[128,1280]{1,0:T(8,128)(2,1)S(1)} %bitcast.11), channel_id=1, source_target_pairs={{0,1},{1,0},{2,3},{3,2},{4,5},{5,4},{6,7},{7,6},{8,9},{9,8},{10,11... | collective-permute-start | bytes 983048 | tf_op jit(solution)/shard_map/ppermute | solution.py:499
  94.1 1.3 %collective-permute-done.7.other_ref = bf16[128,1280]{1,0:T(8,128)(2,1)S(1)} collective-permute-done((bf16[128,1280]{1,0:T(8,128)(2,1)S(1)}, bf16[128,1280]{1,0:T(8,128)(2,1)S(1)}, u32[]{:S(2)}, u32[]{:S(2)}) %collective-permute-start.7) | collective-permute-done | bytes 327712 | tf_op jit(solution)/shard_map/ppermute | solution.py:499
  95.4 1.1 choose.1
  96.5 3.6 %all-to-all-start.3 = ((bf16[16,8,2176]{2,1,0:T(8,128)(2,1)}), bf16[16,8,2176]{2,1,0:T(8,128)(2,1)S(1)}, u32[]{:S(2)}, u32[]{:S(2)}) async-start(bf16[16,8,2176]{2,1,0:T(8,128)(2,1)} %bitcast.6), calls=%async_computation.3 | async-start | bytes 1114112 | tf_op jit(solution)/shard_map/all_to_all | solution.py:500
  100.1 0.6 collective-permute-start.6
  100.7 1.3 %collective-permute-done.6.other_ref = bf16[8,64,384]{2,1,0:T(8,128)(2,1)S(1)} collective-permute-done((bf16[8,64,384]{2,1,0:T(8,128)(2,1)S(1)}, bf16[8,64,384]{2,1,0:T(8,128)(2,1)S(1)}, u32[]{:S(2)}, u32[]{:S(2)}) %collective-permute-start.6) | collective-permute-done | bytes 393248 | tf_op jit(solution)/shard_map/ppermute | solution.py:494
  102.0 0.0 copy-start
  102.0 2.2 %copy-done = bf16[8,1,512,512]{3,2,1,0:T(8,128)(2,1)S(1)} copy-done((bf16[8,1,512,512]{3,2,1,0:T(8,128)(2,1)S(1)}, bf16[8,1,512,512]{3,2,1,0:T(8,128)(2,1)}, u32[]{:S(2)}) %copy-start) | copy-done | bytes 4194328
  104.2 0.9 project.1
  105.1 5.7 %all-to-all-done.3 = bf16[16,8,2176]{2,1,0:T(8,128)(2,1)S(1)} async-done(((bf16[16,8,2176]{2,1,0:T(8,128)(2,1)}), bf16[16,8,2176]{2,1,0:T(8,128)(2,1)S(1)}, u32[]{:S(2)}, u32[]{:S(2)}) %all-to-all-start.3) | async-done | bytes 557088 | tf_op jit(solution)/shard_map/all_to_all | solution.py:500
  110.8 3.1 %couple.1 = (f32[8,1,64,64]{3,2,1,0:T(8,128)}, f32[8,64,64]{2,1,0:T(8,128)}) custom-call(bf16[8,192,512]{2,1,0:T(8,128)(2,1)S(1)} %get-tuple-element.22.image_ref, f32[8,64,64]{2,1,0:T(8,128)S(1)} %get-tuple-element.23.upper_ref, bf16[128,2176]{1,0:T(8,128)(2,1)S(1)} %bitcast.9), custom_call_target="tpu_custom_call" | custom-call | tf_op jit(solution)/shard_map/couple/pallas_call | solution.py:446
  (2 shorter events, 0.0 us)
Async XLA Ops:
  0.6 14.9 %copy-start.2 = (s32[8]{0:T(128)S(1)}, s32[8]{0:T(128)}, u32[]{:S(2)}) copy-start(s32[8]{0:T(128)} %param.9) | copy-start | bytes 100
  0.6 14.9 %copy-start.3 = (s32[8,1]{0,1:T(1,128)S(1)}, s32[8,1]{0,1:T(1,128)}, u32[]{:S(2)}) copy-start(s32[8,1]{0,1:T(1,128)} %param.8) | copy-start | bytes 100
  3.8 10.6 %collective-permute-start = (f32[4,256,128]{2,1,0:T(8,128)S(1)}, f32[4,256,128]{2,1,0:T(8,128)S(1)}, u32[]{:S(2)}, u32[]{:S(2)}) collective-permute-start(f32[4,256,128]{2,1,0:T(8,128)S(1)} %get-tuple-element.13.own_a), channel_id=1, source_target_pairs={{0,16},{2,18},{4,20},{6,22},{8,24},{10,26},{12,28},{14,30},{16,32}... | collective-permute-start | bytes 1572872 | tf_op jit(solution)/shard_map/ppermute | solution.py:483
  5.9 14.1 %collective-permute-start.1 = (f32[4,256,128]{2,1,0:T(8,128)S(1)}, f32[4,256,128]{2,1,0:T(8,128)S(1)}, u32[]{:S(2)}, u32[]{:S(2)}) collective-permute-start(f32[4,256,128]{2,1,0:T(8,128)S(1)} %rest_probes.1.own_b), channel_id=1, source_target_pairs={{0,16},{2,18},{4,20},{6,22},{8,24},{10,26},{12,28},{14,30},{16,32}... | collective-permute-start | bytes 1572872 | tf_op jit(solution)/shard_map/ppermute | solution.py:483
  14.4 2.6 %collective-permute-start.2 = (f32[4,256,128]{2,1,0:T(8,128)S(1)}, f32[4,256,128]{2,1,0:T(8,128)S(1)}, u32[]{:S(2)}, u32[]{:S(2)}) collective-permute-start(f32[4,256,128]{2,1,0:T(8,128)S(1)} %collective-permute-done.moved_a), channel_id=1, source_target_pairs={{0,1},{1,0},{2,3},{3,2},{4,5},{5,4},{6,7},{7,6},{8,9},{9,8},{10,11... | collective-permute-start | bytes 1572872 | tf_op jit(solution)/shard_map/ppermute | solution.py:484
  19.8 55.0 %copy-start.1 = (s32[8,1]{0,1:T(1,128)S(1)}, s32[8,1]{0,1:T(1,128)}, u32[]{:S(2)}) copy-start(s32[8,1]{0,1:T(1,128)} %param.13) | copy-start | bytes 100
  20.0 2.6 %collective-permute-start.3 = (f32[4,256,128]{2,1,0:T(8,128)S(1)}, f32[4,256,128]{2,1,0:T(8,128)S(1)}, u32[]{:S(2)}, u32[]{:S(2)}) collective-permute-start(f32[4,256,128]{2,1,0:T(8,128)S(1)} %collective-permute-done.1.moved_b), channel_id=1, source_target_pairs={{0,1},{1,0},{2,3},{3,2},{4,5},{5,4},{6,7},{7,6},{8,9},{9,8},{10,11... | collective-permute-start | bytes 1572872 | tf_op jit(solution)/shard_map/ppermute | solution.py:487
  25.4 2.0 %collective-permute-start.4 = (f32[8,128,128]{2,1,0:T(8,128)S(1)}, f32[8,128,128]{2,1,0:T(8,128)S(1)}, u32[]{:S(2)}, u32[]{:S(2)}) collective-permute-start(f32[8,128,128]{2,1,0:T(8,128)S(1)} %get-tuple-element.19), channel_id=1, source_target_pairs={{0,1},{1,0},{2,3},{3,2},{4,5},{5,4},{6,7},{7,6},{8,9},{9,8},{10,11... | collective-permute-start | bytes 1572872 | tf_op jit(solution)/shard_map/ppermute | solution.py:489
  52.5 2.7 %collective-permute-start.5 = (f32[64,64]{1,0:T(8,128)S(1)}, f32[64,64]{1,0:T(8,128)S(1)}, u32[]{:S(2)}, u32[]{:S(2)}) collective-permute-start(f32[64,64]{1,0:T(8,128)S(1)} %get-tuple-element.21.gram_ref), channel_id=1, source_target_pairs={{0,1},{1,0},{2,3},{3,2},{4,5},{5,4},{6,7},{7,6},{8,9},{9,8},{10,11... | collective-permute-start | bytes 49160 | tf_op jit(solution)/shard_map/ppermute | solution.py:492
  91.9 3.5 %collective-permute-start.7 = (bf16[128,1280]{1,0:T(8,128)(2,1)S(1)}, bf16[128,1280]{1,0:T(8,128)(2,1)S(1)}, u32[]{:S(2)}, u32[]{:S(2)}) collective-permute-start(bf16[128,1280]{1,0:T(8,128)(2,1)S(1)} %bitcast.11), channel_id=1, source_target_pairs={{0,1},{1,0},{2,3},{3,2},{4,5},{5,4},{6,7},{7,6},{8,9},{9,8},{10,11... | collective-permute-start | bytes 983048 | tf_op jit(solution)/shard_map/ppermute | solution.py:499
  96.5 14.2 %all-to-all-start.3 = ((bf16[16,8,2176]{2,1,0:T(8,128)(2,1)}), bf16[16,8,2176]{2,1,0:T(8,128)(2,1)S(1)}, u32[]{:S(2)}, u32[]{:S(2)}) async-start(bf16[16,8,2176]{2,1,0:T(8,128)(2,1)} %bitcast.6), calls=%async_computation.3 | async-start | bytes 1114112 | tf_op jit(solution)/shard_map/all_to_all | solution.py:500
  100.1 1.9 %collective-permute-start.6 = (bf16[8,64,384]{2,1,0:T(8,128)(2,1)S(1)}, bf16[8,64,384]{2,1,0:T(8,128)(2,1)S(1)}, u32[]{:S(2)}, u32[]{:S(2)}) collective-permute-start(bf16[8,64,384]{2,1,0:T(8,128)(2,1)S(1)} %all_to_all.21.own_ref), channel_id=1, source_target_pairs={{0,1},{1,0},{2,3},{3,2},{4,5},{5,4},{6,7},{7,6},{8,9},{9,8},{10,11... | collective-permute-start | bytes 1179656 | tf_op jit(solution)/shard_map/ppermute | solution.py:494
  102.0 2.2 %copy-start = (bf16[8,1,512,512]{3,2,1,0:T(8,128)(2,1)S(1)}, bf16[8,1,512,512]{3,2,1,0:T(8,128)(2,1)}, u32[]{:S(2)}) copy-start(bf16[8,1,512,512]{3,2,1,0:T(8,128)(2,1)} %far_ref.1) | copy-start | bytes 12582916

commit v8 on v7

--- a/solution.py
+++ b/solution.py
@@ -437,8 +437,9 @@
         ]
         terms = dot(image_ref[i], jnp.concatenate(far, axis=0).astype(bf16), NT)
         coupling_ref[i, 0] = terms[:RANK] + terms[RANK : 2 * RANK] + terms[2 * RANK :]
+    roots = dot(jnp.concatenate([upper_ref[i] for i in range(count)], axis=0), inverse, NT, highest) * scale
     for i in range(count):
-        root_ref[i] = dot(upper_ref[i], inverse, NT, highest) * scale
+        root_ref[i] = roots[i * RANK : (i + 1) * RANK]
 
 
 def couple(image, upper, received, scale):
@@ -481,10 +482,10 @@
     mixing, probes = (pltpu.with_memory_space_constraint(x, pltpu.HBM) for x in (mixing.T, probes))
     own = mixed_probes(mixing, probes)
     moved = [lax.ppermute(x, ("leaf", "blk"), shift) for x in own]
-    other = [lax.ppermute(moved[0], "blk", pair)]
-    (near_tiles,) = load(near_meta, other[0], near_tiles)
-    moved[1], near_tiles = lax.optimization_barrier((moved[1], near_tiles))
-    other.append(lax.ppermute(moved[1], "blk", pair))
+    (near_tiles,) = load(near_meta, own[1], near_tiles)
+    other = lax.ppermute(moved[0], "blk", pair)
+    moved[1], near_tiles, other = lax.optimization_barrier((moved[1], near_tiles, other))
+    other = [other, lax.ppermute(moved[1], "blk", pair)]
     keep, send = compress(near_meta, own + moved + other, near_tiles)
     halves = keep + lax.ppermute(send, "blk", pair)
     terms = lax.all_to_all(halves, "blk", 0, 0, tiled=True, axis_index_groups=lanes)

time: 114 us -> 114 us (level)
    ppermute x2, waiting for transfers between devices: 7.43 us -> 8.87 us  [shards(): moved = [lax.ppermute(x, ('leaf', 'blk'), shift) for x in own]]
    ppermute x2, waiting for transfers between devices: 2.97 us -> 1.54 us  [the longest x1 1.54 us: shards(): other = [other, lax.ppermute(moved[1], 'blk', pair)]]
  transfers between devices with their start and end apart: 9 -> 9, of which waited for: 9 -> 8; matrix products, arithmetic and copies ran while one was open for 0% -> 0% of each run, Pallas kernels for 4% -> 4%
where the time goes in v8:
time: 114 us
  blocking collectives  58 us (51%)
  waiting for transfers between devices  21.1 us (19%)
  Pallas kernels  18 us (16%)
  starting transfers between devices  13.4 us (12%)
  local copies, waits for them, and re-layouts  2.2 us (2%)
    all_to_all x1, blocking collectives, shards(): lax.all_to_all(halves, 'blk', 0, 0, tiled=True, axis_index_groups=lanes)  24.7 us
    all_to_all x1, blocking collectives, shards(): own = lax.all_to_all(own, 'blk', 0, 0, tiled=True, axis_index_groups=lanes)  17.5 us
    all_to_all x1, blocking collectives, shards(): lax.all_to_all(payload.reshape(subtrees, count, -1), 'leaf', 0, 0, tiled=...  15.8 us
    ppermute x2, waiting for transfers between devices, shards(): moved = [lax.ppermute(x, ('leaf', 'blk'), shift) for x in own]  8.87 us
    all_to_all x1, waiting for transfers between devices, shards(): lax.all_to_all(chosen.reshape(subtrees, count, -1), 'leaf', 0, 0, tiled=T...  5.69 us
    all_to_all x1, starting transfers between devices, shards(): lax.all_to_all(chosen.reshape(subtrees, count, -1), 'leaf', 0, 0, tiled=T...  3.58 us
    pallas_call x1, Pallas kernels, mixed_probes(): pl.pallas_call(first_probes_kernel, out_shape=(half, pltpu.VMEM((count -...  3.17 us
    pallas_call x1, Pallas kernels, couple(): pl.pallas_call(functools.partial(couple_kernel, scale), out_shape=(jax.Sh...  2.96 us
  transfers between devices with their start and end apart: 9, of which 8 were waited for; matrix products, arithmetic and copies ran while one was open for 0% of the time, Pallas kernels for 4%

profile of v8, /device:TPU:1, one launch (start us, length us, event | category | flops | bytes accessed | tf_op | source)
XLA Modules:
  0.0 113.7 jit_solution(5625161609727453698)
XLA Ops:
  0.6 0.0 copy-start.2
  0.6 0.0 copy-start.3
  0.7 3.2 %first_probes.1 = (f32[4,256,128]{2,1,0:T(8,128)S(1)}, bf16[4,512,512]{2,1,0:T(8,128)(2,1)S(1)}, bf16[512,256]{1,0:T(8,128)(2,1)S(1)}) custom-call(f32[64,512]{1,0:T(8,128)} %bitcast.14, bf16[8,512,512]{2,1,0:T(8,128)(2,1)} %probes_ref.1), custom_call_target="tpu_custom_call" | custom-call | flops 402653184 | bytes 2621440 | tf_op jit(solution)/shard_map/first_probes/pallas_call | solution.py:142
  3.8 1.3 %collective-permute-start = (f32[4,256,128]{2,1,0:T(8,128)S(1)}, f32[4,256,128]{2,1,0:T(8,128)S(1)}, u32[]{:S(2)}, u32[]{:S(2)}) collective-permute-start(f32[4,256,128]{2,1,0:T(8,128)S(1)} %get-tuple-element.14.own_a), channel_id=1, source_target_pairs={{0,16},{2,18},{4,20},{6,22},{8,24},{10,26},{12,28},{14,30},{16,32}... | collective-permute-start | bytes 1572872 | tf_op jit(solution)/shard_map/ppermute | solution.py:484
  5.1 0.8 rest_probes.1.after_ref.own_b
  5.9 1.3 %collective-permute-start.1 = (f32[4,256,128]{2,1,0:T(8,128)S(1)}, f32[4,256,128]{2,1,0:T(8,128)S(1)}, u32[]{:S(2)}, u32[]{:S(2)}) collective-permute-start(f32[4,256,128]{2,1,0:T(8,128)S(1)} %rest_probes.1.after_ref.own_b), channel_id=1, source_target_pairs={{0,16},{2,18},{4,20},{6,22},{8,24},{10,26},{12,28},{14,30},{16,32}... | collective-permute-start | bytes 1572872 | tf_op jit(solution)/shard_map/ppermute | solution.py:484
  7.2 7.2 %collective-permute-done.moved_a = f32[4,256,128]{2,1,0:T(8,128)S(1)} collective-permute-done((f32[4,256,128]{2,1,0:T(8,128)S(1)}, f32[4,256,128]{2,1,0:T(8,128)S(1)}, u32[]{:S(2)}, u32[]{:S(2)}) %collective-permute-start) | collective-permute-done | bytes 524320 | tf_op jit(solution)/shard_map/ppermute | solution.py:484
  14.4 1.1 collective-permute-start.2
  15.5 0.0 copy-done.2
  15.5 0.0 copy-done.3
  15.5 0.1 pad_add_fusion.meta_ref
  15.6 2.7 %load.1.near_ref = bf16[8,1,512,512]{3,2,1,0:T(8,128)(2,1)S(1)} custom-call(s32[17]{0:T(128)S(1)} %pad_add_fusion.meta_ref, f32[4,256,128]{2,1,0:T(8,128)S(1)} %rest_probes.1.after_ref.own_b, bf16[8,1,512,512]{3,2,1,0:T(8,128)(2,1)} %refs_0_.1), custom_call_target="tpu_custom_call" | custom-call | bytes 8388608 | tf_op jit(solution)/shard_map/load/pallas_call | solution.py:189
  18.3 0.0 copy-start.1
  18.4 1.7 %collective-permute-done.1.moved_b = f32[4,256,128]{2,1,0:T(8,128)S(1)} collective-permute-done((f32[4,256,128]{2,1,0:T(8,128)S(1)}, f32[4,256,128]{2,1,0:T(8,128)S(1)}, u32[]{:S(2)}, u32[]{:S(2)}) %collective-permute-start.1) | collective-permute-done | bytes 524320 | tf_op jit(solution)/shard_map/ppermute | solution.py:484
  20.0 0.0 collective-permute-done.2.other_a
  20.0 1.1 collective-permute-start.3
  21.1 1.5 %collective-permute-done.3.other_b = f32[4,256,128]{2,1,0:T(8,128)S(1)} collective-permute-done((f32[4,256,128]{2,1,0:T(8,128)S(1)}, f32[4,256,128]{2,1,0:T(8,128)S(1)}, u32[]{:S(2)}, u32[]{:S(2)}) %collective-permute-start.3) | collective-permute-done | bytes 524320 | tf_op jit(solution)/shard_map/ppermute | solution.py:488
  22.6 2.8 %compress.1 = (f32[8,128,128]{2,1,0:T(8,128)S(1)}, f32[8,128,128]{2,1,0:T(8,128)S(1)}) custom-call(s32[17]{0:T(128)S(1)} %pad_add_fusion.meta_ref, f32[4,256,128]{2,1,0:T(8,128)S(1)} %get-tuple-element.14.own_a, f32[4,256,128]{2,1,0:T(8,128)S(1)} %rest_probes.1.after_ref.own_b, f32[4,256,128]{2,1,0:T(8,128)S(1)} %collective-permute-done.moved_a, ...), custom_call_target="tpu_custom_call" | custom-call | flops 805306368 | bytes 8388608 | tf_op jit(solution)/shard_map/compress/pallas_call | solution.py:235
  25.4 0.5 collective-permute-start.4
  25.9 1.5 %collective-permute-done.4 = f32[8,128,128]{2,1,0:T(8,128)S(1)} collective-permute-done((f32[8,128,128]{2,1,0:T(8,128)S(1)}, f32[8,128,128]{2,1,0:T(8,128)S(1)}, u32[]{:S(2)}, u32[]{:S(2)}) %collective-permute-start.4) | collective-permute-done | bytes 524320 | tf_op jit(solution)/shard_map/ppermute | solution.py:490
  27.4 0.1 add.9
  27.5 24.7 %all_to_all.20.terms_ref = f32[8,128,128]{2,1,0:T(8,128)S(1)} all-to-all(f32[8,128,128]{2,1,0:T(8,128)S(1)} %add.9), channel_id=1, replica_groups={{0,2,4,6,8,10,12,14},{1,3,5,7,9,11,13,15},{16,18,20,22,24,26,28,30},{17..., dimensions={0} | all-to-all | bytes 1048576 | tf_op jit(solution)/shard_map/all_to_all | solution.py:491
  52.2 0.3 gram.1
  52.5 1.8 %collective-permute-start.5 = (f32[64,64]{1,0:T(8,128)S(1)}, f32[64,64]{1,0:T(8,128)S(1)}, u32[]{:S(2)}, u32[]{:S(2)}) collective-permute-start(f32[64,64]{1,0:T(8,128)S(1)} %get-tuple-element.23.gram_ref), channel_id=1, source_target_pairs={{0,1},{1,0},{2,3},{3,2},{4,5},{5,4},{6,7},{7,6},{8,9},{9,8},{10,11... | collective-permute-start | bytes 49160 | tf_op jit(solution)/shard_map/ppermute | solution.py:493
  54.3 0.9 collective-permute-done.5.other_ref
  55.2 2.0 %basis.1 = bf16[8,64,384]{2,1,0:T(8,128)(2,1)S(1)} custom-call(s32[1]{0:T(128)} %bitcast.core_ref, f32[128,128]{1,0:T(8,128)S(1)} %get-tuple-element.22.mixed_ref, f32[64,64]{1,0:T(8,128)S(1)} %get-tuple-element.23.gram_ref, f32[64,64]{1,0:T(8,128)S(1)} %collective-permute-done.5.other_ref), custom_call_target="tpu_custom_call" | custom-call | tf_op jit(solution)/shard_map/basis/pallas_call | solution.py:289
  57.2 17.5 %all_to_all.21.own_ref = bf16[8,64,384]{2,1,0:T(8,128)(2,1)S(1)} all-to-all(bf16[8,64,384]{2,1,0:T(8,128)(2,1)S(1)} %basis.1), channel_id=1, replica_groups={{0,2,4,6,8,10,12,14},{1,3,5,7,9,11,13,15},{16,18,20,22,24,26,28,30},{17..., dimensions={0} | all-to-all | bytes 786432 | tf_op jit(solution)/shard_map/all_to_all | solution.py:494
  74.8 0.0 copy-done.1
  74.8 1.3 %spread.1 = bf16[128,1280]{1,0:T(8,128)(2,1)S(1)} custom-call(s32[8]{0:T(128)S(1)} %bitcast.13, bf16[8,64,384]{2,1,0:T(8,128)(2,1)S(1)} %all_to_all.21.own_ref), custom_call_target="tpu_custom_call" | custom-call | tf_op jit(solution)/shard_map/spread/pallas_call | solution.py:340
  76.1 15.8 %all_to_all.22 = bf16[16,8,1280]{2,1,0:T(8,128)(2,1)S(1)} all-to-all(bf16[16,8,1280]{2,1,0:T(8,128)(2,1)S(1)} %bitcast.10), channel_id=1, replica_groups=mesh['leaf'=16,'blk'=16] {'leaf'}, dimensions={0} | all-to-all | bytes 655360 | tf_op jit(solution)/shard_map/all_to_all | solution.py:497
  91.9 2.3 %collective-permute-start.7 = (bf16[128,1280]{1,0:T(8,128)(2,1)S(1)}, bf16[128,1280]{1,0:T(8,128)(2,1)S(1)}, u32[]{:S(2)}, u32[]{:S(2)}) collective-permute-start(bf16[128,1280]{1,0:T(8,128)(2,1)S(1)} %bitcast.11), channel_id=1, source_target_pairs={{0,1},{1,0},{2,3},{3,2},{4,5},{5,4},{6,7},{7,6},{8,9},{9,8},{10,11... | collective-permute-start | bytes 983048 | tf_op jit(solution)/shard_map/ppermute | solution.py:500
  94.1 1.3 %collective-permute-done.7.other_ref = bf16[128,1280]{1,0:T(8,128)(2,1)S(1)} collective-permute-done((bf16[128,1280]{1,0:T(8,128)(2,1)S(1)}, bf16[128,1280]{1,0:T(8,128)(2,1)S(1)}, u32[]{:S(2)}, u32[]{:S(2)}) %collective-permute-start.7) | collective-permute-done | bytes 327712 | tf_op jit(solution)/shard_map/ppermute | solution.py:500
  95.4 1.1 choose.1
  96.5 3.6 %all-to-all-start.3 = ((bf16[16,8,2176]{2,1,0:T(8,128)(2,1)}), bf16[16,8,2176]{2,1,0:T(8,128)(2,1)S(1)}, u32[]{:S(2)}, u32[]{:S(2)}) async-start(bf16[16,8,2176]{2,1,0:T(8,128)(2,1)} %bitcast.6), calls=%async_computation.3 | async-start | bytes 1114112 | tf_op jit(solution)/shard_map/all_to_all | solution.py:501
  100.1 0.6 collective-permute-start.6
  100.7 1.3 %collective-permute-done.6.other_ref = bf16[8,64,384]{2,1,0:T(8,128)(2,1)S(1)} collective-permute-done((bf16[8,64,384]{2,1,0:T(8,128)(2,1)S(1)}, bf16[8,64,384]{2,1,0:T(8,128)(2,1)S(1)}, u32[]{:S(2)}, u32[]{:S(2)}) %collective-permute-start.6) | collective-permute-done | bytes 393248 | tf_op jit(solution)/shard_map/ppermute | solution.py:495
  102.0 0.0 copy-start
  102.0 2.2 %copy-done = bf16[8,1,512,512]{3,2,1,0:T(8,128)(2,1)S(1)} copy-done((bf16[8,1,512,512]{3,2,1,0:T(8,128)(2,1)S(1)}, bf16[8,1,512,512]{3,2,1,0:T(8,128)(2,1)}, u32[]{:S(2)}) %copy-start) | copy-done | bytes 4194328
  104.2 0.9 project.1
  105.1 5.7 %all-to-all-done.3 = bf16[16,8,2176]{2,1,0:T(8,128)(2,1)S(1)} async-done(((bf16[16,8,2176]{2,1,0:T(8,128)(2,1)}), bf16[16,8,2176]{2,1,0:T(8,128)(2,1)S(1)}, u32[]{:S(2)}, u32[]{:S(2)}) %all-to-all-start.3) | async-done | bytes 557088 | tf_op jit(solution)/shard_map/all_to_all | solution.py:501
  110.8 3.0 %couple.1 = (f32[8,1,64,64]{3,2,1,0:T(8,128)}, f32[8,64,64]{2,1,0:T(8,128)}) custom-call(bf16[8,192,512]{2,1,0:T(8,128)(2,1)S(1)} %get-tuple-element.24.image_ref, f32[8,64,64]{2,1,0:T(8,128)S(1)} %get-tuple-element.25.upper_ref, bf16[128,2176]{1,0:T(8,128)(2,1)S(1)} %bitcast.9), custom_call_target="tpu_custom_call" | custom-call | tf_op jit(solution)/shard_map/couple/pallas_call | solution.py:447
  (2 shorter events, 0.0 us)
Async XLA Ops:
  0.6 14.9 %copy-start.2 = (s32[8]{0:T(128)S(1)}, s32[8]{0:T(128)}, u32[]{:S(2)}) copy-start(s32[8]{0:T(128)} %param.9) | copy-start | bytes 100
  0.6 14.9 %copy-start.3 = (s32[8,1]{0,1:T(1,128)S(1)}, s32[8,1]{0,1:T(1,128)}, u32[]{:S(2)}) copy-start(s32[8,1]{0,1:T(1,128)} %param.8) | copy-start | bytes 100
  3.8 10.6 %collective-permute-start = (f32[4,256,128]{2,1,0:T(8,128)S(1)}, f32[4,256,128]{2,1,0:T(8,128)S(1)}, u32[]{:S(2)}, u32[]{:S(2)}) collective-permute-start(f32[4,256,128]{2,1,0:T(8,128)S(1)} %get-tuple-element.14.own_a), channel_id=1, source_target_pairs={{0,16},{2,18},{4,20},{6,22},{8,24},{10,26},{12,28},{14,30},{16,32}... | collective-permute-start | bytes 1572872 | tf_op jit(solution)/shard_map/ppermute | solution.py:484
  5.9 14.1 %collective-permute-start.1 = (f32[4,256,128]{2,1,0:T(8,128)S(1)}, f32[4,256,128]{2,1,0:T(8,128)S(1)}, u32[]{:S(2)}, u32[]{:S(2)}) collective-permute-start(f32[4,256,128]{2,1,0:T(8,128)S(1)} %rest_probes.1.after_ref.own_b), channel_id=1, source_target_pairs={{0,16},{2,18},{4,20},{6,22},{8,24},{10,26},{12,28},{14,30},{16,32}... | collective-permute-start | bytes 1572872 | tf_op jit(solution)/shard_map/ppermute | solution.py:484
  14.4 5.6 %collective-permute-start.2 = (f32[4,256,128]{2,1,0:T(8,128)S(1)}, f32[4,256,128]{2,1,0:T(8,128)S(1)}, u32[]{:S(2)}, u32[]{:S(2)}) collective-permute-start(f32[4,256,128]{2,1,0:T(8,128)S(1)} %collective-permute-done.moved_a), channel_id=1, source_target_pairs={{0,1},{1,0},{2,3},{3,2},{4,5},{5,4},{6,7},{7,6},{8,9},{9,8},{10,11... | collective-permute-start | bytes 1572872 | tf_op jit(solution)/shard_map/ppermute | solution.py:486
  18.3 56.4 %copy-start.1 = (s32[8,1]{0,1:T(1,128)S(1)}, s32[8,1]{0,1:T(1,128)}, u32[]{:S(2)}) copy-start(s32[8,1]{0,1:T(1,128)} %param.13) | copy-start | bytes 100
  20.0 2.6 %collective-permute-start.3 = (f32[4,256,128]{2,1,0:T(8,128)S(1)}, f32[4,256,128]{2,1,0:T(8,128)S(1)}, u32[]{:S(2)}, u32[]{:S(2)}) collective-permute-start(f32[4,256,128]{2,1,0:T(8,128)S(1)} %collective-permute-done.1.moved_b), channel_id=1, source_target_pairs={{0,1},{1,0},{2,3},{3,2},{4,5},{5,4},{6,7},{7,6},{8,9},{9,8},{10,11... | collective-permute-start | bytes 1572872 | tf_op jit(solution)/shard_map/ppermute | solution.py:488
  25.4 2.0 %collective-permute-start.4 = (f32[8,128,128]{2,1,0:T(8,128)S(1)}, f32[8,128,128]{2,1,0:T(8,128)S(1)}, u32[]{:S(2)}, u32[]{:S(2)}) collective-permute-start(f32[8,128,128]{2,1,0:T(8,128)S(1)} %get-tuple-element.21), channel_id=1, source_target_pairs={{0,1},{1,0},{2,3},{3,2},{4,5},{5,4},{6,7},{7,6},{8,9},{9,8},{10,11... | collective-permute-start | bytes 1572872 | tf_op jit(solution)/shard_map/ppermute | solution.py:490
  52.5 2.7 %collective-permute-start.5 = (f32[64,64]{1,0:T(8,128)S(1)}, f32[64,64]{1,0:T(8,128)S(1)}, u32[]{:S(2)}, u32[]{:S(2)}) collective-permute-start(f32[64,64]{1,0:T(8,128)S(1)} %get-tuple-element.23.gram_ref), channel_id=1, source_target_pairs={{0,1},{1,0},{2,3},{3,2},{4,5},{5,4},{6,7},{7,6},{8,9},{9,8},{10,11... | collective-permute-start | bytes 49160 | tf_op jit(solution)/shard_map/ppermute | solution.py:493
  91.9 3.5 %collective-permute-start.7 = (bf16[128,1280]{1,0:T(8,128)(2,1)S(1)}, bf16[128,1280]{1,0:T(8,128)(2,1)S(1)}, u32[]{:S(2)}, u32[]{:S(2)}) collective-permute-start(bf16[128,1280]{1,0:T(8,128)(2,1)S(1)} %bitcast.11), channel_id=1, source_target_pairs={{0,1},{1,0},{2,3},{3,2},{4,5},{5,4},{6,7},{7,6},{8,9},{9,8},{10,11... | collective-permute-start | bytes 983048 | tf_op jit(solution)/shard_map/ppermute | solution.py:500
  96.5 14.2 %all-to-all-start.3 = ((bf16[16,8,2176]{2,1,0:T(8,128)(2,1)}), bf16[16,8,2176]{2,1,0:T(8,128)(2,1)S(1)}, u32[]{:S(2)}, u32[]{:S(2)}) async-start(bf16[16,8,2176]{2,1,0:T(8,128)(2,1)} %bitcast.6), calls=%async_computation.3 | async-start | bytes 1114112 | tf_op jit(solution)/shard_map/all_to_all | solution.py:501
  100.1 1.9 %collective-permute-start.6 = (bf16[8,64,384]{2,1,0:T(8,128)(2,1)S(1)}, bf16[8,64,384]{2,1,0:T(8,128)(2,1)S(1)}, u32[]{:S(2)}, u32[]{:S(2)}) collective-permute-start(bf16[8,64,384]{2,1,0:T(8,128)(2,1)S(1)} %all_to_all.21.own_ref), channel_id=1, source_target_pairs={{0,1},{1,0},{2,3},{3,2},{4,5},{5,4},{6,7},{7,6},{8,9},{9,8},{10,11... | collective-permute-start | bytes 1179656 | tf_op jit(solution)/shard_map/ppermute | solution.py:495
  102.0 2.2 %copy-start = (bf16[8,1,512,512]{3,2,1,0:T(8,128)(2,1)S(1)}, bf16[8,1,512,512]{3,2,1,0:T(8,128)(2,1)}, u32[]{:S(2)}) copy-start(bf16[8,1,512,512]{3,2,1,0:T(8,128)(2,1)} %far_ref.1) | copy-start | bytes 12582916

commit v9 on v8

--- a/solution.py
+++ b/solution.py
@@ -309,7 +309,7 @@
     width = own_ref.shape[2] - LANES
     wide = width // LANES
     tiles = work_ref.shape[0]
-    total = jnp.zeros((RANK, RANK), f32)
+    uppers = []
     for r in range(count):
         block = own_ref[r].astype(f32)
         for q in range(blocks):
@@ -317,11 +317,12 @@
                 work_ref[q * wide + t, pl.ds(r, groups, stride=count), :] = block[
                     q * groups : (q + 1) * groups, t * LANES : (t + 1) * LANES
                 ]
-        upper = upper_half(block, width)
-        total = total + dot(upper, upper, TN, highest)
+        uppers.append(upper_half(block, width))
         work_ref[tiles - 2, pl.ds(r, groups, stride=count), :] = jnp.full(
             (groups, LANES), far_ref[r].astype(f32), f32
         )
+    uppers = jnp.concatenate(uppers, axis=0)
+    total = dot(uppers, uppers, TN, highest)
     work_ref[tiles - 1] = jnp.zeros((groups * count, LANES), f32)
     for p in range(2):
         low_row = 2 * p * groups

time: 114 us -> 114 us (level)
  no operation moved by 1% of the time
where the time goes in v9:
time: 114 us; the launch traced here: 113 us
  blocking collectives  58 us (51%)
  waiting for transfers between devices  21.1 us (19%)
  Pallas kernels  17.8 us (16%)
  starting transfers between devices  13.4 us (12%)
  local copies, waits for them, and re-layouts  2.2 us (2%)
    all_to_all x1, blocking collectives, shards(): lax.all_to_all(halves, 'blk', 0, 0, tiled=True, axis_index_groups=lanes)  24.7 us
    all_to_all x1, blocking collectives, shards(): own = lax.all_to_all(own, 'blk', 0, 0, tiled=True, axis_index_groups=lanes)  17.5 us
    all_to_all x1, blocking collectives, shards(): lax.all_to_all(payload.reshape(subtrees, count, -1), 'leaf', 0, 0, tiled=...  15.8 us
    ppermute x2, waiting for transfers between devices, shards(): moved = [lax.ppermute(x, ('leaf', 'blk'), shift) for x in own]  8.87 us
    all_to_all x1, waiting for transfers between devices, shards(): lax.all_to_all(chosen.reshape(subtrees, count, -1), 'leaf', 0, 0, tiled=T...  5.69 us
    all_to_all x1, starting transfers between devices, shards(): lax.all_to_all(chosen.reshape(subtrees, count, -1), 'leaf', 0, 0, tiled=T...  3.58 us
    pallas_call x1, Pallas kernels, mixed_probes(): pl.pallas_call(first_probes_kernel, out_shape=(half, pltpu.VMEM((count -...  3.17 us
    pallas_call x1, Pallas kernels, couple(): pl.pallas_call(functools.partial(couple_kernel, scale), out_shape=(jax.Sh...  2.96 us
  transfers between devices with their start and end apart: 9, of which 8 were waited for; matrix products, arithmetic and copies ran while one was open for 0% of the time, Pallas kernels for 4%

profile of v9, /device:TPU:1, one launch (start us, length us, event | category | flops | bytes accessed | tf_op | source)
XLA Modules:
  0.0 113.5 jit_solution(5942453053984694434)
XLA Ops:
  0.6 0.0 copy-start.2
  0.6 0.0 copy-start.3
  0.7 3.2 %first_probes.1 = (f32[4,256,128]{2,1,0:T(8,128)S(1)}, bf16[4,512,512]{2,1,0:T(8,128)(2,1)S(1)}, bf16[512,256]{1,0:T(8,128)(2,1)S(1)}) custom-call(f32[64,512]{1,0:T(8,128)} %bitcast.14, bf16[8,512,512]{2,1,0:T(8,128)(2,1)} %probes_ref.1), custom_call_target="tpu_custom_call" | custom-call | flops 402653184 | bytes 2621440 | tf_op jit(solution)/shard_map/first_probes/pallas_call | solution.py:142
  3.8 1.3 %collective-permute-start = (f32[4,256,128]{2,1,0:T(8,128)S(1)}, f32[4,256,128]{2,1,0:T(8,128)S(1)}, u32[]{:S(2)}, u32[]{:S(2)}) collective-permute-start(f32[4,256,128]{2,1,0:T(8,128)S(1)} %get-tuple-element.14.own_a), channel_id=1, source_target_pairs={{0,16},{2,18},{4,20},{6,22},{8,24},{10,26},{12,28},{14,30},{16,32}... | collective-permute-start | bytes 1572872 | tf_op jit(solution)/shard_map/ppermute | solution.py:485
  5.1 0.8 rest_probes.1.after_ref.own_b
  5.9 1.3 %collective-permute-start.1 = (f32[4,256,128]{2,1,0:T(8,128)S(1)}, f32[4,256,128]{2,1,0:T(8,128)S(1)}, u32[]{:S(2)}, u32[]{:S(2)}) collective-permute-start(f32[4,256,128]{2,1,0:T(8,128)S(1)} %rest_probes.1.after_ref.own_b), channel_id=1, source_target_pairs={{0,16},{2,18},{4,20},{6,22},{8,24},{10,26},{12,28},{14,30},{16,32}... | collective-permute-start | bytes 1572872 | tf_op jit(solution)/shard_map/ppermute | solution.py:485
  7.2 7.2 %collective-permute-done.moved_a = f32[4,256,128]{2,1,0:T(8,128)S(1)} collective-permute-done((f32[4,256,128]{2,1,0:T(8,128)S(1)}, f32[4,256,128]{2,1,0:T(8,128)S(1)}, u32[]{:S(2)}, u32[]{:S(2)}) %collective-permute-start) | collective-permute-done | bytes 524320 | tf_op jit(solution)/shard_map/ppermute | solution.py:485
  14.4 1.1 collective-permute-start.2
  15.5 0.0 copy-done.2
  15.5 0.0 copy-done.3
  15.5 0.1 pad_add_fusion.meta_ref
  15.6 2.7 %load.1.near_ref = bf16[8,1,512,512]{3,2,1,0:T(8,128)(2,1)S(1)} custom-call(s32[17]{0:T(128)S(1)} %pad_add_fusion.meta_ref, f32[4,256,128]{2,1,0:T(8,128)S(1)} %rest_probes.1.after_ref.own_b, bf16[8,1,512,512]{3,2,1,0:T(8,128)(2,1)} %refs_0_.1), custom_call_target="tpu_custom_call" | custom-call | bytes 8388608 | tf_op jit(solution)/shard_map/load/pallas_call | solution.py:189
  18.3 0.0 copy-start.1
  18.4 1.7 %collective-permute-done.1.moved_b = f32[4,256,128]{2,1,0:T(8,128)S(1)} collective-permute-done((f32[4,256,128]{2,1,0:T(8,128)S(1)}, f32[4,256,128]{2,1,0:T(8,128)S(1)}, u32[]{:S(2)}, u32[]{:S(2)}) %collective-permute-start.1) | collective-permute-done | bytes 524320 | tf_op jit(solution)/shard_map/ppermute | solution.py:485
  20.0 0.0 collective-permute-done.2.other_a
  20.0 1.1 collective-permute-start.3
  21.1 1.5 %collective-permute-done.3.other_b = f32[4,256,128]{2,1,0:T(8,128)S(1)} collective-permute-done((f32[4,256,128]{2,1,0:T(8,128)S(1)}, f32[4,256,128]{2,1,0:T(8,128)S(1)}, u32[]{:S(2)}, u32[]{:S(2)}) %collective-permute-start.3) | collective-permute-done | bytes 524320 | tf_op jit(solution)/shard_map/ppermute | solution.py:489
  22.6 2.8 %compress.1 = (f32[8,128,128]{2,1,0:T(8,128)S(1)}, f32[8,128,128]{2,1,0:T(8,128)S(1)}) custom-call(s32[17]{0:T(128)S(1)} %pad_add_fusion.meta_ref, f32[4,256,128]{2,1,0:T(8,128)S(1)} %get-tuple-element.14.own_a, f32[4,256,128]{2,1,0:T(8,128)S(1)} %rest_probes.1.after_ref.own_b, f32[4,256,128]{2,1,0:T(8,128)S(1)} %collective-permute-done.moved_a, ...), custom_call_target="tpu_custom_call" | custom-call | flops 805306368 | bytes 8388608 | tf_op jit(solution)/shard_map/compress/pallas_call | solution.py:235
  25.4 0.5 collective-permute-start.4
  25.9 1.5 %collective-permute-done.4 = f32[8,128,128]{2,1,0:T(8,128)S(1)} collective-permute-done((f32[8,128,128]{2,1,0:T(8,128)S(1)}, f32[8,128,128]{2,1,0:T(8,128)S(1)}, u32[]{:S(2)}, u32[]{:S(2)}) %collective-permute-start.4) | collective-permute-done | bytes 524320 | tf_op jit(solution)/shard_map/ppermute | solution.py:491
  27.4 0.1 add.9
  27.5 24.7 %all_to_all.20.terms_ref = f32[8,128,128]{2,1,0:T(8,128)S(1)} all-to-all(f32[8,128,128]{2,1,0:T(8,128)S(1)} %add.9), channel_id=1, replica_groups={{0,2,4,6,8,10,12,14},{1,3,5,7,9,11,13,15},{16,18,20,22,24,26,28,30},{17..., dimensions={0} | all-to-all | bytes 1048576 | tf_op jit(solution)/shard_map/all_to_all | solution.py:492
  52.2 0.3 gram.1
  52.5 1.8 %collective-permute-start.5 = (f32[64,64]{1,0:T(8,128)S(1)}, f32[64,64]{1,0:T(8,128)S(1)}, u32[]{:S(2)}, u32[]{:S(2)}) collective-permute-start(f32[64,64]{1,0:T(8,128)S(1)} %get-tuple-element.23.gram_ref), channel_id=1, source_target_pairs={{0,1},{1,0},{2,3},{3,2},{4,5},{5,4},{6,7},{7,6},{8,9},{9,8},{10,11... | collective-permute-start | bytes 49160 | tf_op jit(solution)/shard_map/ppermute | solution.py:494
  54.3 0.9 collective-permute-done.5.other_ref
  55.2 2.0 %basis.1 = bf16[8,64,384]{2,1,0:T(8,128)(2,1)S(1)} custom-call(s32[1]{0:T(128)} %bitcast.core_ref, f32[128,128]{1,0:T(8,128)S(1)} %get-tuple-element.22.mixed_ref, f32[64,64]{1,0:T(8,128)S(1)} %get-tuple-element.23.gram_ref, f32[64,64]{1,0:T(8,128)S(1)} %collective-permute-done.5.other_ref), custom_call_target="tpu_custom_call" | custom-call | tf_op jit(solution)/shard_map/basis/pallas_call | solution.py:289
  57.2 17.5 %all_to_all.21.own_ref = bf16[8,64,384]{2,1,0:T(8,128)(2,1)S(1)} all-to-all(bf16[8,64,384]{2,1,0:T(8,128)(2,1)S(1)} %basis.1), channel_id=1, replica_groups={{0,2,4,6,8,10,12,14},{1,3,5,7,9,11,13,15},{16,18,20,22,24,26,28,30},{17..., dimensions={0} | all-to-all | bytes 786432 | tf_op jit(solution)/shard_map/all_to_all | solution.py:495
  74.8 0.0 copy-done.1
  74.8 1.0 spread.1
  75.8 15.8 %all_to_all.22 = bf16[16,8,1280]{2,1,0:T(8,128)(2,1)S(1)} all-to-all(bf16[16,8,1280]{2,1,0:T(8,128)(2,1)S(1)} %bitcast.10), channel_id=1, replica_groups=mesh['leaf'=16,'blk'=16] {'leaf'}, dimensions={0} | all-to-all | bytes 655360 | tf_op jit(solution)/shard_map/all_to_all | solution.py:498
  91.6 2.3 %collective-permute-start.7 = (bf16[128,1280]{1,0:T(8,128)(2,1)S(1)}, bf16[128,1280]{1,0:T(8,128)(2,1)S(1)}, u32[]{:S(2)}, u32[]{:S(2)}) collective-permute-start(bf16[128,1280]{1,0:T(8,128)(2,1)S(1)} %bitcast.11), channel_id=1, source_target_pairs={{0,1},{1,0},{2,3},{3,2},{4,5},{5,4},{6,7},{7,6},{8,9},{9,8},{10,11... | collective-permute-start | bytes 983048 | tf_op jit(solution)/shard_map/ppermute | solution.py:501
  93.9 1.3 %collective-permute-done.7.other_ref = bf16[128,1280]{1,0:T(8,128)(2,1)S(1)} collective-permute-done((bf16[128,1280]{1,0:T(8,128)(2,1)S(1)}, bf16[128,1280]{1,0:T(8,128)(2,1)S(1)}, u32[]{:S(2)}, u32[]{:S(2)}) %collective-permute-start.7) | collective-permute-done | bytes 327712 | tf_op jit(solution)/shard_map/ppermute | solution.py:501
  95.1 1.1 choose.1
  96.3 3.6 %all-to-all-start.3 = ((bf16[16,8,2176]{2,1,0:T(8,128)(2,1)}), bf16[16,8,2176]{2,1,0:T(8,128)(2,1)S(1)}, u32[]{:S(2)}, u32[]{:S(2)}) async-start(bf16[16,8,2176]{2,1,0:T(8,128)(2,1)} %bitcast.6), calls=%async_computation.3 | async-start | bytes 1114112 | tf_op jit(solution)/shard_map/all_to_all | solution.py:502
  99.8 0.6 collective-permute-start.6
  100.4 1.3 %collective-permute-done.6.other_ref = bf16[8,64,384]{2,1,0:T(8,128)(2,1)S(1)} collective-permute-done((bf16[8,64,384]{2,1,0:T(8,128)(2,1)S(1)}, bf16[8,64,384]{2,1,0:T(8,128)(2,1)S(1)}, u32[]{:S(2)}, u32[]{:S(2)}) %collective-permute-start.6) | collective-permute-done | bytes 393248 | tf_op jit(solution)/shard_map/ppermute | solution.py:496
  101.8 0.0 copy-start
  101.8 2.2 %copy-done = bf16[8,1,512,512]{3,2,1,0:T(8,128)(2,1)S(1)} copy-done((bf16[8,1,512,512]{3,2,1,0:T(8,128)(2,1)S(1)}, bf16[8,1,512,512]{3,2,1,0:T(8,128)(2,1)}, u32[]{:S(2)}) %copy-start) | copy-done | bytes 4194328
  103.9 0.9 project.1
  104.8 5.7 %all-to-all-done.3 = bf16[16,8,2176]{2,1,0:T(8,128)(2,1)S(1)} async-done(((bf16[16,8,2176]{2,1,0:T(8,128)(2,1)}), bf16[16,8,2176]{2,1,0:T(8,128)(2,1)S(1)}, u32[]{:S(2)}, u32[]{:S(2)}) %all-to-all-start.3) | async-done | bytes 557088 | tf_op jit(solution)/shard_map/all_to_all | solution.py:502
  110.5 3.0 %couple.1 = (f32[8,1,64,64]{3,2,1,0:T(8,128)}, f32[8,64,64]{2,1,0:T(8,128)}) custom-call(bf16[8,192,512]{2,1,0:T(8,128)(2,1)S(1)} %get-tuple-element.24.image_ref, f32[8,64,64]{2,1,0:T(8,128)S(1)} %get-tuple-element.25.upper_ref, bf16[128,2176]{1,0:T(8,128)(2,1)S(1)} %bitcast.9), custom_call_target="tpu_custom_call" | custom-call | tf_op jit(solution)/shard_map/couple/pallas_call | solution.py:448
  (2 shorter events, 0.0 us)
Async XLA Ops:
  0.6 14.9 %copy-start.2 = (s32[8]{0:T(128)S(1)}, s32[8]{0:T(128)}, u32[]{:S(2)}) copy-start(s32[8]{0:T(128)} %param.9) | copy-start | bytes 100
  0.6 14.9 %copy-start.3 = (s32[8,1]{0,1:T(1,128)S(1)}, s32[8,1]{0,1:T(1,128)}, u32[]{:S(2)}) copy-start(s32[8,1]{0,1:T(1,128)} %param.8) | copy-start | bytes 100
  3.8 10.6 %collective-permute-start = (f32[4,256,128]{2,1,0:T(8,128)S(1)}, f32[4,256,128]{2,1,0:T(8,128)S(1)}, u32[]{:S(2)}, u32[]{:S(2)}) collective-permute-start(f32[4,256,128]{2,1,0:T(8,128)S(1)} %get-tuple-element.14.own_a), channel_id=1, source_target_pairs={{0,16},{2,18},{4,20},{6,22},{8,24},{10,26},{12,28},{14,30},{16,32}... | collective-permute-start | bytes 1572872 | tf_op jit(solution)/shard_map/ppermute | solution.py:485
  5.9 14.1 %collective-permute-start.1 = (f32[4,256,128]{2,1,0:T(8,128)S(1)}, f32[4,256,128]{2,1,0:T(8,128)S(1)}, u32[]{:S(2)}, u32[]{:S(2)}) collective-permute-start(f32[4,256,128]{2,1,0:T(8,128)S(1)} %rest_probes.1.after_ref.own_b), channel_id=1, source_target_pairs={{0,16},{2,18},{4,20},{6,22},{8,24},{10,26},{12,28},{14,30},{16,32}... | collective-permute-start | bytes 1572872 | tf_op jit(solution)/shard_map/ppermute | solution.py:485
  14.4 5.6 %collective-permute-start.2 = (f32[4,256,128]{2,1,0:T(8,128)S(1)}, f32[4,256,128]{2,1,0:T(8,128)S(1)}, u32[]{:S(2)}, u32[]{:S(2)}) collective-permute-start(f32[4,256,128]{2,1,0:T(8,128)S(1)} %collective-permute-done.moved_a), channel_id=1, source_target_pairs={{0,1},{1,0},{2,3},{3,2},{4,5},{5,4},{6,7},{7,6},{8,9},{9,8},{10,11... | collective-permute-start | bytes 1572872 | tf_op jit(solution)/shard_map/ppermute | solution.py:487
  18.3 56.4 %copy-start.1 = (s32[8,1]{0,1:T(1,128)S(1)}, s32[8,1]{0,1:T(1,128)}, u32[]{:S(2)}) copy-start(s32[8,1]{0,1:T(1,128)} %param.13) | copy-start | bytes 100
  20.0 2.6 %collective-permute-start.3 = (f32[4,256,128]{2,1,0:T(8,128)S(1)}, f32[4,256,128]{2,1,0:T(8,128)S(1)}, u32[]{:S(2)}, u32[]{:S(2)}) collective-permute-start(f32[4,256,128]{2,1,0:T(8,128)S(1)} %collective-permute-done.1.moved_b), channel_id=1, source_target_pairs={{0,1},{1,0},{2,3},{3,2},{4,5},{5,4},{6,7},{7,6},{8,9},{9,8},{10,11... | collective-permute-start | bytes 1572872 | tf_op jit(solution)/shard_map/ppermute | solution.py:489
  25.4 2.0 %collective-permute-start.4 = (f32[8,128,128]{2,1,0:T(8,128)S(1)}, f32[8,128,128]{2,1,0:T(8,128)S(1)}, u32[]{:S(2)}, u32[]{:S(2)}) collective-permute-start(f32[8,128,128]{2,1,0:T(8,128)S(1)} %get-tuple-element.21), channel_id=1, source_target_pairs={{0,1},{1,0},{2,3},{3,2},{4,5},{5,4},{6,7},{7,6},{8,9},{9,8},{10,11... | collective-permute-start | bytes 1572872 | tf_op jit(solution)/shard_map/ppermute | solution.py:491
  52.5 2.7 %collective-permute-start.5 = (f32[64,64]{1,0:T(8,128)S(1)}, f32[64,64]{1,0:T(8,128)S(1)}, u32[]{:S(2)}, u32[]{:S(2)}) collective-permute-start(f32[64,64]{1,0:T(8,128)S(1)} %get-tuple-element.23.gram_ref), channel_id=1, source_target_pairs={{0,1},{1,0},{2,3},{3,2},{4,5},{5,4},{6,7},{7,6},{8,9},{9,8},{10,11... | collective-permute-start | bytes 49160 | tf_op jit(solution)/shard_map/ppermute | solution.py:494
  91.6 3.5 %collective-permute-start.7 = (bf16[128,1280]{1,0:T(8,128)(2,1)S(1)}, bf16[128,1280]{1,0:T(8,128)(2,1)S(1)}, u32[]{:S(2)}, u32[]{:S(2)}) collective-permute-start(bf16[128,1280]{1,0:T(8,128)(2,1)S(1)} %bitcast.11), channel_id=1, source_target_pairs={{0,1},{1,0},{2,3},{3,2},{4,5},{5,4},{6,7},{7,6},{8,9},{9,8},{10,11... | collective-permute-start | bytes 983048 | tf_op jit(solution)/shard_map/ppermute | solution.py:501
  96.3 14.2 %all-to-all-start.3 = ((bf16[16,8,2176]{2,1,0:T(8,128)(2,1)}), bf16[16,8,2176]{2,1,0:T(8,128)(2,1)S(1)}, u32[]{:S(2)}, u32[]{:S(2)}) async-start(bf16[16,8,2176]{2,1,0:T(8,128)(2,1)} %bitcast.6), calls=%async_computation.3 | async-start | bytes 1114112 | tf_op jit(solution)/shard_map/all_to_all | solution.py:502
  99.8 1.9 %collective-permute-start.6 = (bf16[8,64,384]{2,1,0:T(8,128)(2,1)S(1)}, bf16[8,64,384]{2,1,0:T(8,128)(2,1)S(1)}, u32[]{:S(2)}, u32[]{:S(2)}) collective-permute-start(bf16[8,64,384]{2,1,0:T(8,128)(2,1)S(1)} %all_to_all.21.own_ref), channel_id=1, source_target_pairs={{0,1},{1,0},{2,3},{3,2},{4,5},{5,4},{6,7},{7,6},{8,9},{9,8},{10,11... | collective-permute-start | bytes 1179656 | tf_op jit(solution)/shard_map/ppermute | solution.py:496
  101.8 2.2 %copy-start = (bf16[8,1,512,512]{3,2,1,0:T(8,128)(2,1)S(1)}, bf16[8,1,512,512]{3,2,1,0:T(8,128)(2,1)}, u32[]{:S(2)}) copy-start(bf16[8,1,512,512]{3,2,1,0:T(8,128)(2,1)} %far_ref.1) | copy-start | bytes 12582916
